TPU v7x, 128 devices: a whole 4x4x4 slice. The times are simulated.
128 devices in a mesh: batch: 16 (over y, x), slab: 8 (over z, core).
Axes of the slice: x: 4, y: 4, z: 4, core: 2. Of those that a mesh axis runs over, the one named last changes fastest.
Arguments:
- images: bfloat16 [1024, 384, 384], P(('batch', 'slab')), may hold values from -6 to 6
- classes: int32 [1024], P(('batch', 'slab')), may hold values from 0 to 767
- shifts: int32 [1024, 2], P(('batch', 'slab')), may hold values from -16 to 16
- defocus_class: int32 [1024], P(('batch', 'slab')), may hold values from 0 to 15
- defocus: float32 [16], replicated, may hold values from 150 to 600
- run_counts: int32 [1024, 8], P(('batch', 'slab')), may hold values from 1 to 96, 384 in all within a row
- dest_map: int32 [768, 384], replicated, may hold values from 0 to 15
- ref: bfloat16 [384, 128, 768], P('batch', 'slab'), may hold values from -6 to 6
Outputs:
- updated: bfloat16 [384, 128, 768], P('batch', 'slab')
Inputs may be any that keep to these rules, and one draw needn't show every extreme that they name: `run_counts`: each particle's counts sum to 384; in every particle's row the largest count is exactly 96.
All inputs are finite; a program needn't handle non-finite values.
Results may differ from a plain program's by a relative error of at most 0.0065.
Values may be sent and summed in bfloat16 or wider, within the bound.
A program may use at most 128 MiB of HBM per device.

v0:
```python
import math

import jax
import jax.numpy as jnp
from jax import lax
from jax.sharding import PartitionSpec as P

TAU_PRIOR = 4.0
PHASE_OFFSET = 0.1


def dft_tables(length):
    index = jnp.arange(length, dtype=jnp.int32)
    turns = index[:, None] * index[None, :] % length
    angle = 2.0 * math.pi / length * turns.astype(jnp.float32)
    factor = 1.0 / math.sqrt(length)
    cosine = jnp.cos(angle) * factor
    sine = jnp.sin(angle) * factor
    table_left = jnp.concatenate([cosine, -sine], axis=0).astype(jnp.bfloat16)
    upper_rows = jnp.concatenate([cosine, -sine], axis=1)
    lower_rows = jnp.concatenate([sine, cosine], axis=1)
    table_right = jnp.concatenate([upper_rows, lower_rows], axis=0).astype(jnp.bfloat16)
    return (table_left, table_right)


def contrast(focus_value, freq_row, freq_col, length):
    half_length = length // 2
    spatial_row = ((freq_row + half_length) % length - half_length).astype(jnp.float32) / length
    spatial_col = ((freq_col + half_length) % length - half_length).astype(jnp.float32) / length
    return -jnp.sin(
        focus_value * (spatial_row * spatial_row + spatial_col * spatial_col) + PHASE_OFFSET
    )


def shifted_parts(real_part, imag_part, shift_x, shift_y, freq_row, freq_col, length):
    turns = (freq_col * shift_x + freq_row * shift_y) % length
    angle = 2.0 * math.pi / length * turns.astype(jnp.float32)
    cosine = jnp.cos(angle)
    sine = jnp.sin(angle)
    return (real_part * cosine + imag_part * sine, imag_part * cosine - real_part * sine)


def lookup(values, indices):
    matches = indices[:, None] == jnp.arange(values.shape[0], dtype=jnp.int32)[None, :]
    return jnp.sum(jnp.where(matches, values[None, :], 0.0), axis=1)


def insert_window(
    flat_rows,
    row_index,
    plane_index,
    focus_in,
    is_valid,
    rows_window,
    planes_window,
    row_start,
    defocus,
    length,
):
    bin_count = rows_window * planes_window + 1
    segment_ids = jnp.where(
        is_valid, row_index * planes_window + plane_index, rows_window * planes_window
    )
    numerator = jax.ops.segment_sum(flat_rows.astype(jnp.float32), segment_ids, bin_count)[
        :-1
    ].reshape(rows_window, planes_window, 2 * length)
    focus_rows = lookup(defocus, focus_in)
    global_rows = row_start + row_index
    transfer_in = contrast(
        focus_rows[:, None],
        global_rows[:, None],
        jnp.arange(length, dtype=jnp.int32)[None, :],
        length,
    )
    second = jax.ops.segment_sum(transfer_in * transfer_in, segment_ids, bin_count)[:-1].reshape(
        rows_window, planes_window, length
    )
    return (numerator, second)


def per_device(images, classes, shifts, defocus_class, defocus, run_counts, dest_map, ref):
    particle_count = images.shape[0]
    length = images.shape[1]
    slab_count = lax.axis_size("slab")
    capacity = 2 * length // slab_count
    plane_count = ref.shape[1]
    table_left, table_right = dft_tables(length)
    section = jnp.einsum(
        "ay,pyx->pax", table_left, images, preferred_element_type=jnp.float32
    ).astype(jnp.bfloat16)
    joined = jnp.concatenate([section[:, :length], section[:, length:]], axis=2)
    spectrum = jnp.einsum("pyc,cd->pyd", joined, table_right, preferred_element_type=jnp.float32)
    freq_row = jnp.arange(length, dtype=jnp.int32)[None, :, None]
    freq_col = jnp.arange(length, dtype=jnp.int32)[None, None, :]
    real_part, imag_part = shifted_parts(
        spectrum[..., :length],
        spectrum[..., length:],
        shifts[:, 0][:, None, None],
        shifts[:, 1][:, None, None],
        freq_row,
        freq_col,
        length,
    )
    focus_values = lookup(defocus, defocus_class)
    transfer = contrast(focus_values[:, None, None], freq_row, freq_col, length)
    weighted = jnp.concatenate([transfer * real_part, transfer * imag_part], axis=2).astype(
        jnp.bfloat16
    )
    run_ends = jnp.cumsum(run_counts, axis=1)
    run_starts = run_ends - run_counts
    dest_rows = dest_map[classes]
    padded = jnp.concatenate(
        [weighted, jnp.zeros((particle_count, capacity, 2 * length), jnp.bfloat16)], axis=1
    )

    def take_run(block, begin):
        return lax.dynamic_slice_in_dim(block, begin, capacity, 0)

    def take_owner(begin_cols):
        return jax.vmap(take_run)(padded, begin_cols)

    run_slots = jax.vmap(take_owner, in_axes=1)(run_starts)
    offsets = jnp.arange(capacity, dtype=jnp.int32)
    slot_rows = run_starts.T[:, :, None] + offsets[None, None, :]
    is_valid = offsets[None, None, :] < run_counts.T[:, :, None]
    safe_rows = jnp.minimum(slot_rows, length - 1)
    slot_planes = jnp.take_along_axis(
        jnp.broadcast_to(dest_rows[None], (slab_count, particle_count, length)), safe_rows, axis=2
    )
    slot_codes = jnp.where(
        is_valid,
        (defocus_class[None, :, None] * plane_count + slot_planes) * length + safe_rows,
        -1,
    )
    received, codes_in = (
        lax.all_to_all(run_slots, "slab", split_axis=0, concat_axis=0, tiled=True),
        lax.all_to_all(slot_codes, "slab", split_axis=0, concat_axis=0, tiled=True),
    )
    flat_rows = received.reshape(-1, 2 * length)
    flat_codes = codes_in.reshape(-1)
    is_valid_in = flat_codes >= 0
    safe_codes = jnp.maximum(flat_codes, 0)
    row_index = safe_codes % length
    rest_code = safe_codes // length
    plane_index = rest_code % plane_count
    focus_in = rest_code // plane_count
    numerator, second = insert_window(
        flat_rows,
        row_index,
        plane_index,
        focus_in,
        is_valid_in,
        length,
        plane_count,
        0,
        defocus,
        length,
    )
    own_sums, own_second = (
        lax.psum_scatter(
            numerator.astype(jnp.bfloat16), "batch", scatter_dimension=0, tiled=True
        ).astype(jnp.float32),
        lax.psum_scatter(
            second.astype(jnp.bfloat16), "batch", scatter_dimension=0, tiled=True
        ).astype(jnp.float32),
    )
    prior = ref.astype(jnp.float32)
    denom = own_second + TAU_PRIOR
    real_new = (TAU_PRIOR * prior[..., :length] + own_sums[..., :length]) / denom
    imag_new = (TAU_PRIOR * prior[..., length:] + own_sums[..., length:]) / denom
    return jnp.concatenate([real_new, imag_new], axis=2).astype(jnp.bfloat16)


def solution(mesh):
    placed = (
        P(("batch", "slab"), None, None),
        P(("batch", "slab")),
        P(("batch", "slab"), None),
        P(("batch", "slab")),
        P(),
        P(("batch", "slab"), None),
        P(),
        P("batch", "slab", None),
    )
    return jax.shard_map(
        per_device, mesh=mesh, in_specs=placed, out_specs=P("batch", "slab", None), check_vma=False
    )
```

profile of v0, /device:TPU:1, one launch (start us, length us, event | category | flops | bytes accessed | tf_op | source)
XLA Modules:
  0.0 509.7 jit_solution(9996493862388140103)
XLA Ops:
  6.5 0.9 copy.23
  8.3 1.8 gather_fusion
  10.2 47.6 %gather_fusion.1 = s32[6144]{0:T(1024)S(1)} fusion(s32[8,8,384]{2,1,0:T(8,128)S(1)} %broadcast_in_dim.44, s32[6144]{0:T(1024)S(1)} %reshape.370), kind=kCustom, calls=%fused_computation.1 | custom fusion | bytes 122880 | tf_op jit(solution)/shard_map/jit(take_along_axis)/gather | solution.py:127
  58.6 6.8 %all-to-all-start = ((s32[8,8,96]{2,1,0:T(8,128)}), s32[8,8,96]{2,1,0:T(8,128)S(1)}, u32[]{:S(2)}, u32[]{:S(2)}) async-start(s32[8,8,96]{2,1,0:T(8,128)} %add_select_fusion.6), calls=%async_computation | async-start | bytes 65536 | tf_op jit(solution)/shard_map/all_to_all | solution.py:137
  65.5 2.6 negate_convert_fusion
  68.0 2.3 fusion.42
  70.4 2.9 convert_bitcast_fusion
  74.4 4.0 fusion.12
  78.4 37.9 %multiply_convert_fusion.1 = (bf16[8,384,384]{2,1,0:T(8,128)(2,1)S(1)}, bf16[8,384,384]{2,1,0:T(8,128)(2,1)S(1)}) fusion(f32[8,384,768]{2,1,0:T(8,128)S(1)} %fusion.12, s32[8,384]{1,0:T(8,128)S(1)} %get-tuple-element.19, s32[8,384]{1,0:T(8,128)S(1)} %get-tuple-element.20, f32[384,384]{1,0:T(8,128)S(1)} %broadcast_add_fusion, f32[8]{0:T(128)S(1)} %select_reduce_fusion.1), kind=kLoop, calls=%fused_computation.30 | loop fusion | flops 25952256 | bytes 14770208 | tf_op jit(solution)/shard_map/convert.5
  116.7 4.8 copy.31
  121.6 5.3 %concatenate.39.clone = bf16[8,480,768]{2,0,1:T(8,128)(2,1)} pad(bf16[8,384,768]{2,0,1:T(8,128)(2,1)} %copy.31, bf16[]{:T(256)} %constant.140.clone.1), padding=0_0x0_96x0_0 | pad | bytes 10616834 | tf_op jit(solution)/shard_map/concatenate | solution.py:112
  126.9 22.5 %gather_fusion.2 = bf16[64,96,768]{2,0,1:T(8,128)(2,1)} fusion(bf16[8,480,768]{2,0,1:T(8,128)(2,1)} %concatenate.39.clone, s32[64]{0:T(128)S(1)} %reshape.376), kind=kCustom, calls=%fused_computation.2 | custom fusion | bytes 18875136 | tf_op jit(solution)/shard_map/vmap(vmap())/gather | solution.py:117
  149.4 12.6 %copy.28 = bf16[8,8,96,768]{3,2,1,0:T(8,128)(2,1)} copy(bf16[8,8,96,768]{3,1,0,2:T(8,128)(2,1)} %bitcast.34) | data formatting | bytes 18874368 | tf_op jit(solution)/shard_map/vmap(vmap())/gather | solution.py:117
  162.0 5.0 all-to-all-start.1
  167.7 104.4 %all-to-all-done.1 = bf16[8,8,96,768]{3,2,1,0:T(8,128)(2,1)} async-done(((bf16[8,8,96,768]{3,2,1,0:T(8,128)(2,1)}), bf16[8,8,96,768]{3,2,1,0:T(8,128)(2,1)}, u32[]{:S(2)}, u32[]{:S(2)}) %all-to-all-start.1) | async-done | bytes 9437216 | tf_op jit(solution)/shard_map/all_to_all | solution.py:136
  272.1 50.1 %scatter_custom_fusion = f32[6145,768]{1,0:T(8,128)} fusion(s32[6144]{0:T(1024)S(1)} %bitcast.37, bf16[6144,768]{1,0:T(8,128)(2,1)} %bitcast.15, f32[]{:T(128)} %constant.88.clone.1), kind=kCustom, calls=%fused_computation.6 | custom fusion | flops 9437184 | bytes 28314628 | tf_op jit(solution)/shard_map/scatter-add | solution.py:64
  322.3 11.2 %slice.97 = bf16[6144,768]{1,0:T(8,128)(2,1)} slice(f32[6145,768]{1,0:T(8,128)} %scatter_custom_fusion), slice={[0:6144], [0:768]} | slice | bytes 18874368 | tf_op jit(solution)/shard_map/slice | solution.py:64
  334.3 76.6 %scatter_custom_fusion.1 = f32[6145,384]{1,0:T(8,128)} fusion(s32[6144]{0:T(1024)S(1)} %bitcast.38, f32[]{:T(128)} %constant.88.clone.1, f32[]{:T(128)} %constant.137.clone.1, f32[384]{0:T(512)S(1)} %fusion.68, f32[6144]{0:T(1024)S(1)} %fusion.57, f32[6144]{0:T(1024)S(1)} %select_reduce_fusion), kind=kCustom, calls=%fused_computation.10 | custom fusion | flops 11796480 | bytes 9489928 | tf_op jit(solution)/shard_map/scatter-add | solution.py:75
  410.9 6.5 %slice.98 = bf16[6144,384]{1,0:T(8,128)(2,1)} slice(f32[6145,384]{1,0:T(8,128)} %scatter_custom_fusion.1), slice={[0:6144], [0:384]} | slice | bytes 9437184 | tf_op jit(solution)/shard_map/slice | solution.py:75
  417.5 1.3 convert_element_type.79
  419.6 2.2 convert_element_type.88
  421.8 78.4 %reduce-scatter.5.cloned.1.call-done = bf16[24,16,384]{2,1,0:T(8,128)(2,1)} async-done(((bf16[384,16,384]{2,1,0:T(8,128)(2,1)}), bf16[24,16,384]{2,1,0:T(8,128)(2,1)}) %reduce-scatter.5.cloned.1.call-update) | async-done | bytes 294928 | tf_op jit(solution)/shard_map/reduce_scatter | solution.py:163
  500.2 1.5 fusion.36
  501.8 0.9 pad_maximum_fusion.1
  (51 shorter events, 5.5 us)
Async XLA Ops:
  6.5 63.9 %copy-start = (bf16[8,384,384]{2,1,0:T(8,128)(2,1)S(1)}, bf16[8,384,384]{2,1,0:T(8,128)(2,1)}, u32[]{:S(2)}) copy-start(bf16[8,384,384]{2,1,0:T(8,128)(2,1)} %param.8) | copy-start | bytes 7077892
  10.2 47.7 %copy-start.2 = (s32[8,8]{1,0:T(8,128)S(1)}, s32[8,8]{1,0:T(8,128)}, u32[]{:S(2)}) copy-start(s32[8,8]{1,0:T(8,128)} %param.13) | copy-start | bytes 772
  10.2 47.7 %copy-start.5 = (s32[8]{0:T(128)S(1)}, s32[8]{0:T(128)}, u32[]{:S(2)}) copy-start(s32[8]{0:T(128)} %param.11) | copy-start | bytes 100
  58.6 103.3 %all-to-all-start = ((s32[8,8,96]{2,1,0:T(8,128)}), s32[8,8,96]{2,1,0:T(8,128)S(1)}, u32[]{:S(2)}, u32[]{:S(2)}) async-start(s32[8,8,96]{2,1,0:T(8,128)} %add_select_fusion.6), calls=%async_computation | async-start | bytes 65536 | tf_op jit(solution)/shard_map/all_to_all | solution.py:137
  73.3 0.7 copy-start.3
  73.4 0.8 copy-start.4
  162.0 110.2 %all-to-all-start.1 = ((bf16[8,8,96,768]{3,2,1,0:T(8,128)(2,1)}), bf16[8,8,96,768]{3,2,1,0:T(8,128)(2,1)}, u32[]{:S(2)}, u32[]{:S(2)}) async-start(bf16[8,8,96,768]{3,2,1,0:T(8,128)(2,1)} %copy.28), calls=%async_computation.1 | async-start | bytes 18874368 | tf_op jit(solution)/shard_map/all_to_all | solution.py:136
  167.0 252.6 %reduce-scatter.3.cloned.1.call-start = ((), (), s32[]{:S(2)}) async-start(), calls=%async_computation.4 | async-start | bytes 10027008 | tf_op jit(solution)/shard_map/reduce_scatter | solution.py:160
  333.5 166.7 %reduce-scatter.5.cloned.1.call-start = ((), (), s32[]{:S(2)}) async-start(), calls=%async_computation.5 | async-start | bytes 5013504 | tf_op jit(solution)/shard_map/reduce_scatter | solution.py:163
  417.4 85.2 %copy-start.1 = (bf16[8,384,384]{2,1,0:T(8,128)(2,1)S(1)}, bf16[8,384,384]{2,1,0:T(8,128)(2,1)}, u32[]{:S(2)}) copy-start(bf16[8,384,384]{2,1,0:T(8,128)(2,1)} %param.8) | copy-start | bytes 7077892
Sparse Core Ops, SparseCore 0:
  333.6 85.9 reduce-scatter.2
  423.3 76.8 reduce-scatter.4
where the time goes:
time: 518 us; the launch traced here: 510 us
  waiting for transfers between devices  184 us (36%)
  other arithmetic  178 us (34%)
  local copies, waits for them, and re-layouts  115 us (22%)
  between operations  13.9 us (3%)
  starting transfers between devices  12.1 us (2%)
  matrix products  6.9 us (1%)
    all_to_all x1, waiting for transfers between devices, per_device(): lax.all_to_all(run_slots, 'slab', split_axis=0, concat_axis=0, tiled=True)  104 us
    reduce_scatter x1, waiting for transfers between devices, per_device(): lax.psum_scatter(second.astype(jnp.bfloat16), 'batch', scatter_dimension=...  78.4 us
    scatter-add x1, other arithmetic, insert_window(): jax.ops.segment_sum(transfer_in * transfer_in, segment_ids, bin_count)[:-1]  76.6 us
    scatter-add x1, other arithmetic, insert_window(): jax.ops.segment_sum(flat_rows.astype(jnp.float32), segment_ids, bin_count)  50.1 us
    gather x3, local copies, waits for them, and re-layouts, per_device(): jnp.take_along_axis(jnp.broadcast_to(dest_rows[None], (slab_count, partic...  47.7 us
    another operation x4, other arithmetic  44.3 us
    gather x3, local copies, waits for them, and re-layouts, take_run(): return lax.dynamic_slice_in_dim(block, begin, capacity, 0)  35.2 us
    slice x1, local copies, waits for them, and re-layouts, insert_window(): jax.ops.segment_sum(flat_rows.astype(jnp.float32), segment_ids, bin_count)  11.2 us
  transfers between devices with their start and end apart: 4, of which 3 were waited for; matrix products, arithmetic and copies ran while one was open for 36% of the time, Pallas kernels for 0%

commit v1 on v0

v1 whole, which is shorter than its diff:
```python
import functools
import math

import jax
import jax.numpy as jnp
import ml_dtypes
import numpy as np
from jax import lax
from jax.experimental import pallas as pl
from jax.experimental.pallas import tpu as pltpu
from jax.sharding import PartitionSpec as P

TAU_PRIOR = 4.0
PHASE_OFFSET = 0.1
MESH = pl.DeviceIdType.MESH

K = 384
NB = 16
NS = 8
PP = 8
KYB = K // NB
CH = 3
KYC = KYB // CH
PAIRS = KYC // 2
PL = 16
NDEF = 16
BF = jnp.bfloat16
F32 = jnp.float32


def chunk_rows():
    rows = [
        KYB * b + KYC * c + i for c in range(CH) for b in range(NB) for i in range(KYC)
    ]
    return np.array(rows, np.int32).reshape(CH, NB * KYC)


def tables():
    index = np.arange(K)
    angle = 2.0 * np.pi / K * ((index[:, None] * index[None, :]) % K)
    cosine = (np.cos(angle) / math.sqrt(K)).astype(np.float32)
    sine = (np.sin(angle) / math.sqrt(K)).astype(np.float32)
    rows = chunk_rows()
    left = np.stack(
        [np.concatenate([cosine[r], -sine[r]], axis=0) for r in rows], axis=0
    ).astype(ml_dtypes.bfloat16)
    right = np.concatenate(
        [np.concatenate([cosine, -sine], 1), np.concatenate([sine, cosine], 1)], 0
    ).astype(ml_dtypes.bfloat16)
    return left, right


def split3(x):
    high = lax.reduce_precision(x, 8, 7)
    rest = x - high
    mid = lax.reduce_precision(rest, 8, 7)
    low = rest - mid
    return high, mid, low


def kernel(
    img, left, right, uu, vv, codes, tw, rw, ref,
    out,
    scr, sendb, recvb, crecv, zsend, zrecv, nsend, nrecv, wts,
    code_s, code_r, row_s, row_r, z_s, z_r, n_s, n_r,
):
    mb = lax.axis_index("batch")
    ms = lax.axis_index("slab")
    core = lax.rem(ms, 2)
    zbase = ms - core
    mz = ms // 2
    me = mb * 2 + core

    barrier = pltpu.get_barrier_semaphore()

    def greet_plane(q, carry):
        i = lax.rem(me + q, 32)
        pl.semaphore_signal(
            barrier, inc=1, device_id=(i // 2, zbase + lax.rem(i, 2)), device_id_type=MESH
        )
        return carry

    def greet_slab(q, carry):
        pl.semaphore_signal(
            barrier, inc=1, device_id=(mb, lax.rem(ms + q, NS)), device_id_type=MESH
        )
        return carry

    lax.fori_loop(1, 32, greet_plane, 0)
    lax.fori_loop(1, NS, greet_slab, 0)

    def compute(c):
        def two(pp, carry):
            lc = left[c]
            for j in range(2):
                p = pp * 2 + j
                sec = jnp.dot(lc, img[p], preferred_element_type=F32).astype(BF)
                joined = jnp.concatenate([sec[:128], sec[128:]], axis=1)
                spec = jnp.dot(joined, right[...], preferred_element_type=F32)
                factor = jnp.dot(
                    uu[p, pl.ds(pl.multiple_of(c * 128, 128), 128), :],
                    vv[p],
                    preferred_element_type=F32,
                )
                sr, si = spec[:, :K], spec[:, K:]
                fr, fi = factor[:, :K], factor[:, K:]
                wr = sr * fr - si * fi
                wi = sr * fi + si * fr
                for g in range(3):
                    cols = slice(g * 128, (g + 1) * 128)
                    scr[g, pl.ds(p, 128, stride=8), :] = wr[:, cols]
                    scr[3 + g, pl.ds(p, 128, stride=8), :] = wi[:, cols]
            return carry

        lax.fori_loop(0, PP // 2, two, 0)

    def send_rows(c):
        def one(q, carry):
            b = lax.rem(mb + q, NB)
            start = pl.multiple_of(b * 64, 64)
            for h in range(2):
                for g in range(3):
                    sendb[c, b * 2 + h, :, pl.ds(g * 128, 128)] = scr[
                        3 * h + g, pl.ds(start, 64), :
                    ].astype(BF)
            for h in range(2):
                def remote(h=h):
                    pltpu.make_async_remote_copy(
                        src_ref=sendb.at[c, b * 2 + h],
                        dst_ref=recvb.at[c, me],
                        send_sem=row_s.at[c],
                        recv_sem=row_r.at[c],
                        device_id=(b, zbase + h),
                        device_id_type=MESH,
                    ).start()

                def local(h=h):
                    pltpu.make_async_copy(
                        sendb.at[c, b * 2 + h], recvb.at[c, me], row_r.at[c]
                    ).start()

                own = jnp.logical_and(q == 0, core == h)
                pl.when(own)(local)
                pl.when(jnp.logical_not(own))(remote)
            return carry

        lax.fori_loop(0, NB, one, 0)

    compute(0)
    pl.semaphore_wait(barrier, 31 + NS - 1)

    def send_codes(q, carry):
        i = lax.rem(me + q, 32)
        pltpu.make_async_remote_copy(
            src_ref=codes.at[i // 2],
            dst_ref=crecv.at[pl.ds(pl.multiple_of(me * 16, 16), 16), :],
            send_sem=code_s,
            recv_sem=code_r,
            device_id=(i // 2, zbase + lax.rem(i, 2)),
            device_id_type=MESH,
        ).start()
        return carry

    pltpu.make_async_copy(
        codes.at[mb], crecv.at[pl.ds(pl.multiple_of(me * 16, 16), 16), :], code_r
    ).start()
    lax.fori_loop(1, 32, send_codes, 0)
    send_rows(0)

    def produce(c, carry):
        compute(c)
        send_rows(c)
        return carry

    lax.fori_loop(1, CH, produce, 0)

    pltpu.make_async_copy(crecv, crecv, code_r).wait()

    lane = lax.broadcasted_iota(jnp.int32, (32, 128), 1)
    sub = lax.broadcasted_iota(jnp.int32, (32, 128), 0)
    mine = (lane // 16) == lax.rem(sub, 8)

    def pair_codes(pair):
        got = crecv[pl.ds(pair, 32, stride=16), :]
        return jnp.sum(jnp.where(mine, got, 0).reshape(4, 8, 128), axis=1)

    spot = lax.broadcasted_iota(jnp.int32, (256, 128), 0)

    def one_hot(code4):
        place = code4 & 255
        return jnp.concatenate(
            [
                jnp.where(spot == place[g : g + 1, :], 1.0, 0.0).astype(BF)
                for g in range(4)
            ],
            axis=1,
        )

    row_id = lax.broadcasted_iota(jnp.int32, (128, 128), 0)
    row_class = jnp.where(row_id < 3 * NDEF, lax.rem(row_id, NDEF), -1)

    def count(pair, carry):
        code4 = pair_codes(pair)
        kind = code4 >> 8
        kinds = jnp.concatenate(
            [
                jnp.where(row_class == kind[g : g + 1, :], 1.0, 0.0).astype(BF)
                for g in range(4)
            ],
            axis=1,
        )
        tally = lax.dot_general(
            one_hot(code4), kinds, (((1,), (1,)), ((), ())), preferred_element_type=F32
        )
        start = pl.multiple_of(pair * 32, 32)
        nsend[:, pl.ds(start, 32), :] = tally.astype(BF).reshape(NS, 32, 128)
        return carry

    lax.fori_loop(0, CH * PAIRS, count, 0)

    pltpu.make_async_copy(nsend.at[ms], nrecv.at[mz], n_r).start()

    def send_counts(q, carry):
        peer = lax.rem(ms + 2 * q, NS)
        pltpu.make_async_remote_copy(
            src_ref=nsend.at[peer],
            dst_ref=nrecv.at[mz],
            send_sem=n_s,
            recv_sem=n_r,
            device_id=(mb, peer),
            device_id_type=MESH,
        ).start()
        return carry

    lax.fori_loop(1, NS // 2, send_counts, 0)

    def scatter(c, carry):
        pltpu.make_async_copy(recvb.at[c], recvb.at[c], row_r.at[c]).wait()

        def one(j, inner):
            start = pl.multiple_of(j * 16, 16)
            rows = recvb[c, :, pl.ds(start, 16), :].reshape(512, K)
            hot = one_hot(pair_codes(c * PAIRS + j))
            part = jnp.dot(hot, rows, preferred_element_type=F32)
            zsend[c, :, pl.ds(pl.multiple_of(j * 32, 32), 32), :] = part.astype(
                BF
            ).reshape(NS, 32, K)
            return inner

        lax.fori_loop(0, PAIRS, one, 0)

        pltpu.make_async_copy(zsend.at[c, ms], zrecv.at[c, ms], z_r.at[c]).start()

        def send(q, inner):
            peer = lax.rem(ms + q, NS)
            pltpu.make_async_remote_copy(
                src_ref=zsend.at[c, peer],
                dst_ref=zrecv.at[c, ms],
                send_sem=z_s.at[c],
                recv_sem=z_r.at[c],
                device_id=(mb, peer),
                device_id_type=MESH,
            ).start()
            return inner

        lax.fori_loop(1, NS, send, 0)
        return carry

    lax.fori_loop(0, CH, scatter, 0)

    pltpu.make_async_copy(nrecv, nrecv, n_r).wait()
    totals = (
        nrecv[0].astype(F32) + nrecv[1].astype(F32) + nrecv[2].astype(F32) + nrecv[3].astype(F32)
    )
    wts[...] = (
        jnp.dot(
            totals * tw[...], rw[...], precision=lax.Precision.HIGHEST,
            preferred_element_type=F32,
        )
        + TAU_PRIOR
    )

    def finish(c, carry):
        pltpu.make_async_copy(zrecv.at[c], zrecv.at[c], z_r.at[c]).wait()
        start = pl.multiple_of(c * 128, 128)
        denom = wts[pl.ds(start, 128), :]
        for h in range(2):
            total = TAU_PRIOR * ref[pl.ds(start, 128), pl.ds(h * K, K)].astype(F32)
            for z in range(NS // 2):
                total += zrecv[c, 2 * z + h].astype(F32)
            out[pl.ds(start, 128), pl.ds(h * K, K)] = (total / denom).astype(BF)
        return carry

    lax.fori_loop(0, CH, finish, 0)

    def drain(src, dst, send_sem, recv_sem):
        pltpu.make_async_remote_copy(
            src_ref=src, dst_ref=dst, send_sem=send_sem, recv_sem=recv_sem,
            device_id=(mb, ms), device_id_type=MESH,
        ).wait_send()

    drain(crecv.at[pl.ds(0, 31 * 16), :], crecv.at[pl.ds(0, 31 * 16), :], code_s, code_r)
    drain(nsend.at[pl.ds(0, 3)], nsend.at[pl.ds(0, 3)], n_s, n_r)

    def drain_chunk(c, carry):
        drain(sendb.at[c, pl.ds(0, 31)], recvb.at[c, pl.ds(0, 31)], row_s.at[c], row_r.at[c])
        drain(zsend.at[c, pl.ds(0, 7)], zrecv.at[c, pl.ds(0, 7)], z_s.at[c], z_r.at[c])
        return carry

    lax.fori_loop(0, CH, drain_chunk, 0)


def per_device(images, classes, shifts, defocus_class, defocus, run_counts, dest_map, ref):
    left, right = tables()
    rows = jnp.asarray(chunk_rows().reshape(-1))
    freq = jnp.arange(K, dtype=jnp.int32)

    def square(k):
        half = ((k + K // 2) % K - K // 2).astype(F32) / K
        return half * half

    own_focus = jnp.sum(
        jnp.where(defocus_class[:, None] == jnp.arange(NDEF)[None, :], defocus[None, :], 0.0),
        axis=1,
    )
    step = 2.0 * math.pi / K
    turn_y = step * ((rows[None, :] * shifts[:, 1:2]) % K).astype(F32)
    turn_x = step * ((freq[None, :] * shifts[:, 0:1]) % K).astype(F32)
    eyr, eyi = jnp.cos(turn_y), -jnp.sin(turn_y)
    exr, exi = jnp.cos(turn_x), -jnp.sin(turn_x)
    arg_y = own_focus[:, None] * square(rows)[None, :] + PHASE_OFFSET
    arg_x = own_focus[:, None] * square(freq)[None, :]
    say, cay = -jnp.sin(arg_y), -jnp.cos(arg_y)
    cbx, sbx = jnp.cos(arg_x), jnp.sin(arg_x)
    u = jnp.stack([say * eyr, say * eyi, cay * eyr, cay * eyi], axis=-1)
    v1r, v1i, v2r, v2i = cbx * exr, cbx * exi, sbx * exr, sbx * exi
    v = jnp.stack(
        [
            jnp.concatenate([v1r, v1i], 1),
            jnp.concatenate([-v1i, v1r], 1),
            jnp.concatenate([v2r, v2i], 1),
            jnp.concatenate([-v2i, v2r], 1),
        ],
        axis=1,
    )
    uh, um, ul = split3(u)
    vh, vm, vl = split3(v)
    zu = jnp.zeros(u.shape[:2] + (8,), F32)
    zv = jnp.zeros((v.shape[0], 8, v.shape[2]), F32)
    uu = jnp.concatenate([uh, uh, um, uh, ul, um, zu], axis=2).astype(BF)
    vv = jnp.concatenate([vh, vm, vh, vl, vh, vm, zv], axis=1).astype(BF)

    ends = jnp.cumsum(run_counts, axis=1)
    slab = jnp.sum((freq[None, :, None] >= ends[:, None, :]).astype(jnp.int32), axis=2)
    inner = dest_map[classes]
    code = (
        (defocus_class[:, None] << 8) + slab * 32 + (freq % 2 * 16)[None, :] + inner
    )
    code = code.reshape(PP, NB, CH * PAIRS, 2).transpose(1, 2, 3, 0).reshape(NB, CH * PAIRS, 16)
    code = jnp.tile(code, (1, 1, 8))
    codes = jnp.concatenate([code, jnp.zeros((NB, 16 - CH * PAIRS, 128), jnp.int32)], axis=1)

    own_rows = lax.axis_index("batch") * KYB + jnp.arange(KYB, dtype=jnp.int32)
    arg2_y = 2.0 * (defocus[None, :] * square(own_rows)[:, None] + PHASE_OFFSET)
    arg2_x = 2.0 * (defocus[:, None] * square(freq)[None, :])
    tw = jnp.concatenate(
        [
            -0.5 * jnp.cos(arg2_y),
            0.5 * jnp.sin(arg2_y),
            jnp.full((KYB, NDEF), 0.5, F32),
            jnp.zeros((KYB, 128 - 3 * NDEF), F32),
        ],
        axis=1,
    )
    tw = jnp.broadcast_to(tw[:, None, :], (KYB, PL, 128)).reshape(KYB * PL, 128)
    rw = jnp.concatenate(
        [
            jnp.cos(arg2_x),
            jnp.sin(arg2_x),
            jnp.ones((NDEF, K), F32),
            jnp.zeros((128 - 3 * NDEF, K), F32),
        ],
        axis=0,
    )

    vmem = pl.BlockSpec(memory_space=pltpu.VMEM)
    dma = pltpu.SemaphoreType.DMA
    out = pl.pallas_call(
        kernel,
        out_shape=jax.ShapeDtypeStruct((KYB * PL, 2 * K), BF),
        in_specs=[vmem] * 9,
        out_specs=vmem,
        scratch_shapes=[
            pltpu.VMEM((6, NB * KYC * PP, 128), F32),
            pltpu.VMEM((CH, 32, KYC * PP, K), BF),
            pltpu.VMEM((CH, 32, KYC * PP, K), BF),
            pltpu.VMEM((32 * 16, 128), jnp.int32),
            pltpu.VMEM((CH, NS, KYC * PL, K), BF),
            pltpu.VMEM((CH, NS, KYC * PL, K), BF),
            pltpu.VMEM((NS, KYB * PL, 128), BF),
            pltpu.VMEM((NS // 2, KYB * PL, 128), BF),
            pltpu.VMEM((KYB * PL, K), F32),
            dma, dma, dma((CH,)), dma((CH,)), dma((CH,)), dma((CH,)), dma, dma,
        ],
        compiler_params=pltpu.CompilerParams(
            collective_id=0, has_side_effects=True, vmem_limit_bytes=60 * 1024 * 1024
        ),
    )(
        images, jnp.asarray(left), jnp.asarray(right), uu, vv, codes, tw, rw,
        ref.reshape(KYB * PL, 2 * K),
    )
    return out.reshape(KYB, PL, 2 * K)


def solution(mesh):
    placed = (
        P(("batch", "slab"), None, None),
        P(("batch", "slab")),
        P(("batch", "slab"), None),
        P(("batch", "slab")),
        P(),
        P(("batch", "slab"), None),
        P(),
        P("batch", "slab", None),
    )
    return jax.shard_map(
        per_device, mesh=mesh, in_specs=placed, out_specs=P("batch", "slab", None), check_vma=False
    )
```

time: 518 us -> 113 us (0.22); the launches traced: 510 us -> 113 us
  waiting for transfers between devices: 184 us -> 0 us
  other arithmetic: 178 us -> 7.11 us
  local copies, waits for them, and re-layouts: 115 us -> 18.3 us
  Pallas kernels: 0 us -> 87 us
  between operations: 13.9 us -> 0.24 us
  starting transfers between devices: 12.1 us -> 0 us
  matrix products: 6.9 us -> 0 us
    scatter-add x2 -> x0, other arithmetic: 127 us -> none  [the longest x1 76.6 us: insert_window(): jax.ops.segment_sum(transfer_in * transfer_in, segment_ids, bin_count)[:-1]]
    all_to_all x2 -> x0, waiting for transfers between devices: 104 us -> none  [the longest x1 104 us: per_device(): lax.all_to_all(run_slots, 'slab', split_axis=0, concat_axis=0, tiled=True)]
    pallas_call x0 -> x1, Pallas kernels: none -> 87 us  [per_device(): pl.pallas_call(kernel, out_shape=jax.ShapeDtypeStruct((KYB * PL, 2 * K),...]
    gather x7 -> x2, local copies, waits for them, and re-layouts: 84.7 us -> 0.69 us  [per_device(): inner = dest_map[classes]]
    reduce_scatter x2 -> x0, waiting for transfers between devices: 79.2 us -> none  [the longest x1 78.4 us: per_device(): lax.psum_scatter(second.astype(jnp.bfloat16), 'batch', scatter_dimension=...]
    another operation x5, other arithmetic: 44.3 us -> 2.98 us
    slice x3 -> x0, local copies, waits for them, and re-layouts: 18.3 us -> none  [the longest x1 11.2 us: insert_window(): jax.ops.segment_sum(flat_rows.astype(jnp.float32), segment_ids, bin_count)]
    all_to_all x2 -> x0, starting transfers between devices: 11.8 us -> none  [the longest x1 6.81 us: per_device(): lax.all_to_all(slot_codes, 'slab', split_axis=0, concat_axis=0, tiled=True)]
  transfers between devices with their start and end apart: 4 -> 0, of which waited for: 3 -> 0; matrix products, arithmetic and copies ran while one was open for 36% -> 0% of each run, Pallas kernels for 0% -> 0%
where the time goes in v1:
time: 113 us
  Pallas kernels  87 us (77%)
  local copies, waits for them, and re-layouts  18.3 us (16%)
  other arithmetic  7.11 us (6%)
    pallas_call x1, Pallas kernels, per_device(): pl.pallas_call(kernel, out_shape=jax.ShapeDtypeStruct((KYB * PL, 2 * K),...  87 us
    concatenate x1, local copies, waits for them, and re-layouts, per_device(): uu = jnp.concatenate([uh, uh, um, uh, ul, um, zu], axis=2).astype(BF)  5.19 us
    another operation x2, other arithmetic  2.81 us
    concatenate x1, local copies, waits for them, and re-layouts, per_device(): vv = jnp.concatenate([vh, vm, vh, vl, vh, vm, zv], axis=1).astype(BF)  2.78 us

profile of v1, /device:TPU:1, one launch (start us, length us, event | category | flops | bytes accessed | tf_op | source)
XLA Modules:
  0.0 112.7 jit_solution(6495042905830339611)
XLA Ops:
  0.0 0.8 slice_bitcast_fusion
  0.8 0.9 select_reduce_fusion
  1.7 0.2 fusion.8
  2.0 0.1 fusion.5
  2.2 2.8 %concatenate.34.vv = bf16[8,32,768]{2,1,0:T(8,128)(2,1)} concatenate(bf16[8,4,768]{2,1,0:T(4,128)(2,1)S(1)} %get-tuple-element.9, bf16[8,4,768]{2,1,0:T(4,128)(2,1)S(1)} %get-tuple-element.8, bf16[8,4,768]{2,1,0:T(4,128)(2,1)S(1)} %get-tuple-element.9, bf16[8,4,768]{2,1,0:T(4,128)(2,1)S(1)} %get-tuple-element.7, bf16[8,4,768]{2,1,0:T(4,128)(2,1)S(1)} %get-tuple-element.9, ...), dimensions={1} | concatenate | bytes 786432 | tf_op jit(solution)/shard_map/concatenate | solution.py:351
  5.0 0.2 fusion.23
  5.2 0.6 fusion.43
  5.8 0.5 copy.46
  6.3 1.7 %copy.47 = f32[8,384,4]{2,1,0:T(8,128)} copy(f32[8,384,4]{1,0,2:T(8,128)S(1)} %get-tuple-element.10) | data formatting | bytes 98304 | tf_op jit(solution)/shard_map/reduce_precision | solution.py:54
  8.0 2.7 %fusion = (bf16[8,384,4]{2,1,0:T(8,128)(2,1)}, bf16[8,384,4]{2,1,0:T(8,128)(2,1)S(1)}) fusion(f32[8,384,4]{2,1,0:T(8,128)S(1)} %copy.46, f32[8,384,4]{2,1,0:T(8,128)} %copy.47), kind=kLoop, calls=%fused_computation.3 | loop fusion | flops 61440 | bytes 147456 | tf_op jit(solution)/shard_map/convert.11
  10.6 1.2 %copy.48 = bf16[8,384,4]{2,1,0:T(8,128)(2,1)S(1)} copy(bf16[8,384,4]{1,0,2:T(8,128)(2,1)} %get-tuple-element.11) | data formatting | bytes 49152 | tf_op jit(solution)/shard_map/convert.7
  11.9 1.0 broadcast_in_dim.28
  12.9 5.2 %concatenate.29.uu = bf16[8,384,32]{2,1,0:T(8,128)(2,1)} concatenate(bf16[8,384,4]{2,1,0:T(8,128)(2,1)S(1)} %copy.48, bf16[8,384,4]{2,1,0:T(8,128)(2,1)S(1)} %copy.48, bf16[8,384,4]{2,1,0:T(8,128)(2,1)S(1)} %get-tuple-element.6, bf16[8,384,4]{2,1,0:T(8,128)(2,1)S(1)} %copy.48, bf16[8,384,4]{2,1,0:T(8,128)(2,1)S(1)} %copy-done.1, bf16[8,384,4]{2,1,0:T(8,128)(2,1)S(1)} %get-tuple-element.6, ...), dimensions={2} | concatenate | bytes 393216 | tf_op jit(solution)/shard_map/concatenate | solution.py:350
  18.1 0.2 fusion.7
  18.4 0.8 maximum_maximum_fusion.rw
  19.6 0.7 broadcast_in_dim.32
  20.3 0.2 reduce_window_sum.11
  20.8 0.6 gather_fusion
  21.5 0.7 broadcast_shift-left_fusion
  22.2 0.3 add_bitcast_fusion
  22.8 0.2 tile.12
  23.1 0.7 concatenate.35.codes
  23.8 87.0 %shard_map.109 = bf16[384,768]{1,0:T(8,128)(2,1)} custom-call(bf16[8,384,384]{2,1,0:T(8,128)(2,1)} %img.1, bf16[3,256,384]{2,1,0:T(8,128)(2,1)} %constant.111.clone.left, bf16[768,768]{1,0:T(8,128)(2,1)} %constant.112.clone.right, bf16[8,384,32]{2,1,0:T(8,128)(2,1)} %concatenate.29.uu, bf16[8,32,768]{2,1,0:T(8,128)(2,1)} %concatenate.34.vv, ...), custom_call_target="tpu_custom_call" | custom-call | tf_op jit(solution)/shard_map/pallas_call | solution.py:388
  110.8 1.9 %copy.63 = bf16[24,16,768]{2,1,0:T(8,128)(2,1)} copy(bf16[24,16,768]{2,1,0:T(8,128)(2,1)} %bitcast.22) | data formatting | bytes 1179648
  (44 shorter events, 1.5 us)
Async XLA Ops:
  0.0 20.8 %copy-start = (s32[768,384]{1,0:T(8,128)S(1)}, s32[768,384]{1,0:T(8,128)}, u32[]{:S(2)}) copy-start(s32[768,384]{1,0:T(8,128)} %param.17) | copy-start | bytes 3538948
  0.0 5.0 %copy-start.4 = (s32[384]{0:T(512)S(1)}, s32[384]{0:T(512)}, u32[]{:S(2)}) copy-start(s32[384]{0:T(512)} %constant.110.clone) | copy-start | bytes 4612
  0.0 5.0 %copy-start.5 = (f32[384]{0:T(512)S(1)}, f32[384]{0:T(512)}, u32[]{:S(2)}) copy-start(f32[384]{0:T(512)} %constant.131) | copy-start | bytes 4612
  10.6 2.2 %copy-start.1 = (bf16[8,384,4]{2,1,0:T(8,128)(2,1)S(1)}, bf16[8,384,4]{2,1,0:T(8,128)(2,1)}, u32[]{:S(2)}) copy-start(bf16[8,384,4]{2,1,0:T(8,128)(2,1)} %get-tuple-element.5) | copy-start | bytes 73732
  12.9 5.2 %copy-start.3 = (f32[16]{0:T(128)S(1)}, f32[16]{0:T(128)}, u32[]{:S(2)}) copy-start(f32[16]{0:T(128)} %param.15) | copy-start | bytes 196
  12.9 7.5 %copy-start.2 = (s32[8,8]{1,0:T(8,128)S(1)}, s32[8,8]{1,0:T(8,128)}, u32[]{:S(2)}) copy-start(s32[8,8]{1,0:T(8,128)} %param.16) | copy-start | bytes 772
  12.9 7.9 %copy-start.6 = (s32[8]{0:T(128)S(1)}, s32[8]{0:T(128)}, u32[]{:S(2)}) copy-start(s32[8]{0:T(128)} %param.12) | copy-start | bytes 100

commit v2 on v1

v2 whole, which is shorter than its diff:
```python
import functools
import math

import jax
import jax.numpy as jnp
import ml_dtypes
import numpy as np
from jax import lax
from jax.experimental import pallas as pl
from jax.experimental.pallas import tpu as pltpu
from jax.sharding import PartitionSpec as P

TAU_PRIOR = 4.0
PHASE_OFFSET = 0.1
MESH = pl.DeviceIdType.MESH

K = 384
NB = 16
NS = 8
PP = 8
KYB = K // NB
CH = 6
KYC = KYB // CH
PAIRS = KYC // 2
ROWS = NB * KYC
BLK = KYC * PP
PL = 16
NDEF = 16
BF = jnp.bfloat16
F32 = jnp.float32
TURNS = (
    (0, 1), (1, 0), (0, 3), (3, 0), (1, 1), (1, 3), (3, 3), (3, 1),
    (1, 2), (2, 1), (3, 2), (2, 3), (0, 2), (2, 0), (2, 2),
)


def chunk_rows():
    rows = [
        KYB * b + KYC * c + i for c in range(CH) for b in range(NB) for i in range(KYC)
    ]
    return np.array(rows, np.int32).reshape(CH, NB * KYC)


def tables():
    index = np.arange(K)
    angle = 2.0 * np.pi / K * ((index[:, None] * index[None, :]) % K)
    cosine = (np.cos(angle) / math.sqrt(K)).astype(np.float32)
    sine = (np.sin(angle) / math.sqrt(K)).astype(np.float32)
    rows = chunk_rows()
    left = np.stack(
        [np.concatenate([cosine[r], -sine[r]], axis=0) for r in rows], axis=0
    ).astype(ml_dtypes.bfloat16)
    right = np.concatenate(
        [np.concatenate([cosine, -sine], 1), np.concatenate([sine, cosine], 1)], 0
    ).astype(ml_dtypes.bfloat16)
    return left, right


def kernel(
    img, left, right, u1r, u1i, u2r, u2i, v1r, v1i, v2r, v2i, code, tw, rw, ref,
    out,
    ub, vb, uu, secs, scr, cscr, codes, sendb, recvb, crecv, zsend, zrecv, nsend, nrecv, wts,
    code_s, code_r, row_s, row_r, z_s, z_r, n_s, n_r,
):
    mb = lax.axis_index("batch")
    ms = lax.axis_index("slab")
    core = lax.rem(ms, 2)
    zbase = ms - core
    mz = ms // 2
    me = mb * 2 + core
    my = mb // 4
    mx = lax.rem(mb, 4)

    def peer_of(turn):
        dy, dx = turn
        py = lax.rem(my + jnp.where(core == 0, dy, dx), 4)
        px = lax.rem(mx + jnp.where(core == 0, dx, 4 - dy), 4)
        return py * 4 + px

    barrier = pltpu.get_barrier_semaphore()

    def greet_plane(q, carry):
        i = lax.rem(me + q, 32)
        pl.semaphore_signal(
            barrier, inc=1, device_id=(i // 2, zbase + lax.rem(i, 2)), device_id_type=MESH
        )
        return carry

    def greet_slab(q, carry):
        pl.semaphore_signal(
            barrier, inc=1, device_id=(mb, lax.rem(ms + q, NS)), device_id_type=MESH
        )
        return carry

    lax.fori_loop(1, 32, greet_plane, 0)
    lax.fori_loop(1, NS, greet_slab, 0)

    def parts(x):
        high = x.astype(BF).astype(F32)
        return high, x - high

    zero = jnp.zeros((PP, K), F32)
    for k, x in enumerate((u1r, u1i, u2r, u2i)):
        high, rest = parts(x[...])
        ub[:, k, :] = high
        ub[:, 4 + k, :] = high
        ub[:, 8 + k, :] = rest
        ub[:, 12 + k, :] = zero
    plus = {n: parts(x[...]) for n, x in (("1r", v1r), ("1i", v1i), ("2r", v2r), ("2i", v2i))}
    sides = ((("1r", 1), ("1i", 1)), (("1i", -1), ("1r", 1)), (("2r", 1), ("2i", 1)), (("2i", -1), ("2r", 1)))
    for k, both in enumerate(sides):
        for h, (name, sign) in enumerate(both):
            high, rest = plus[name]
            cols = pl.ds(h * K, K)
            vb[:, k, cols] = high * sign
            vb[:, 4 + k, cols] = rest * sign
            vb[:, 8 + k, cols] = high * sign
            vb[:, 12 + k, cols] = zero
    for p in range(PP):
        uu[p] = ub[p].T.astype(BF)

    def compute(c):
        lc = left[c]

        def one_left(p, carry):
            sec = jnp.dot(lc, img[p], preferred_element_type=F32).astype(BF)
            start = pl.multiple_of(p * ROWS, ROWS)
            secs[pl.ds(start, ROWS), pl.ds(0, K)] = sec[:ROWS]
            secs[pl.ds(start, ROWS), pl.ds(K, K)] = sec[ROWS:]
            return carry

        lax.fori_loop(0, PP, one_left, 0, unroll=2)

        def four(t, carry):
            start = pl.multiple_of(t * 4 * ROWS, 4 * ROWS)
            spec = jnp.dot(
                secs[pl.ds(start, 4 * ROWS), :], right[...], preferred_element_type=F32
            )
            for j in range(4):
                p = t * 4 + j
                factor = jnp.dot(
                    uu[p, pl.ds(pl.multiple_of(c * ROWS, ROWS), ROWS), :],
                    vb[p].astype(BF),
                    preferred_element_type=F32,
                )
                rows = slice(j * ROWS, (j + 1) * ROWS)
                sr, si = spec[rows, :K], spec[rows, K:]
                fr, fi = factor[:, :K], factor[:, K:]
                wr = sr * fr - si * fi
                wi = sr * fi + si * fr
                for g in range(3):
                    cols = slice(g * 128, (g + 1) * 128)
                    scr[g, pl.ds(p, ROWS, stride=8), :] = wr[:, cols]
                    scr[3 + g, pl.ds(p, ROWS, stride=8), :] = wi[:, cols]
            return carry

        lax.fori_loop(0, PP // 4, four, 0)

        def pack(b, carry):
            start = pl.multiple_of(b * BLK, BLK)
            for h in range(2):
                for g in range(3):
                    sendb[c, b * 2 + h, :, pl.ds(g * 128, 128)] = scr[
                        3 * h + g, pl.ds(start, BLK), :
                    ].astype(BF)
            return carry

        lax.fori_loop(0, NB, pack, 0)

    def to_plane(b, h, src, dst, send_sem, recv_sem):
        pltpu.make_async_remote_copy(
            src_ref=src, dst_ref=dst, send_sem=send_sem, recv_sem=recv_sem,
            device_id=(b, zbase + h), device_id_type=MESH,
        ).start()

    def send_rows(c):
        other = 1 - core
        to_plane(mb, other, sendb.at[c, mb * 2 + other], recvb.at[c, me], row_s.at[c], row_r.at[c])
        pltpu.make_async_copy(sendb.at[c, me], recvb.at[c, me], row_r.at[c]).start()
        for flip in range(2):
            h = core if flip == 0 else other
            for turn in TURNS:
                b = peer_of(turn)
                to_plane(b, h, sendb.at[c, b * 2 + h], recvb.at[c, me], row_s.at[c], row_r.at[c])

    compute(0)

    row8 = lax.broadcasted_iota(jnp.int32, (PP, 128), 0)
    lane8 = lax.broadcasted_iota(jnp.int32, (PP, 128), 1)
    spread = jnp.where(lax.rem(lane8, PP) == row8, 1.0, 0.0)
    raw = code[...]

    def turned(x):
        return lax.dot_general(
            x.astype(F32), spread, (((0,), (0,)), ((), ())),
            precision=lax.Precision.HIGHEST, preferred_element_type=F32,
        ).astype(jnp.int32)

    cscr[...] = turned(raw & 255) + (turned(raw >> 8) << 8)
    even_lane = lax.rem(lax.broadcasted_iota(jnp.int32, (12, 128), 1) // PP, 2) == 0

    def arrange(b, carry):
        codes[b, pl.ds(0, 12), :] = jnp.where(
            even_lane,
            cscr[pl.ds(b * KYB, 12, stride=2), :],
            cscr[pl.ds(b * KYB + 1, 12, stride=2), :],
        )
        codes[b, pl.ds(12, 4), :] = jnp.zeros((4, 128), jnp.int32)
        return carry

    lax.fori_loop(0, NB, arrange, 0)

    pl.semaphore_wait(barrier, 31 + NS - 1)

    def send_codes(q, carry):
        i = lax.rem(me + q, 32)
        to_plane(
            i // 2, lax.rem(i, 2), codes.at[i // 2],
            crecv.at[pl.ds(pl.multiple_of(me * 16, 16), 16), :], code_s, code_r,
        )
        return carry

    send_rows(0)
    pltpu.make_async_copy(
        codes.at[mb], crecv.at[pl.ds(pl.multiple_of(me * 16, 16), 16), :], code_r
    ).start()
    lax.fori_loop(1, 32, send_codes, 0)

    def produce(c, carry):
        compute(c)
        send_rows(c)
        return carry

    lax.fori_loop(1, CH, produce, 0)

    pltpu.make_async_copy(crecv, crecv, code_r).wait()

    lane = lax.broadcasted_iota(jnp.int32, (32, 128), 1)
    sub = lax.broadcasted_iota(jnp.int32, (32, 128), 0)
    mine = (lane // 16) == lax.rem(sub, 8)

    def pair_codes(pair):
        got = crecv[pl.ds(pair, 32, stride=16), :]
        return jnp.sum(jnp.where(mine, got, 0).reshape(4, 8, 128), axis=1)

    spot = lax.broadcasted_iota(jnp.int32, (256, 128), 0)

    def one_hot(code4):
        place = code4 & 255
        return jnp.concatenate(
            [
                jnp.where(spot == place[g : g + 1, :], 1.0, 0.0).astype(BF)
                for g in range(4)
            ],
            axis=1,
        )

    row_id = lax.broadcasted_iota(jnp.int32, (128, 128), 0)
    row_class = jnp.where(row_id < 3 * NDEF, lax.rem(row_id, NDEF), -1)

    def count(pair, carry):
        code4 = pair_codes(pair)
        kind = code4 >> 8
        kinds = jnp.concatenate(
            [
                jnp.where(row_class == kind[g : g + 1, :], 1.0, 0.0).astype(BF)
                for g in range(4)
            ],
            axis=1,
        )
        tally = lax.dot_general(
            one_hot(code4), kinds, (((1,), (1,)), ((), ())), preferred_element_type=F32
        )
        start = pl.multiple_of(pair * 32, 32)
        nsend[:, pl.ds(start, 32), :] = tally.astype(BF).reshape(NS, 32, 128)
        return carry

    lax.fori_loop(0, CH * PAIRS, count, 0)

    pltpu.make_async_copy(nsend.at[ms], nrecv.at[mz], n_r).start()

    def send_counts(q, carry):
        peer = lax.rem(ms + 2 * q, NS)
        pltpu.make_async_remote_copy(
            src_ref=nsend.at[peer], dst_ref=nrecv.at[mz], send_sem=n_s, recv_sem=n_r,
            device_id=(mb, peer), device_id_type=MESH,
        ).start()
        return carry

    lax.fori_loop(1, NS // 2, send_counts, 0)

    def scatter(c, carry):
        pltpu.make_async_copy(recvb.at[c], recvb.at[c], row_r.at[c]).wait()

        def one(j, inner):
            pair = c * PAIRS + j
            start = pl.multiple_of(j * 16, 16)
            rows = recvb[c, :, pl.ds(start, 16), :].reshape(512, K)
            hot = one_hot(pair_codes(pair))
            part = jnp.dot(hot, rows, preferred_element_type=F32)
            zsend[pair] = part.astype(BF).reshape(NS, 32, K)
            for q in range(1, NS):
                peer = lax.rem(ms + q, NS)
                pltpu.make_async_remote_copy(
                    src_ref=zsend.at[pair, peer], dst_ref=zrecv.at[pair, ms],
                    send_sem=z_s.at[pair], recv_sem=z_r.at[pair],
                    device_id=(mb, peer), device_id_type=MESH,
                ).start()
            pltpu.make_async_copy(zsend.at[pair, ms], zrecv.at[pair, ms], z_r.at[pair]).start()
            return inner

        lax.fori_loop(0, PAIRS, one, 0)
        return carry

    lax.fori_loop(0, CH, scatter, 0)

    pltpu.make_async_copy(nrecv, nrecv, n_r).wait()
    totals = (
        nrecv[0].astype(F32) + nrecv[1].astype(F32) + nrecv[2].astype(F32) + nrecv[3].astype(F32)
    )
    scaled = (totals.reshape(KYB, PL, 128) * tw[...][:, None, :]).reshape(KYB * PL, 128)
    wts[...] = (
        jnp.dot(scaled, rw[...], precision=lax.Precision.HIGHEST, preferred_element_type=F32)
        + TAU_PRIOR
    )

    def finish(pair, carry):
        pltpu.make_async_copy(zrecv.at[pair], zrecv.at[pair], z_r.at[pair]).wait()
        start = pl.multiple_of(pair * 32, 32)
        inverse = 1.0 / wts[pl.ds(start, 32), :]
        for h in range(2):
            total = TAU_PRIOR * ref[pl.ds(start, 32), pl.ds(h * K, K)].astype(F32)
            for z in range(NS // 2):
                total += zrecv[pair, 2 * z + h].astype(F32)
            out[pl.ds(start, 32), pl.ds(h * K, K)] = (total * inverse).astype(BF)
        return carry

    lax.fori_loop(0, CH * PAIRS, finish, 0)

    def drain(src, dst, send_sem, recv_sem):
        pltpu.make_async_remote_copy(
            src_ref=src, dst_ref=dst, send_sem=send_sem, recv_sem=recv_sem,
            device_id=(mb, ms), device_id_type=MESH,
        ).wait_send()

    drain(crecv.at[pl.ds(0, 31 * 16), :], crecv.at[pl.ds(0, 31 * 16), :], code_s, code_r)
    drain(nsend.at[pl.ds(0, 3)], nsend.at[pl.ds(0, 3)], n_s, n_r)

    def drain_rows(c, carry):
        drain(sendb.at[c, pl.ds(0, 31)], recvb.at[c, pl.ds(0, 31)], row_s.at[c], row_r.at[c])
        return carry

    def drain_sums(pair, carry):
        drain(zsend.at[pair, pl.ds(0, 7)], zrecv.at[pair, pl.ds(0, 7)], z_s.at[pair], z_r.at[pair])
        return carry

    lax.fori_loop(0, CH, drain_rows, 0)
    lax.fori_loop(0, CH * PAIRS, drain_sums, 0)


def per_device(images, classes, shifts, defocus_class, defocus, run_counts, dest_map, ref):
    left, right = tables()
    order = chunk_rows().reshape(-1)
    freq = np.arange(K)

    def square(k):
        half = ((k + K // 2) % K - K // 2).astype(np.float32) / np.float32(K)
        return half * half

    own_focus = jnp.sum(
        jnp.where(defocus_class[:, None] == jnp.arange(NDEF)[None, :], defocus[None, :], 0.0),
        axis=1,
    )
    step = 2.0 * math.pi / K
    turn_y = step * ((jnp.asarray(order, jnp.int32)[None, :] * shifts[:, 1:2]) % K).astype(F32)
    turn_x = step * ((jnp.asarray(freq, jnp.int32)[None, :] * shifts[:, 0:1]) % K).astype(F32)
    eyr, eyi = jnp.cos(turn_y), -jnp.sin(turn_y)
    exr, exi = jnp.cos(turn_x), -jnp.sin(turn_x)
    arg_y = own_focus[:, None] * jnp.asarray(square(order))[None, :] + PHASE_OFFSET
    arg_x = own_focus[:, None] * jnp.asarray(square(freq))[None, :]
    say, cay = -jnp.sin(arg_y), -jnp.cos(arg_y)
    cbx, sbx = jnp.cos(arg_x), jnp.sin(arg_x)
    factors = (
        say * eyr, say * eyi, cay * eyr, cay * eyi,
        cbx * exr, cbx * exi, sbx * exr, sbx * exi,
    )

    freq = jnp.arange(K, dtype=jnp.int32)
    ends = jnp.cumsum(run_counts, axis=1)
    slab = jnp.sum((freq[None, :, None] >= ends[:, None, :]).astype(jnp.int32), axis=2)
    code = (
        (defocus_class[:, None] << 8) + slab * 32 + (freq % 2 * 16)[None, :] + dest_map[classes]
    )

    def by_class(lane_of, arg, scale_cos):
        group = lane_of // NDEF
        return jnp.where(
            group == 0,
            scale_cos[0] * jnp.cos(arg),
            jnp.where(
                group == 1, scale_cos[1] * jnp.sin(arg), jnp.where(group == 2, scale_cos[2], 0.0)
            ),
        )

    many = jnp.tile(defocus, 128 // NDEF)
    own_rows = lax.axis_index("batch") * KYB + jnp.arange(KYB, dtype=jnp.int32)
    own_half = ((own_rows + K // 2) % K - K // 2).astype(F32) / K
    arg2_y = 2.0 * (many[None, :] * (own_half * own_half)[:, None] + PHASE_OFFSET)
    arg2_x = 2.0 * (many[:, None] * jnp.asarray(square(np.arange(K)))[None, :])
    lanes = jnp.arange(128, dtype=jnp.int32)
    tw = by_class(lanes[None, :], arg2_y, (-0.5, 0.5, 0.5))
    rw = by_class(lanes[:, None], arg2_x, (1.0, 1.0, 1.0))

    vmem = pl.BlockSpec(memory_space=pltpu.VMEM)
    dma = pltpu.SemaphoreType.DMA
    pairs = CH * PAIRS
    out = pl.pallas_call(
        kernel,
        out_shape=jax.ShapeDtypeStruct((KYB * PL, 2 * K), BF),
        in_specs=[vmem] * 15,
        out_specs=vmem,
        scratch_shapes=[
            pltpu.VMEM((PP, 16, K), F32),
            pltpu.VMEM((PP, 16, 2 * K), F32),
            pltpu.VMEM((PP, K, 16), BF),
            pltpu.VMEM((PP * ROWS, 2 * K), BF),
            pltpu.VMEM((6, PP * ROWS, 128), F32),
            pltpu.VMEM((K, 128), jnp.int32),
            pltpu.VMEM((NB, 16, 128), jnp.int32),
            pltpu.VMEM((CH, 32, BLK, K), BF),
            pltpu.VMEM((CH, 32, BLK, K), BF),
            pltpu.VMEM((32 * 16, 128), jnp.int32),
            pltpu.VMEM((pairs, NS, 2 * PL, K), BF),
            pltpu.VMEM((pairs, NS, 2 * PL, K), BF),
            pltpu.VMEM((NS, KYB * PL, 128), BF),
            pltpu.VMEM((NS // 2, KYB * PL, 128), BF),
            pltpu.VMEM((KYB * PL, K), F32),
            dma, dma, dma((CH,)), dma((CH,)), dma((pairs,)), dma((pairs,)), dma, dma,
        ],
        compiler_params=pltpu.CompilerParams(
            collective_id=0, has_side_effects=True, vmem_limit_bytes=60 * 1024 * 1024
        ),
    )(
        images, jnp.asarray(left), jnp.asarray(right), *factors, code, tw, rw,
        ref.reshape(KYB * PL, 2 * K),
    )
    return out.reshape(KYB, PL, 2 * K)


def solution(mesh):
    placed = (
        P(("batch", "slab"), None, None),
        P(("batch", "slab")),
        P(("batch", "slab"), None),
        P(("batch", "slab")),
        P(),
        P(("batch", "slab"), None),
        P(),
        P("batch", "slab", None),
    )
    return jax.shard_map(
        per_device, mesh=mesh, in_specs=placed, out_specs=P("batch", "slab", None), check_vma=False
    )
```

time: 113 us -> 90.6 us (0.80)
  local copies, waits for them, and re-layouts: 18.3 us -> 3.98 us
  Pallas kernels: 87 us -> 77.8 us
  other arithmetic: 7.11 us -> 8.5 us
    pallas_call x1, Pallas kernels: 87 us -> 77.8 us  [per_device(): pl.pallas_call(kernel, out_shape=jax.ShapeDtypeStruct((KYB * PL, 2 * K),...]
    concatenate x6 -> x0, local copies, waits for them, and re-layouts: 8.88 us -> none  [the longest x1 5.19 us: per_device(): uu = jnp.concatenate([uh, uh, um, uh, ul, um, zu], axis=2).astype(BF)]
    select_n x1 -> x5, other arithmetic: 0.01 us -> 3.73 us  [the longest x2 2.97 us: by_class(): jnp.where(group == 0, scale_cos[0] * jnp.cos(arg), jnp.where(group == 1,...]
    another operation x4 -> x0, other arithmetic: 2.82 us -> none
    another operation x11 -> x0, local copies, waits for them, and re-layouts: 2.28 us -> none
    reduce_precision x1 -> x0, local copies, waits for them, and re-layouts: 1.67 us -> none  [split3(): high = lax.reduce_precision(x, 8, 7)]
where the time goes in v2:
time: 90.6 us; the launch traced here: 90.3 us
  Pallas kernels  77.8 us (86%)
  other arithmetic  8.5 us (9%)
  local copies, waits for them, and re-layouts  3.98 us (4%)
    pallas_call x1, Pallas kernels, per_device(): pl.pallas_call(kernel, out_shape=jax.ShapeDtypeStruct((KYB * PL, 2 * K),...  77.8 us
    select_n x2, other arithmetic, by_class(): jnp.where(group == 0, scale_cos[0] * jnp.cos(arg), jnp.where(group == 1,...  2.97 us
    unnamed x3, local copies, waits for them, and re-layouts  1.92 us

profile of v2, /device:TPU:1, one launch (start us, length us, event | category | flops | bytes accessed | tf_op | source)
XLA Modules:
  0.0 90.3 jit_solution(8515320699599147971)
XLA Ops:
  0.0 0.0 copy-start
  0.0 0.8 compare_select_fusion
  0.8 0.7 broadcast_shift-left_fusion
  1.4 0.9 select_reduce_fusion
  2.3 0.8 slice_bitcast_fusion
  3.1 0.8 reduce_window_sum.11
  3.9 0.7 broadcast_in_dim.94
  4.6 0.1 mul.189
  4.7 0.1 convert_reduce_fusion
  4.8 0.0 copy-done
  4.8 0.6 gather_fusion
  5.4 0.7 add_add_fusion.code
  6.0 0.7 select_select_fusion.1.tw
  6.8 1.6 %fusion.2 = (f32[8,384]{1,0:T(8,128)}, f32[8,384]{1,0:T(8,128)}, f32[8,384]{1,0:T(8,128)}, f32[8,384]{1,0:T(8,128)}, f32[8,384]{1,0:T(8,128)}, /*index=5*/f32[8,384]{1,0:T(8,128)}, f32[8,384]{1,0:T(8,128)}, f32[8,384]{1,0:T(8,128)}) fusion(s32[8]{0:T(128)S(1)} %get-tuple-element.13, f32[384]{0:T(512)} %constant.136.clone, f32[8]{0:T(128)S(1)} %select_reduce_fusion, ...), kind=kLoop, calls=%fused_computation.10 | loop fusion | flops 98304 | bytes 103008 | tf_op jit(solution)/shard_map/mul | solution.py:385
  8.4 2.2 %select_select_fusion.rw = f32[128,384]{1,0:T(8,128)} fusion(f32[128]{0:T(128)S(1)} %compare_select_fusion.1, f32[384]{0:T(512)} %constant.136.clone, f32[128]{0:T(128)S(1)} %mul.189, pred[128]{0:T(512)(128)(4,1)S(1)} %get-tuple-element.20, pred[128]{0:T(512)(128)(4,1)S(1)} %get-tuple-element.19), kind=kLoop, calls=%fused_computation.1 | loop fusion | flops 196608 | bytes 199424 | tf_op jit(solution)/shard_map/jit(_where)/select_n | solution.py:397
  10.6 77.8 %shard_map.145 = bf16[384,768]{1,0:T(8,128)(2,1)} custom-call(bf16[8,384,384]{2,1,0:T(8,128)(2,1)} %img.1, bf16[6,128,384]{2,1,0:T(8,128)(2,1)} %constant.137.clone.left, bf16[768,768]{1,0:T(8,128)(2,1)} %constant.138.clone.right, f32[8,384]{1,0:T(8,128)} %get-tuple-element.15.u1r, f32[8,384]{1,0:T(8,128)} %get-tuple-element.17.u1i, ...), custom_call_target="tpu_custom_call" | custom-call | tf_op jit(solution)/shard_map/pallas_call | solution.py:417
  88.4 1.9 %copy.17 = bf16[24,16,768]{2,1,0:T(8,128)(2,1)} copy(bf16[24,16,768]{2,1,0:T(8,128)(2,1)} %bitcast.6) | data formatting | bytes 1179648
  (6 shorter events, 0.0 us)
Async XLA Ops:
  0.0 4.8 %copy-start = (s32[768,384]{1,0:T(8,128)S(1)}, s32[768,384]{1,0:T(8,128)}, u32[]{:S(2)}) copy-start(s32[768,384]{1,0:T(8,128)} %param.21) | copy-start | bytes 3538948

commit v3 on v2

--- a/solution.py
+++ b/solution.py
@@ -1,4 +1,3 @@
-import functools
 import math
 
 import jax
@@ -57,10 +56,10 @@
 
 
 def kernel(
-    img, left, right, u1r, u1i, u2r, u2i, v1r, v1i, v2r, v2i, code, tw, rw, ref,
+    classes, kinds_in, defocus, shifts, counts, left, img_in, right_in, dest_in, ref_in,
     out,
-    ub, vb, uu, secs, scr, cscr, codes, sendb, recvb, crecv, zsend, zrecv, nsend, nrecv, wts,
-    code_s, code_r, row_s, row_r, z_s, z_r, n_s, n_r,
+    img, right, dest, ref, ub, vb, uu, secs, scr, cscr, codes, sendb, recvb, crecv, zsend, zrecv, nsend, nrecv, wts,
+    img_m, right_m, dest_m, ref_m, code_s, code_r, row_s, row_r, z_s, z_r, n_s, n_r,
 ):
     mb = lax.axis_index("batch")
     ms = lax.axis_index("slab")
@@ -78,6 +77,12 @@
         return py * 4 + px
 
     barrier = pltpu.get_barrier_semaphore()
+    loads = [pltpu.make_async_copy(img_in.at[p], img.at[p], img_m.at[p]) for p in range(PP)]
+    load_right = pltpu.make_async_copy(right_in, right, right_m)
+    load_dest = pltpu.make_async_copy(dest_in, dest, dest_m)
+    load_ref = pltpu.make_async_copy(ref_in, ref, ref_m)
+    for load in (*loads, load_right, load_dest, load_ref):
+        load.start()
 
     def greet_plane(q, carry):
         i = lax.rem(me + q, 32)
@@ -99,18 +104,46 @@
         high = x.astype(BF).astype(F32)
         return high, x - high
 
+    sub_p = lax.broadcasted_iota(jnp.int32, (PP, K), 0)
+    col = lax.broadcasted_iota(jnp.int32, (PP, K), 1)
+    order = ((col // KYC) & (NB - 1)) * KYB + (col // ROWS) * KYC + (col & (KYC - 1))
+
+    def pick(index, values):
+        got = jnp.full(index.shape, values[0])
+        for i, value in enumerate(values[1:], 1):
+            got = jnp.where(index == i, value, got)
+        return got
+
+    def square(k):
+        half = jnp.where(k >= K // 2, k - K, k).astype(F32) * (1.0 / K)
+        return half * half
+
+    def wave(k, shift):
+        turn = (k * shift).astype(F32)
+        turn = turn - K * jnp.floor((turn + 0.5) * (1.0 / K))
+        angle = turn * (2.0 * math.pi / K)
+        return jnp.cos(angle), -jnp.sin(angle)
+
+    eyr, eyi = wave(order, pick(sub_p, [shifts[1, p] for p in range(PP)]))
+    exr, exi = wave(col, pick(sub_p, [shifts[0, p] for p in range(PP)]))
+    focus = pick(sub_p, [defocus[kinds_in[p]] for p in range(PP)])
+    arg_y = focus * square(order) + PHASE_OFFSET
+    arg_x = focus * square(col)
+    say, cay = -jnp.sin(arg_y), -jnp.cos(arg_y)
+    cbx, sbx = jnp.cos(arg_x), jnp.sin(arg_x)
+
     zero = jnp.zeros((PP, K), F32)
-    for k, x in enumerate((u1r, u1i, u2r, u2i)):
-        high, rest = parts(x[...])
+    for k, x in enumerate((say * eyr, say * eyi, cay * eyr, cay * eyi)):
+        high, rest = parts(x)
         ub[:, k, :] = high
         ub[:, 4 + k, :] = high
         ub[:, 8 + k, :] = rest
         ub[:, 12 + k, :] = zero
-    plus = {n: parts(x[...]) for n, x in (("1r", v1r), ("1i", v1i), ("2r", v2r), ("2i", v2i))}
-    sides = ((("1r", 1), ("1i", 1)), (("1i", -1), ("1r", 1)), (("2r", 1), ("2i", 1)), (("2i", -1), ("2r", 1)))
+    side = [parts(x) for x in (cbx * exr, cbx * exi, sbx * exr, sbx * exi)]
+    sides = (((0, 1), (1, 1)), ((1, -1), (0, 1)), ((2, 1), (3, 1)), ((3, -1), (2, 1)))
     for k, both in enumerate(sides):
         for h, (name, sign) in enumerate(both):
-            high, rest = plus[name]
+            high, rest = side[name]
             cols = pl.ds(h * K, K)
             vb[:, k, cols] = high * sign
             vb[:, 4 + k, cols] = rest * sign
@@ -119,10 +152,12 @@
     for p in range(PP):
         uu[p] = ub[p].T.astype(BF)
 
-    def compute(c):
+    def compute(c, first=False):
         lc = left[c]
 
         def one_left(p, carry):
+            if first:
+                pltpu.make_async_copy(img_in.at[p], img.at[p], img_m.at[p]).wait()
             sec = jnp.dot(lc, img[p], preferred_element_type=F32).astype(BF)
             start = pl.multiple_of(p * ROWS, ROWS)
             secs[pl.ds(start, ROWS), pl.ds(0, K)] = sec[:ROWS]
@@ -130,6 +165,8 @@
             return carry
 
         lax.fori_loop(0, PP, one_left, 0, unroll=2)
+        if first:
+            load_right.wait()
 
         def four(t, carry):
             start = pl.multiple_of(t * 4 * ROWS, 4 * ROWS)
@@ -183,12 +220,31 @@
                 b = peer_of(turn)
                 to_plane(b, h, sendb.at[c, b * 2 + h], recvb.at[c, me], row_s.at[c], row_r.at[c])
 
-    compute(0)
-
+    compute(0, first=True)
+
+    pl.semaphore_wait(barrier, 31 + NS - 1)
+
+    def send_codes(q, carry):
+        i = lax.rem(me + q, 32)
+        to_plane(
+            i // 2, lax.rem(i, 2), codes.at[i // 2],
+            crecv.at[pl.ds(pl.multiple_of(me * 16, 16), 16), :], code_s, code_r,
+        )
+        return carry
+
+    send_rows(0)
     row8 = lax.broadcasted_iota(jnp.int32, (PP, 128), 0)
     lane8 = lax.broadcasted_iota(jnp.int32, (PP, 128), 1)
     spread = jnp.where(lax.rem(lane8, PP) == row8, 1.0, 0.0)
-    raw = code[...]
+    load_dest.wait()
+    end = counts[:, 0:1]
+    slab = jnp.zeros((PP, K), jnp.int32)
+    for i in range(1, NS):
+        slab = slab + jnp.where(col >= end, 1, 0)
+        end = end + counts[:, i : i + 1]
+    plane = pick(sub_p, [dest[pl.ds(classes[p], 1), :] for p in range(PP)])
+    place = slab * 32 + (col & 1) * PL + plane
+    kind_p = pick(sub_p, [kinds_in[p] for p in range(PP)])
 
     def turned(x):
         return lax.dot_general(
@@ -196,7 +252,7 @@
             precision=lax.Precision.HIGHEST, preferred_element_type=F32,
         ).astype(jnp.int32)
 
-    cscr[...] = turned(raw & 255) + (turned(raw >> 8) << 8)
+    cscr[...] = turned(place) + (turned(kind_p) << 8)
     even_lane = lax.rem(lax.broadcasted_iota(jnp.int32, (12, 128), 1) // PP, 2) == 0
 
     def arrange(b, carry):
@@ -210,17 +266,6 @@
 
     lax.fori_loop(0, NB, arrange, 0)
 
-    pl.semaphore_wait(barrier, 31 + NS - 1)
-
-    def send_codes(q, carry):
-        i = lax.rem(me + q, 32)
-        to_plane(
-            i // 2, lax.rem(i, 2), codes.at[i // 2],
-            crecv.at[pl.ds(pl.multiple_of(me * 16, 16), 16), :], code_s, code_r,
-        )
-        return carry
-
-    send_rows(0)
     pltpu.make_async_copy(
         codes.at[mb], crecv.at[pl.ds(pl.multiple_of(me * 16, 16), 16), :], code_r
     ).start()
@@ -288,6 +333,29 @@
         return carry
 
     lax.fori_loop(1, NS // 2, send_counts, 0)
+
+    lane_k = lax.broadcasted_iota(jnp.int32, (KYB, 128), 1)
+    own_ky = mb * KYB + lax.broadcasted_iota(jnp.int32, (KYB, 128), 0)
+    every = [defocus[i] for i in range(NDEF)]
+    arg2_y = 2.0 * (pick(lane_k & (NDEF - 1), every) * square(own_ky) + PHASE_OFFSET)
+    group = lane_k // NDEF
+    tw = jnp.where(
+        group == 0,
+        -0.5 * jnp.cos(arg2_y),
+        jnp.where(group == 1, 0.5 * jnp.sin(arg2_y), jnp.where(group == 2, 0.5, 0.0)),
+    )
+    row_k = lax.broadcasted_iota(jnp.int32, (NDEF, K), 0)
+    col_k = lax.broadcasted_iota(jnp.int32, (NDEF, K), 1)
+    arg2_x = 2.0 * (pick(row_k, every) * square(col_k))
+    rw = jnp.concatenate(
+        [
+            jnp.cos(arg2_x),
+            jnp.sin(arg2_x),
+            jnp.ones((NDEF, K), F32),
+            jnp.zeros((128 - 3 * NDEF, K), F32),
+        ],
+        axis=0,
+    )
 
     def scatter(c, carry):
         pltpu.make_async_copy(recvb.at[c], recvb.at[c], row_r.at[c]).wait()
@@ -314,13 +382,14 @@
 
     lax.fori_loop(0, CH, scatter, 0)
 
+    load_ref.wait()
     pltpu.make_async_copy(nrecv, nrecv, n_r).wait()
     totals = (
         nrecv[0].astype(F32) + nrecv[1].astype(F32) + nrecv[2].astype(F32) + nrecv[3].astype(F32)
     )
-    scaled = (totals.reshape(KYB, PL, 128) * tw[...][:, None, :]).reshape(KYB * PL, 128)
+    scaled = (totals.reshape(KYB, PL, 128) * tw[:, None, :]).reshape(KYB * PL, 128)
     wts[...] = (
-        jnp.dot(scaled, rw[...], precision=lax.Precision.HIGHEST, preferred_element_type=F32)
+        jnp.dot(scaled, rw, precision=lax.Precision.HIGHEST, preferred_element_type=F32)
         + TAU_PRIOR
     )
 
@@ -360,66 +429,21 @@
 
 def per_device(images, classes, shifts, defocus_class, defocus, run_counts, dest_map, ref):
     left, right = tables()
-    order = chunk_rows().reshape(-1)
-    freq = np.arange(K)
-
-    def square(k):
-        half = ((k + K // 2) % K - K // 2).astype(np.float32) / np.float32(K)
-        return half * half
-
-    own_focus = jnp.sum(
-        jnp.where(defocus_class[:, None] == jnp.arange(NDEF)[None, :], defocus[None, :], 0.0),
-        axis=1,
-    )
-    step = 2.0 * math.pi / K
-    turn_y = step * ((jnp.asarray(order, jnp.int32)[None, :] * shifts[:, 1:2]) % K).astype(F32)
-    turn_x = step * ((jnp.asarray(freq, jnp.int32)[None, :] * shifts[:, 0:1]) % K).astype(F32)
-    eyr, eyi = jnp.cos(turn_y), -jnp.sin(turn_y)
-    exr, exi = jnp.cos(turn_x), -jnp.sin(turn_x)
-    arg_y = own_focus[:, None] * jnp.asarray(square(order))[None, :] + PHASE_OFFSET
-    arg_x = own_focus[:, None] * jnp.asarray(square(freq))[None, :]
-    say, cay = -jnp.sin(arg_y), -jnp.cos(arg_y)
-    cbx, sbx = jnp.cos(arg_x), jnp.sin(arg_x)
-    factors = (
-        say * eyr, say * eyi, cay * eyr, cay * eyi,
-        cbx * exr, cbx * exi, sbx * exr, sbx * exi,
-    )
-
-    freq = jnp.arange(K, dtype=jnp.int32)
-    ends = jnp.cumsum(run_counts, axis=1)
-    slab = jnp.sum((freq[None, :, None] >= ends[:, None, :]).astype(jnp.int32), axis=2)
-    code = (
-        (defocus_class[:, None] << 8) + slab * 32 + (freq % 2 * 16)[None, :] + dest_map[classes]
-    )
-
-    def by_class(lane_of, arg, scale_cos):
-        group = lane_of // NDEF
-        return jnp.where(
-            group == 0,
-            scale_cos[0] * jnp.cos(arg),
-            jnp.where(
-                group == 1, scale_cos[1] * jnp.sin(arg), jnp.where(group == 2, scale_cos[2], 0.0)
-            ),
-        )
-
-    many = jnp.tile(defocus, 128 // NDEF)
-    own_rows = lax.axis_index("batch") * KYB + jnp.arange(KYB, dtype=jnp.int32)
-    own_half = ((own_rows + K // 2) % K - K // 2).astype(F32) / K
-    arg2_y = 2.0 * (many[None, :] * (own_half * own_half)[:, None] + PHASE_OFFSET)
-    arg2_x = 2.0 * (many[:, None] * jnp.asarray(square(np.arange(K)))[None, :])
-    lanes = jnp.arange(128, dtype=jnp.int32)
-    tw = by_class(lanes[None, :], arg2_y, (-0.5, 0.5, 0.5))
-    rw = by_class(lanes[:, None], arg2_x, (1.0, 1.0, 1.0))
-
     vmem = pl.BlockSpec(memory_space=pltpu.VMEM)
+    smem = pl.BlockSpec(memory_space=pltpu.SMEM)
+    far = pl.BlockSpec(memory_space=pl.ANY)
     dma = pltpu.SemaphoreType.DMA
     pairs = CH * PAIRS
     out = pl.pallas_call(
         kernel,
         out_shape=jax.ShapeDtypeStruct((KYB * PL, 2 * K), BF),
-        in_specs=[vmem] * 15,
+        in_specs=[smem] * 4 + [vmem] * 2 + [far] * 4,
         out_specs=vmem,
         scratch_shapes=[
+            pltpu.VMEM((PP, K, K), BF),
+            pltpu.VMEM((2 * K, 2 * K), BF),
+            pltpu.VMEM(dest_map.shape, jnp.int32),
+            pltpu.VMEM((KYB * PL, 2 * K), BF),
             pltpu.VMEM((PP, 16, K), F32),
             pltpu.VMEM((PP, 16, 2 * K), F32),
             pltpu.VMEM((PP, K, 16), BF),
@@ -435,14 +459,14 @@
             pltpu.VMEM((NS, KYB * PL, 128), BF),
             pltpu.VMEM((NS // 2, KYB * PL, 128), BF),
             pltpu.VMEM((KYB * PL, K), F32),
-            dma, dma, dma((CH,)), dma((CH,)), dma((pairs,)), dma((pairs,)), dma, dma,
+            dma((PP,)), dma, dma, dma, dma, dma, dma((CH,)), dma((CH,)), dma((pairs,)), dma((pairs,)), dma, dma,
         ],
         compiler_params=pltpu.CompilerParams(
             collective_id=0, has_side_effects=True, vmem_limit_bytes=60 * 1024 * 1024
         ),
     )(
-        images, jnp.asarray(left), jnp.asarray(right), *factors, code, tw, rw,
-        ref.reshape(KYB * PL, 2 * K),
+        classes, defocus_class, defocus, shifts.T, run_counts, jnp.asarray(left), images,
+        jnp.asarray(right), dest_map, ref.reshape(KYB * PL, 2 * K),
     )
     return out.reshape(KYB, PL, 2 * K)
 

time: 90.6 us -> 79.2 us (0.87)
  other arithmetic: 8.5 us -> 0 us
  local copies, waits for them, and re-layouts: 3.98 us -> 1.92 us
    select_n x5 -> x0, other arithmetic: 3.73 us -> none  [the longest x2 2.97 us: by_class(): jnp.where(group == 0, scale_cos[0] * jnp.cos(arg), jnp.where(group == 1,...]
    mul x3 -> x0, other arithmetic: 1.63 us -> none  [the longest x1 1.6 us: per_device(): sbx * exi]
    reduce_sum x2 -> x0, other arithmetic: 0.95 us -> none  [the longest x1 0.85 us: per_device(): jnp.sum(jnp.where(defocus_class[:, None] == jnp.arange(NDEF)[None, :], de...]
    unnamed x3 -> x1, local copies, waits for them, and re-layouts: 1.92 us -> 1.92 us
where the time goes in v3:
time: 79.2 us; the launch traced here: 79 us
  Pallas kernels  77.1 us (97%)
  local copies, waits for them, and re-layouts  1.92 us (2%)
    pallas_call x1, Pallas kernels, per_device(): pl.pallas_call(kernel, out_shape=jax.ShapeDtypeStruct((KYB * PL, 2 * K),...  77.1 us
    unnamed x1, local copies, waits for them, and re-layouts  1.92 us

profile of v3, /device:TPU:1, one launch (start us, length us, event | category | flops | bytes accessed | tf_op | source)
XLA Modules:
  0.0 79.0 jit_solution(14282355994852820191)
XLA Ops:
  0.0 77.1 %shard_map.100 = bf16[384,768]{1,0:T(8,128)(2,1)} custom-call(s32[8]{0:T(128)} %classes.1, s32[8]{0:T(128)} %kinds_in.1, f32[16]{0:T(128)} %defocus.1, s32[2,8]{1,0:T(2,128)} %bitcast.5, s32[8,8]{1,0:T(8,128)} %counts.1, bf16[6,128,384]{2,1,0:T(8,128)(2,1)} %constant.4.clone.left, bf16[8,384,384]{2,1,0:T(8,128)(2,1)} %img_in.1, ...), custom_call_target="tpu_custom_call" | custom-call | tf_op jit(solution)/shard_map/pallas_call | solution.py:437
  77.1 1.9 %copy.12 = bf16[24,16,768]{2,1,0:T(8,128)(2,1)} copy(bf16[24,16,768]{2,1,0:T(8,128)(2,1)} %bitcast.3) | data formatting | bytes 1179648

commit v4 on v3

v4 whole, which is shorter than its diff:
```python
import math

import jax
import jax.numpy as jnp
import ml_dtypes
import numpy as np
from jax import lax
from jax.experimental import pallas as pl
from jax.experimental.pallas import tpu as pltpu
from jax.sharding import PartitionSpec as P

TAU_PRIOR = 4.0
PHASE_OFFSET = 0.1
MESH = pl.DeviceIdType.MESH

K = 384
NB = 16
NS = 8
PP = 8
KYB = K // NB
SHARED = 3
TILES = SHARED + 1
PL = 16
NDEF = 16
BF = jnp.bfloat16
F32 = jnp.float32
SLOTS = (
    ((1, 2), (3, 4), (11, 11), (0, 12)),
    ((5, 6), (7, 8), (9, 10), (5, 6)),
)
EXTRA = (((13, 14), (15, 16), (17, 17)), ((18, 19), (20, 21), (22, 23)))
COUNTED = tuple(SLOTS[h] + EXTRA[h] for h in range(2))
NCNT = len(COUNTED[0])
TURNS = (
    (0, 1), (1, 0), (0, 3), (3, 0), (1, 1), (1, 3), (3, 3), (3, 1),
    (1, 2), (2, 1), (3, 2), (2, 3), (0, 2), (2, 0), (2, 2),
)


def tables():
    index = np.arange(K)
    angle = 2.0 * np.pi / K * ((index[:, None] * index[None, :]) % K)
    cosine = (np.cos(angle) / math.sqrt(K)).astype(np.float32)
    sine = (np.sin(angle) / math.sqrt(K)).astype(np.float32)

    def left(t, cores):
        rows = [KYB * b + i for h in cores for b in range(NB) for i in SLOTS[h][t]]
        return np.concatenate([cosine[rows], -sine[rows]], axis=0)

    both = np.stack([left(t, (0, 1)) for t in range(SHARED)], axis=0)
    right = np.concatenate(
        [np.concatenate([cosine, -sine], 1), np.concatenate([sine, cosine], 1)], 0
    )
    kind = ml_dtypes.bfloat16
    return both.astype(kind), left(SHARED, (0,)).astype(kind), right.astype(kind)


def kernel(
    classes, kinds_in, defocus, shifts, counts, left, left_last, img_in, right_in, dest_in, ref_in,
    out,
    img, right, dest, ref, scr, cscr, cwide, codes, cf, sc, vx, pq, wp, wm,
    sendb, recvb, crecv, zsend, zrecv, zlast, zgot, nsend, nrecv, msend, mrecv, wts,
    img_m, right_m, dest_m, ref_m, code_s, code_r, row_s, row_r, z_s, z_r, n_s, n_r, m_s, m_r,
):
    mb = lax.axis_index("batch")
    ms = lax.axis_index("slab")
    core = lax.rem(ms, 2)
    zbase = ms - core
    mz = ms // 2
    me = mb * 2 + core
    my = mb // 4
    mx = lax.rem(mb, 4)

    def peer_of(turn):
        dy, dx = turn
        py = lax.rem(my + jnp.where(core == 0, dy, dx), 4)
        px = lax.rem(mx + jnp.where(core == 0, dx, 4 - dy), 4)
        return py * 4 + px

    barrier = pltpu.get_barrier_semaphore()
    loads = [pltpu.make_async_copy(img_in.at[p], img.at[p], img_m.at[p]) for p in range(PP)]
    load_right = pltpu.make_async_copy(right_in, right, right_m)
    load_dest = pltpu.make_async_copy(dest_in, dest, dest_m)
    load_ref = pltpu.make_async_copy(ref_in, ref, ref_m)
    for load in (*loads, load_dest, load_right, load_ref):
        load.start()

    def greet_plane(q, carry):
        i = lax.rem(me + q, 32)
        pl.semaphore_signal(
            barrier, inc=1, device_id=(i // 2, zbase + lax.rem(i, 2)), device_id_type=MESH
        )
        return carry

    def greet_slab(q, carry):
        pl.semaphore_signal(
            barrier, inc=1, device_id=(mb, lax.rem(ms + q, NS)), device_id_type=MESH
        )
        return carry

    lax.fori_loop(1, 32, greet_plane, 0)
    lax.fori_loop(1, NS, greet_slab, 0)

    def pick(index, values):
        got = jnp.full(index.shape, values[0])
        for i, value in enumerate(values[1:], 1):
            got = jnp.where(index == i, value, got)
        return got

    def square(k):
        half = jnp.where(k >= K // 2, k - K, k).astype(F32) * (1.0 / K)
        return half * half

    def phase(k, shift):
        turn = k.astype(F32) * shift
        turn = turn - K * jnp.floor((turn + 0.5) * (1.0 / K))
        return turn * (2.0 * math.pi / K)

    def to_plane(b, h, src, dst, send_sem, recv_sem):
        pltpu.make_async_remote_copy(
            src_ref=src, dst_ref=dst, send_sem=send_sem, recv_sem=recv_sem,
            device_id=(b, zbase + h), device_id_type=MESH,
        ).start()

    def compute(t, table, size, first=False):
        def one(p, carry):
            if first:
                pltpu.make_async_copy(img_in.at[p], img.at[p], img_m.at[p]).wait()
            sec = jnp.dot(table, img[p], preferred_element_type=F32)
            for g in range(3):
                cols = slice(g * 128, (g + 1) * 128)
                scr[g, pl.ds(p, size, stride=8), :] = sec[:size, cols]
                scr[3 + g, pl.ds(p, size, stride=8), :] = sec[size:, cols]
            return carry

        lax.fori_loop(0, PP, one, 0, unroll=2)

        def pack(i, carry):
            start = pl.multiple_of(i * 16, 16)
            target = lax.rem(i, NB) * 2 + i // NB
            for g in range(6):
                sendb[t, target, :, pl.ds(g * 128, 128)] = scr[g, pl.ds(start, 16), :].astype(BF)
            return carry

        lax.fori_loop(0, size // 2, pack, 0)

    other = 1 - core

    def send_rows(t):
        to_plane(mb, other, sendb.at[t, mb * 2 + other], recvb.at[t, me], row_s.at[t], row_r.at[t])
        pltpu.make_async_copy(sendb.at[t, me], recvb.at[t, me], row_r.at[t]).start()
        for flip in range(2):
            h = core if flip == 0 else other
            for turn in TURNS:
                b = peer_of(turn)
                to_plane(b, h, sendb.at[t, b * 2 + h], recvb.at[t, me], row_s.at[t], row_r.at[t])

    def send_last():
        t = SHARED

        @pl.when(core == 0)
        def _():
            pltpu.make_async_copy(sendb.at[t, me], recvb.at[t, me], row_r.at[t]).start()

        @pl.when(core == 1)
        def _():
            to_plane(mb, 0, sendb.at[t, mb * 2], recvb.at[t, me], row_s.at[t], row_r.at[t])

        for turn in TURNS:
            b = peer_of(turn)
            to_plane(b, 0, sendb.at[t, b * 2], recvb.at[t, me], row_s.at[t], row_r.at[t])

    compute(0, left[0], 64, first=True)
    pl.semaphore_wait(barrier, 31 + NS - 1)
    send_rows(0)

    load_dest.wait()
    sub_p = lax.broadcasted_iota(jnp.int32, (PP, K), 0)
    col = lax.broadcasted_iota(jnp.int32, (PP, K), 1)
    end = counts[:, 0:1]
    slab = jnp.zeros((PP, K), jnp.int32)
    for i in range(1, NS):
        slab = slab + jnp.where(col >= end, 1, 0)
        end = end + counts[:, i : i + 1]
    plane = pick(sub_p, [dest[pl.ds(classes[p], 1), :] for p in range(PP)])
    place = slab * 32 + plane
    row8 = lax.broadcasted_iota(jnp.int32, (PP, 128), 0)
    lane8 = lax.broadcasted_iota(jnp.int32, (PP, 128), 1)
    spread = jnp.where(lax.rem(lane8, PP) == row8, 1.0, 0.0)
    kind8 = pick(row8, [kinds_in[p] for p in range(PP)])

    def turned(x):
        return lax.dot_general(
            x.astype(F32), spread, (((0,), (0,)), ((), ())),
            precision=lax.Precision.HIGHEST, preferred_element_type=F32,
        )

    cscr[...] = turned(place)
    kind_row = turned(kind8)[0:1]
    shift_x = pick(row8, [shifts[0, p] for p in range(PP)])
    shift_y = pick(row8, [shifts[1, p] for p in range(PP)])
    person = pick(lane8, [shift_x, shift_y, kind8, jnp.zeros_like(kind8)])
    person = jnp.where(lane8 < 3, person, 0).astype(F32)
    slot_one = (lax.broadcasted_iota(jnp.int32, (1, 128), 1) // PP) & 1

    def arrange(b, carry):
        base = b * KYB
        for h in range(2):
            rows = [(base + i, base + j) for i, j in SLOTS[h]]
            rows += [(K - base - i, K - base - j) for i, j in SLOTS[h][:SHARED]]
            rows += [(base + i, base + j) for i, j in EXTRA[h]]
            for n, (i, j) in enumerate(rows):
                cwide[n : n + 1, :] = jnp.where(
                    slot_one == 0, cscr[pl.ds(i, 1), :], cscr[pl.ds(j, 1), :] + PL
                )
            cwide[10:11, :] = kind_row
            cwide[16:24, :] = person
            codes[b * 2 + h] = cwide[...].astype(BF)
        return carry

    cwide[...] = jnp.zeros_like(cwide)
    lax.fori_loop(0, NB, arrange, 0)

    def send_codes(q, carry):
        i = lax.rem(me + q, 32)
        to_plane(i // 2, lax.rem(i, 2), codes.at[i], crecv.at[me], code_s, code_r)
        return carry

    pltpu.make_async_copy(codes.at[me], crecv.at[me], code_r).start()
    lax.fori_loop(1, 32, send_codes, 0)

    for t in range(1, SHARED):
        compute(t, left[t], 64)
        send_rows(t)
    compute(SHARED, left_last[...], 32)
    send_last()

    pltpu.make_async_copy(crecv, crecv, code_r).wait()

    def widen(i, carry):
        cf[pl.ds(pl.multiple_of(i * 32, 32), 32), :] = crecv[i].astype(F32)
        return carry

    lax.fori_loop(0, 32, widen, 0)

    lane = lax.broadcasted_iota(jnp.int32, (32, 128), 1)
    sub = lax.broadcasted_iota(jnp.int32, (32, 128), 0)
    mine = (lane // 16) == lax.rem(sub, 8)

    def pair_codes(row):
        got = cf[pl.ds(row, 32, stride=32), :]
        return jnp.sum(jnp.where(mine, got, 0.0).reshape(4, 8, 128), axis=1)

    spot = lax.broadcasted_iota(jnp.int32, (256, 128), 0).astype(F32)

    def one_hot(code4):
        return jnp.concatenate(
            [
                jnp.where(spot == code4[g : g + 1, :], 1.0, 0.0).astype(BF)
                for g in range(4)
            ],
            axis=1,
        )

    row_id = lax.broadcasted_iota(jnp.int32, (128, 128), 0)
    row_class = jnp.where(row_id < 3 * NDEF, lax.rem(row_id, NDEF), -1).astype(F32)
    kind4 = pair_codes(10)
    kinds = jnp.concatenate(
        [jnp.where(row_class == kind4[g : g + 1, :], 1.0, 0.0).astype(BF) for g in range(4)],
        axis=1,
    )

    def count(n, carry):
        tally = lax.dot_general(
            one_hot(pair_codes(jnp.where(n < TILES, n, n + SHARED))), kinds,
            (((1,), (1,)), ((), ())), preferred_element_type=F32,
        )
        start = pl.multiple_of(n * 32, 32)
        nsend[:, pl.ds(start, 32), :] = tally.astype(BF).reshape(NS, 32, 128)
        return carry

    lax.fori_loop(0, NCNT, count, 0)

    def to_slab(q, src, dst, send_sem, recv_sem):
        peer = lax.rem(ms + q, NS)
        pltpu.make_async_remote_copy(
            src_ref=src(peer), dst_ref=dst, send_sem=send_sem, recv_sem=recv_sem,
            device_id=(mb, peer), device_id_type=MESH,
        ).start()

    pltpu.make_async_copy(nsend.at[ms], nrecv.at[ms], n_r).start()
    for q in range(1, NS):
        to_slab(q, lambda peer: nsend.at[peer], nrecv.at[ms], n_s, n_r)

    slot_of = lane8 & 7
    part = lane8 // 8
    flat = [[i for two in SLOTS[h] for i in two] for h in range(2)]
    slot_ky = mb * KYB + jnp.where(core == 0, pick(slot_of, flat[0]), pick(slot_of, flat[1]))
    slot_sq = square(slot_ky)
    col_sq = square(col)
    every = [defocus[i] for i in range(NDEF)]
    quarter = 0.5 * math.pi

    def prepare(i, carry):
        own = cf[pl.ds(pl.multiple_of(i * 32 + 16, 16), 8), :]
        sx, sy, kind = own[:, 0:1], own[:, 1:2], own[:, 2:3]
        focus = jnp.full((PP, 1), every[0])
        for n in range(1, NDEF):
            focus = jnp.where(kind == n, every[n], focus)
        arg = focus * slot_sq + PHASE_OFFSET
        turn = phase(slot_ky, sy)
        sc[i] = jnp.sin(
            jnp.where(
                part == 0,
                arg,
                jnp.where(part == 1, arg + quarter, jnp.where(part == 2, turn - quarter, turn)),
            )
        )
        arg_x = focus * col_sq
        turn_x = phase(col, sx)
        vx[0, i] = jnp.sin(arg_x)
        vx[1, i] = jnp.cos(arg_x)
        vx[2, i] = jnp.cos(turn_x)
        vx[3, i] = -jnp.sin(turn_x)
        return carry

    lax.fori_loop(0, 32, prepare, 0)

    load_right.wait()

    def process(t, mirrored):
        pltpu.make_async_copy(recvb.at[t], recvb.at[t], row_r.at[t]).wait()

        def half(m, carry):
            block = recvb[t, pl.ds(m * 16, 16)].reshape(256, 2 * K)
            start = pl.multiple_of(m * 256, 256)
            pq[0, pl.ds(start, 256), :] = jnp.dot(
                block[:, :K], right[pl.ds(0, K), :], preferred_element_type=F32
            )
            pq[1, pl.ds(start, 256), :] = jnp.dot(
                block[:, K:], right[pl.ds(K, K), :], preferred_element_type=F32
            )
            return carry

        lax.fori_loop(0, 2, half, 0)

        def weigh(i, carry):
            scal = sc[i]
            got = [[], [], [], []]
            for j in range(2):
                lane_j = t * 2 + j
                sa, ca, er, ei = [scal[:, lane_j + 8 * n : lane_j + 8 * n + 1] for n in range(4)]
                rows = pl.ds(pl.multiple_of(i * 16 + j * 8, 8), 8)
                pr, pi = pq[0, rows, pl.ds(0, K)], pq[0, rows, pl.ds(K, K)]
                qr, qi = pq[1, rows, pl.ds(0, K)], pq[1, rows, pl.ds(K, K)]
                ctf = sa * vx[1, i] + ca * vx[0, i]
                gr, gi = ctf * vx[2, i], ctf * vx[3, i]
                fa, fb, fc, fd = er * gr, ei * gi, er * gi, ei * gr
                sr, si = pr + qr, pi + qi
                fr, fi = fa - fb, fc + fd
                got[0].append(sr * fr - si * fi)
                got[1].append(sr * fi + si * fr)
                if mirrored:
                    sr, si = pr - qr, pi - qi
                    fr, fi = fa + fb, fc - fd
                    got[2].append(sr * fr - si * fi)
                    got[3].append(sr * fi + si * fr)
            rows = pl.ds(pl.multiple_of(i * 16, 16), 16)
            for n in range(4 if mirrored else 2):
                to = wp if n < 2 else wm
                to[rows, pl.ds((n % 2) * K, K)] = jnp.concatenate(got[n], axis=0).astype(BF)
            return carry

        lax.fori_loop(0, 32, weigh, 0)

        def total(hot, rows):
            return jnp.dot(hot, rows, preferred_element_type=F32).astype(BF).reshape(NS, 32, 2 * K)

        if mirrored:
            zsend[t, :, pl.ds(0, 32), :] = total(one_hot(pair_codes(t)), wp[...])
            zsend[t, :, pl.ds(32, 32), :] = total(one_hot(pair_codes(TILES + t)), wm[...])
            for q in range(1, NS):
                to_slab(q, lambda peer: zsend.at[t, peer], zrecv.at[t, ms], z_s.at[t], z_r.at[t])
            pltpu.make_async_copy(zsend.at[t, ms], zrecv.at[t, ms], z_r.at[t]).start()
        else:
            zlast[...] = total(one_hot(pair_codes(t)), wp[...])
            for q in range(1, NS):
                to_slab(q, lambda peer: zlast.at[peer], zgot.at[mz], z_s.at[t], z_r.at[t])
            pltpu.make_async_copy(zlast.at[ms], zgot.at[mz], z_r.at[t]).start()

    def weights():
        lane_k = lax.broadcasted_iota(jnp.int32, (KYB, 128), 1)
        own_ky = mb * KYB + lax.broadcasted_iota(jnp.int32, (KYB, 128), 0)
        arg2_y = 2.0 * (pick(lane_k & (NDEF - 1), every) * square(own_ky) + PHASE_OFFSET)
        group = lane_k // NDEF
        tw = jnp.where(
            group == 0,
            -0.5 * jnp.cos(arg2_y),
            jnp.where(group == 1, 0.5 * jnp.sin(arg2_y), jnp.where(group == 2, 0.5, 0.0)),
        )
        row_k = lax.broadcasted_iota(jnp.int32, (NDEF, K), 0)
        col_k = lax.broadcasted_iota(jnp.int32, (NDEF, K), 1)
        arg2_x = 2.0 * (pick(row_k, every) * square(col_k))
        rw = jnp.concatenate(
            [
                jnp.cos(arg2_x),
                jnp.sin(arg2_x),
                jnp.ones((NDEF, K), F32),
                jnp.zeros((128 - 3 * NDEF, K), F32),
            ],
            axis=0,
        )
        pltpu.make_async_copy(nrecv, nrecv, n_r).wait()
        for h in range(2):
            scaled, names = [], []
            for n, two in enumerate(COUNTED[h]):
                if h == 1 and n == SHARED:
                    continue
                for j, i in enumerate(two):
                    if j == 1 and two[0] == two[1]:
                        continue
                    rows = pl.ds(n * 32 + j * PL, PL)
                    x = nrecv[h, rows, :].astype(F32)
                    for z in range(1, NS // 2):
                        x += nrecv[2 * z + h, rows, :].astype(F32)
                    scaled.append(x * tw[i : i + 1, :])
                    names.append(i)
            res = jnp.dot(
                jnp.concatenate(scaled, axis=0), rw,
                precision=lax.Precision.HIGHEST, preferred_element_type=F32,
            )
            res = 1.0 / (res + TAU_PRIOR)
            for m, i in enumerate(names):
                wts[pl.ds(i * PL, PL), :] = res[m * PL : (m + 1) * PL]

    def finish(i, sums):
        rows = pl.ds(i * PL, PL)
        inverse = wts[rows, :]
        for h in range(2):
            cols = pl.ds(h * K, K)
            top = TAU_PRIOR * ref[rows, cols].astype(F32) + sums[:, h * K : (h + 1) * K]
            out[rows, cols] = (top * inverse).astype(BF)

    def mirror_rows(t):
        return [(h, j) for h in (1, 0) for j in range(2) if j == 0 or SLOTS[h][t][0] != SLOTS[h][t][1]]

    def gather(t):
        pltpu.make_async_copy(zrecv.at[t], zrecv.at[t], z_r.at[t]).wait()

        def over_z(h, start):
            rows = pl.ds(start, PL)
            x = zrecv[t, h, rows, :].astype(F32)
            for z in range(1, NS // 2):
                x += zrecv[t, 2 * z + h, rows, :].astype(F32)
            return x

        rows = mirror_rows(t)
        for m, (h, j) in enumerate(rows):
            msend[t, m] = over_z(h, 32 + j * PL).astype(BF)
        pltpu.make_async_remote_copy(
            src_ref=msend.at[t, pl.ds(0, len(rows))], dst_ref=mrecv.at[t, pl.ds(0, len(rows))],
            send_sem=m_s.at[t], recv_sem=m_r.at[t],
            device_id=(NB - 1 - mb, ms), device_id_type=MESH,
        ).start()
        for h, j in rows:
            finish(SLOTS[h][t][j], over_z(h, j * PL))

    process(0, True)
    load_ref.wait()
    weights()
    process(1, True)
    gather(0)
    process(2, True)
    gather(1)

    @pl.when(core == 0)
    def _():
        process(SHARED, False)

    gather(2)

    pltpu.make_async_copy(zgot, zgot, z_r.at[SHARED]).wait()
    for j in range(2):
        rows = pl.ds(j * PL, PL)
        x = zgot[0, rows, :].astype(F32)
        for z in range(1, NS // 2):
            x += zgot[z, rows, :].astype(F32)
        finish(SLOTS[0][SHARED][j], x)

    def drain(src, send_sem, recv_sem):
        return pltpu.make_async_remote_copy(
            src_ref=src, dst_ref=src, send_sem=send_sem, recv_sem=recv_sem,
            device_id=(mb, ms), device_id_type=MESH,
        )

    for t in range(SHARED):
        rows = mirror_rows(t)
        drain(msend.at[t, pl.ds(0, len(rows))], m_s.at[t], m_r.at[t]).wait()
        for m, (h, j) in enumerate(rows):
            finish(KYB - SLOTS[h][t][j], mrecv[t, m].astype(F32))

    drain(crecv.at[pl.ds(0, 31)], code_s, code_r).wait_send()
    drain(nsend.at[pl.ds(0, 7)], n_s, n_r).wait_send()
    for t in range(SHARED):
        drain(sendb.at[t, pl.ds(0, 31)], row_s.at[t], row_r.at[t]).wait_send()
        drain(zsend.at[t, pl.ds(0, 7)], z_s.at[t], z_r.at[t]).wait_send()

    @pl.when(core == 0)
    def _():
        drain(sendb.at[SHARED, pl.ds(0, 15)], row_s.at[SHARED], row_r.at[SHARED]).wait_send()
        drain(zlast.at[pl.ds(0, 7)], z_s.at[SHARED], z_r.at[SHARED]).wait_send()

    @pl.when(core == 1)
    def _():
        drain(sendb.at[SHARED, pl.ds(0, 16)], row_s.at[SHARED], row_r.at[SHARED]).wait_send()


def per_device(images, classes, shifts, defocus_class, defocus, run_counts, dest_map, ref):
    left, left_last, right = tables()
    vmem = pl.BlockSpec(memory_space=pltpu.VMEM)
    smem = pl.BlockSpec(memory_space=pltpu.SMEM)
    far = pl.BlockSpec(memory_space=pl.ANY)
    dma = pltpu.SemaphoreType.DMA
    out = pl.pallas_call(
        kernel,
        out_shape=jax.ShapeDtypeStruct((KYB * PL, 2 * K), BF),
        in_specs=[smem] * 4 + [vmem] * 3 + [far] * 4,
        out_specs=vmem,
        scratch_shapes=[
            pltpu.VMEM((PP, K, K), BF),
            pltpu.VMEM((2 * K, 2 * K), BF),
            pltpu.VMEM(dest_map.shape, jnp.int32),
            pltpu.VMEM((KYB * PL, 2 * K), BF),
            pltpu.VMEM((6, 64 * PP, 128), F32),
            pltpu.VMEM((K, 128), F32),
            pltpu.VMEM((32, 128), F32),
            pltpu.VMEM((32, 32, 128), BF),
            pltpu.VMEM((32 * 32, 128), F32),
            pltpu.VMEM((32, PP, 128), F32),
            pltpu.VMEM((4, 32, PP, K), F32),
            pltpu.VMEM((2, 512, 2 * K), F32),
            pltpu.VMEM((512, 2 * K), BF),
            pltpu.VMEM((512, 2 * K), BF),
            pltpu.VMEM((TILES, 32, 16, 2 * K), BF),
            pltpu.VMEM((TILES, 32, 16, 2 * K), BF),
            pltpu.VMEM((32, 32, 128), BF),
            pltpu.VMEM((SHARED, NS, 64, 2 * K), BF),
            pltpu.VMEM((SHARED, NS, 64, 2 * K), BF),
            pltpu.VMEM((NS, 32, 2 * K), BF),
            pltpu.VMEM((NS // 2, 32, 2 * K), BF),
            pltpu.VMEM((NS, NCNT * 32, 128), BF),
            pltpu.VMEM((NS, NCNT * 32, 128), BF),
            pltpu.VMEM((SHARED, 4, PL, 2 * K), BF),
            pltpu.VMEM((SHARED, 4, PL, 2 * K), BF),
            pltpu.VMEM((KYB * PL, K), F32),
            dma((PP,)), dma, dma, dma, dma, dma, dma((TILES,)), dma((TILES,)),
            dma((TILES,)), dma((TILES,)), dma, dma, dma((SHARED,)), dma((SHARED,)),
        ],
        compiler_params=pltpu.CompilerParams(
            collective_id=0, has_side_effects=True, vmem_limit_bytes=60 * 1024 * 1024
        ),
    )(
        classes, defocus_class, defocus, shifts.T, run_counts, jnp.asarray(left),
        jnp.asarray(left_last), images, jnp.asarray(right), dest_map,
        ref.reshape(KYB * PL, 2 * K),
    )
    return out.reshape(KYB, PL, 2 * K)


def solution(mesh):
    placed = (
        P(("batch", "slab"), None, None),
        P(("batch", "slab")),
        P(("batch", "slab"), None),
        P(("batch", "slab")),
        P(),
        P(("batch", "slab"), None),
        P(),
        P("batch", "slab", None),
    )
    return jax.shard_map(
        per_device, mesh=mesh, in_specs=placed, out_specs=P("batch", "slab", None), check_vma=False
    )
```

time: 79.2 us -> 73.8 us (0.932)
  Pallas kernels: 77.1 us -> 71.7 us
    pallas_call x1, Pallas kernels: 77.1 us -> 71.7 us  [per_device(): pl.pallas_call(kernel, out_shape=jax.ShapeDtypeStruct((KYB * PL, 2 * K),...]
where the time goes in v4:
time: 73.8 us; the launch traced here: 73.6 us
  Pallas kernels  71.7 us (97%)
  local copies, waits for them, and re-layouts  1.92 us (3%)
    pallas_call x1, Pallas kernels, per_device(): pl.pallas_call(kernel, out_shape=jax.ShapeDtypeStruct((KYB * PL, 2 * K),...  71.7 us
    unnamed x1, local copies, waits for them, and re-layouts  1.92 us

profile of v4, /device:TPU:1, one launch (start us, length us, event | category | flops | bytes accessed | tf_op | source)
XLA Modules:
  0.0 73.6 jit_solution(18235091200367491300)
XLA Ops:
  0.0 71.7 %shard_map.109 = bf16[384,768]{1,0:T(8,128)(2,1)} custom-call(s32[8]{0:T(128)} %classes.1, s32[8]{0:T(128)} %kinds_in.1, f32[16]{0:T(128)} %defocus.1, s32[2,8]{1,0:T(2,128)} %bitcast.5, s32[8,8]{1,0:T(8,128)} %counts.1, bf16[3,128,384]{2,1,0:T(8,128)(2,1)} %constant.6.clone.left, bf16[64,384]{1,0:T(8,128)(2,1)} %constant.7.clone.left_last, ...), custom_call_target="tpu_custom_call" | custom-call | tf_op jit(solution)/shard_map/pallas_call | solution.py:524
  71.7 1.9 %copy.13 = bf16[24,16,768]{2,1,0:T(8,128)(2,1)} copy(bf16[24,16,768]{2,1,0:T(8,128)(2,1)} %bitcast.3) | data formatting | bytes 1179648

commit v5 on v4

v5 whole, which is shorter than its diff:
```python
import math

import jax
import jax.numpy as jnp
import ml_dtypes
import numpy as np
from jax import lax
from jax.experimental import pallas as pl
from jax.experimental.pallas import tpu as pltpu
from jax.sharding import PartitionSpec as P

TAU_PRIOR = 4.0
PHASE_OFFSET = 0.1
MESH = pl.DeviceIdType.MESH

K = 384
NB = 16
NS = 8
PP = 8
KYB = K // NB
SHARED = 3
TILES = SHARED + 1
PL = 16
NDEF = 16
BF = jnp.bfloat16
F32 = jnp.float32
LAST = SHARED
EXTRA = 13
NCNT = TILES + 3
TURNS = (
    (0, 1), (1, 0), (0, 3), (3, 0), (1, 1), (1, 3), (3, 3), (3, 1),
    (1, 2), (2, 1), (3, 2), (2, 3), (0, 2), (2, 0), (2, 2),
)


def tables():
    index = np.arange(K)
    angle = 2.0 * np.pi / K * ((index[:, None] * index[None, :]) % K)
    cosine = (np.cos(angle) / math.sqrt(K)).astype(np.float32)
    sine = (np.sin(angle) / math.sqrt(K)).astype(np.float32)

    def left(t):
        rows = [
            KYB * b + (6 * h + 2 * t + 1 + j if t < LAST else 0)
            for h in range(2)
            for b in range(NB)
            for j in range(2)
        ]
        return np.concatenate([cosine[rows], -sine[rows]], axis=0)

    both = np.stack([left(t) for t in range(TILES)], axis=0)
    right = np.concatenate(
        [np.concatenate([cosine, -sine], 1), np.concatenate([sine, cosine], 1)], 0
    )
    kind = ml_dtypes.bfloat16
    return both.astype(kind), right.astype(kind)


def kernel(
    classes, kinds_in, defocus, shifts, counts, left, img_in, right_in, dest_in, ref_in,
    out,
    img, right, dest, ref, scr, cscr, cwide, codes, cf, sc, vx, pq, wp, wm,
    sendb, recvb, crecv, zsend, zrecv, zgot, nsend, nrecv, msend, mrecv, wts, tws,
    img_m, right_m, dest_m, ref_m, code_s, code_r, row_s, row_r, z_s, z_r, n_s, n_r, m_s, m_r,
):
    mb = lax.axis_index("batch")
    ms = lax.axis_index("slab")
    core = lax.rem(ms, 2)
    zbase = ms - core
    mz = ms // 2
    me = mb * 2 + core
    my = mb // 4
    mx = lax.rem(mb, 4)

    def peer_of(turn):
        dy, dx = turn
        py = lax.rem(my + jnp.where(core == 0, dy, dx), 4)
        px = lax.rem(mx + jnp.where(core == 0, dx, 4 - dy), 4)
        return py * 4 + px

    barrier = pltpu.get_barrier_semaphore()
    loads = [pltpu.make_async_copy(img_in.at[p], img.at[p], img_m.at[p]) for p in range(PP)]
    load_right = pltpu.make_async_copy(right_in, right, right_m)
    load_dest = pltpu.make_async_copy(dest_in, dest, dest_m)
    load_ref = pltpu.make_async_copy(ref_in, ref, ref_m)
    for load in (*loads, load_dest, load_right, load_ref):
        load.start()

    def greet_plane(q, carry):
        i = lax.rem(me + q, 32)
        pl.semaphore_signal(
            barrier, inc=1, device_id=(i // 2, zbase + lax.rem(i, 2)), device_id_type=MESH
        )
        return carry

    def greet_slab(q, carry):
        pl.semaphore_signal(
            barrier, inc=1, device_id=(mb, lax.rem(ms + q, NS)), device_id_type=MESH
        )
        return carry

    lax.fori_loop(1, 32, greet_plane, 0)
    lax.fori_loop(1, NS, greet_slab, 0)

    def pick(index, values):
        got = jnp.full(index.shape, values[0])
        for i, value in enumerate(values[1:], 1):
            got = jnp.where(index == i, value, got)
        return got

    def square(k):
        half = jnp.where(k >= K // 2, k - K, k).astype(F32) * (1.0 / K)
        return half * half

    def phase(k, shift):
        turn = k.astype(F32) * shift
        turn = turn - K * jnp.floor((turn + 0.5) * (1.0 / K))
        return turn * (2.0 * math.pi / K)

    def to_plane(b, h, src, dst, send_sem, recv_sem):
        pltpu.make_async_remote_copy(
            src_ref=src, dst_ref=dst, send_sem=send_sem, recv_sem=recv_sem,
            device_id=(b, zbase + h), device_id_type=MESH,
        ).start()

    def compute(t):
        table = left[t]

        def one(p, carry):
            @pl.when(t == 0)
            def _():
                pltpu.make_async_copy(img_in.at[p], img.at[p], img_m.at[p]).wait()

            sec = jnp.dot(table, img[p], preferred_element_type=F32)
            for g in range(3):
                cols = slice(g * 128, (g + 1) * 128)
                scr[g, pl.ds(p, 64, stride=8), :] = sec[:64, cols]
                scr[3 + g, pl.ds(p, 64, stride=8), :] = sec[64:, cols]
            return carry

        lax.fori_loop(0, PP, one, 0)

        def pack(i, carry):
            start = pl.multiple_of(i * 16, 16)
            target = lax.rem(i, NB) * 2 + i // NB
            for g in range(6):
                sendb[t, target, :, pl.ds(g * 128, 128)] = scr[g, pl.ds(start, 16), :].astype(BF)
            return carry

        lax.fori_loop(0, 32, pack, 0)

    other = 1 - core

    def send_rows(t):
        to_plane(mb, other, sendb.at[t, mb * 2 + other], recvb.at[t, me], row_s.at[t], row_r.at[t])
        pltpu.make_async_copy(sendb.at[t, me], recvb.at[t, me], row_r.at[t]).start()
        for flip in range(2):
            h = core if flip == 0 else other
            for turn in TURNS:
                b = peer_of(turn)
                to_plane(b, h, sendb.at[t, b * 2 + h], recvb.at[t, me], row_s.at[t], row_r.at[t])

    def send_last():
        t = LAST

        @pl.when(core == 0)
        def _():
            pltpu.make_async_copy(sendb.at[t, me], recvb.at[t, me], row_r.at[t]).start()

        @pl.when(core == 1)
        def _():
            to_plane(mb, 0, sendb.at[t, mb * 2], recvb.at[t, me], row_s.at[t], row_r.at[t])

        for turn in TURNS:
            b = peer_of(turn)
            to_plane(b, 0, sendb.at[t, b * 2], recvb.at[t, me], row_s.at[t], row_r.at[t])

    sub_p = lax.broadcasted_iota(jnp.int32, (PP, K), 0)
    col = lax.broadcasted_iota(jnp.int32, (PP, K), 1)
    row8 = lax.broadcasted_iota(jnp.int32, (PP, 128), 0)
    lane8 = lax.broadcasted_iota(jnp.int32, (PP, 128), 1)

    def tell():
        load_dest.wait()
        end = counts[:, 0:1]
        slab = jnp.zeros((PP, K), jnp.int32)
        for i in range(1, NS):
            slab = slab + jnp.where(col >= end, 1, 0)
            end = end + counts[:, i : i + 1]
        plane = pick(sub_p, [dest[pl.ds(classes[p], 1), :] for p in range(PP)])
        place = slab * 32 + plane
        spread = jnp.where(lax.rem(lane8, PP) == row8, 1.0, 0.0)
        kind8 = pick(row8, [kinds_in[p] for p in range(PP)])

        def turned(x):
            return lax.dot_general(
                x.astype(F32), spread, (((0,), (0,)), ((), ())),
                precision=lax.Precision.HIGHEST, preferred_element_type=F32,
            )

        cscr[...] = turned(place)
        kind_row = turned(kind8)[0:1]
        shift_x = pick(row8, [shifts[0, p] for p in range(PP)])
        shift_y = pick(row8, [shifts[1, p] for p in range(PP)])
        person = pick(lane8, [shift_x, shift_y, kind8, jnp.zeros_like(kind8)])
        person = jnp.where(lane8 < 3, person, 0).astype(F32)
        slot_one = (lax.broadcasted_iota(jnp.int32, (1, 128), 1) // PP) & 1

        def arrange(d, carry):
            base = d // 2 * KYB
            step = 6 * lax.rem(d, 2)
            for n in range(TILES + SHARED + 3):
                for_two = []
                for j in range(2):
                    if n < SHARED:
                        ky = base + step + 2 * n + 1 + j
                    elif n == LAST:
                        ky = base
                    elif n < TILES + SHARED:
                        ky = K - (base + step + 2 * (n - TILES) + 1 + j)
                    else:
                        ky = jnp.minimum(base + EXTRA + step + 2 * (n - TILES - SHARED) + j, K - 1)
                    for_two.append(cscr[pl.ds(ky, 1), :])
                cwide[n : n + 1, :] = jnp.where(slot_one == 0, for_two[0], for_two[1] + PL)
            codes[d] = cwide[...].astype(BF)
            return carry

        cwide[...] = jnp.zeros_like(cwide)
        cwide[10:11, :] = kind_row
        cwide[16:24, :] = person
        lax.fori_loop(0, 2 * NB, arrange, 0)

        def send_codes(q, carry):
            i = lax.rem(me + q, 32)
            to_plane(i // 2, lax.rem(i, 2), codes.at[i], crecv.at[me], code_s, code_r)
            return carry

        pltpu.make_async_copy(codes.at[me], crecv.at[me], code_r).start()
        lax.fori_loop(1, 32, send_codes, 0)


    def produce(t, carry):
        compute(t)

        @pl.when(t == 0)
        def _():
            pl.semaphore_wait(barrier, 31 + NS - 1)

        @pl.when(t < LAST)
        def _():
            send_rows(t)

        pl.when(t == LAST)(send_last)
        pl.when(t == 0)(tell)
        return carry

    lax.fori_loop(0, TILES, produce, 0)

    pltpu.make_async_copy(crecv, crecv, code_r).wait()

    def widen(i, carry):
        cf[pl.ds(pl.multiple_of(i * 32, 32), 32), :] = crecv[i].astype(F32)
        return carry

    lax.fori_loop(0, 32, widen, 0)

    lane = lax.broadcasted_iota(jnp.int32, (32, 128), 1)
    sub = lax.broadcasted_iota(jnp.int32, (32, 128), 0)
    mine = (lane // 16) == lax.rem(sub, 8)

    def pair_codes(row):
        got = cf[pl.ds(row, 32, stride=32), :]
        return jnp.sum(jnp.where(mine, got, 0.0).reshape(4, 8, 128), axis=1)

    spot = lax.broadcasted_iota(jnp.int32, (256, 128), 0).astype(F32)

    def one_hot(code4):
        return jnp.concatenate(
            [
                jnp.where(spot == code4[g : g + 1, :], 1.0, 0.0).astype(BF)
                for g in range(4)
            ],
            axis=1,
        )

    row_id = lax.broadcasted_iota(jnp.int32, (128, 128), 0)
    row_class = jnp.where(row_id < 3 * NDEF, lax.rem(row_id, NDEF), -1).astype(F32)
    kind4 = pair_codes(10)
    kinds = jnp.concatenate(
        [jnp.where(row_class == kind4[g : g + 1, :], 1.0, 0.0).astype(BF) for g in range(4)],
        axis=1,
    )

    def count(n, carry):
        tally = lax.dot_general(
            one_hot(pair_codes(jnp.where(n < TILES, n, n + SHARED))), kinds,
            (((1,), (1,)), ((), ())), preferred_element_type=F32,
        )
        start = pl.multiple_of(n * 32, 32)
        nsend[:, pl.ds(start, 32), :] = tally.astype(BF).reshape(NS, 32, 128)
        return carry

    lax.fori_loop(0, NCNT, count, 0)

    def to_slab(q, src, dst, send_sem, recv_sem):
        peer = lax.rem(ms + q, NS)
        pltpu.make_async_remote_copy(
            src_ref=src(peer), dst_ref=dst, send_sem=send_sem, recv_sem=recv_sem,
            device_id=(mb, peer), device_id_type=MESH,
        ).start()

    pltpu.make_async_copy(nsend.at[ms], nrecv.at[ms], n_r).start()
    def send_counts(q, carry):
        to_slab(q, lambda peer: nsend.at[peer], nrecv.at[ms], n_s, n_r)
        return carry

    lax.fori_loop(1, NS, send_counts, 0)

    slot_of = (lane8 // 8) * 2 + (lane8 & 1)
    part = (lane8 // 2) & 3
    slot_ky = mb * KYB + jnp.where(slot_of < 2 * SHARED, 6 * core + 1 + slot_of, 0)
    slot_sq = square(slot_ky)
    col_sq = square(col)
    every = [defocus[i] for i in range(NDEF)]
    quarter = 0.5 * math.pi

    def prepare(i, carry):
        own = cf[pl.ds(pl.multiple_of(i * 32 + 16, 16), 8), :]
        sx, sy, kind = own[:, 0:1], own[:, 1:2], own[:, 2:3]
        focus = jnp.full((PP, 1), every[0])
        for n in range(1, NDEF):
            focus = jnp.where(kind == n, every[n], focus)
        arg = focus * slot_sq + PHASE_OFFSET
        turn = phase(slot_ky, sy)
        scal = jnp.sin(
            jnp.where(
                part == 0,
                arg,
                jnp.where(part == 1, arg + quarter, jnp.where(part == 2, turn - quarter, turn)),
            )
        )
        sc[0, i] = scal
        for t in range(1, TILES):
            sc[t, i] = pltpu.roll(scal, 128 - 8 * t, 1)
        arg_x = focus * col_sq
        turn_x = phase(col, sx)
        vx[0, i] = jnp.sin(arg_x)
        vx[1, i] = jnp.cos(arg_x)
        vx[2, i] = jnp.cos(turn_x)
        vx[3, i] = -jnp.sin(turn_x)
        return carry

    lax.fori_loop(0, 32, prepare, 0)

    load_right.wait()

    def process(t):
        pltpu.make_async_copy(recvb.at[t], recvb.at[t], row_r.at[t]).wait()

        def half(m, carry):
            block = recvb[t, pl.ds(m * 16, 16)].reshape(256, 2 * K)
            start = pl.multiple_of(m * 256, 256)
            pq[0, pl.ds(start, 256), :] = jnp.dot(
                block[:, :K], right[pl.ds(0, K), :], preferred_element_type=F32
            )
            pq[1, pl.ds(start, 256), :] = jnp.dot(
                block[:, K:], right[pl.ds(K, K), :], preferred_element_type=F32
            )
            return carry

        lax.fori_loop(0, 2, half, 0)

        def weigh(i, carry):
            scal = sc[t, i]
            got = [[], [], [], []]
            for j in range(2):
                sa, ca, er, ei = [scal[:, 2 * n + j : 2 * n + j + 1] for n in range(4)]
                rows = pl.ds(pl.multiple_of(i * 16 + j * 8, 8), 8)
                pr, pi = pq[0, rows, pl.ds(0, K)], pq[0, rows, pl.ds(K, K)]
                qr, qi = pq[1, rows, pl.ds(0, K)], pq[1, rows, pl.ds(K, K)]
                ctf = sa * vx[1, i] + ca * vx[0, i]
                gr, gi = ctf * vx[2, i], ctf * vx[3, i]
                fa, fb, fc, fd = er * gr, ei * gi, er * gi, ei * gr
                sr, si = pr + qr, pi + qi
                fr, fi = fa - fb, fc + fd
                got[0].append(sr * fr - si * fi)
                got[1].append(sr * fi + si * fr)
                sr, si = pr - qr, pi - qi
                fr, fi = fa + fb, fc - fd
                got[2].append(sr * fr - si * fi)
                got[3].append(sr * fi + si * fr)
            rows = pl.ds(pl.multiple_of(i * 16, 16), 16)
            for n in range(4):
                to = wp if n < 2 else wm
                to[rows, pl.ds((n % 2) * K, K)] = jnp.concatenate(got[n], axis=0).astype(BF)
            return carry

        lax.fori_loop(0, 32, weigh, 0)

        def total(hot, rows):
            return jnp.dot(hot, rows, preferred_element_type=F32).astype(BF).reshape(NS, 32, 2 * K)

        zsend[t, :, pl.ds(0, 32), :] = total(one_hot(pair_codes(t)), wp[...])

        @pl.when(t < LAST)
        def _():
            zsend[t, :, pl.ds(32, 32), :] = total(one_hot(pair_codes(TILES + t)), wm[...])

            def send(q, carry):
                to_slab(q, lambda peer: zsend.at[t, peer], zrecv.at[t, ms], z_s.at[t], z_r.at[t])
                return carry

            lax.fori_loop(1, NS, send, 0)
            pltpu.make_async_copy(zsend.at[t, ms], zrecv.at[t, ms], z_r.at[t]).start()

        @pl.when(t == LAST)
        def _():
            top = pl.ds(0, PL)

            def send(q, carry):
                to_slab(q, lambda peer: zsend.at[t, peer, top], zgot.at[mz], z_s.at[t], z_r.at[t])
                return carry

            lax.fori_loop(1, NS, send, 0)
            pltpu.make_async_copy(zsend.at[t, ms, top], zgot.at[mz], z_r.at[t]).start()

    def weights():
        lane_k = lax.broadcasted_iota(jnp.int32, (32, 128), 1)
        own_ky = mb * KYB + lax.broadcasted_iota(jnp.int32, (32, 128), 0)
        arg2_y = 2.0 * (pick(lane_k & (NDEF - 1), every) * square(own_ky) + PHASE_OFFSET)
        group = lane_k // NDEF
        tws[...] = jnp.where(
            group == 0,
            -0.5 * jnp.cos(arg2_y),
            jnp.where(group == 1, 0.5 * jnp.sin(arg2_y), jnp.where(group == 2, 0.5, 0.0)),
        )
        row_k = lax.broadcasted_iota(jnp.int32, (NDEF, K), 0)
        col_k = lax.broadcasted_iota(jnp.int32, (NDEF, K), 1)
        arg2_x = 2.0 * (pick(row_k, every) * square(col_k))
        rw = jnp.concatenate(
            [
                jnp.cos(arg2_x),
                jnp.sin(arg2_x),
                jnp.ones((NDEF, K), F32),
                jnp.zeros((128 - 3 * NDEF, K), F32),
            ],
            axis=0,
        )
        pltpu.make_async_copy(nrecv, nrecv, n_r).wait()

        def one(h, carry):
            x = nrecv[h].astype(F32)
            for z in range(1, NS // 2):
                x += nrecv[2 * z + h].astype(F32)
            own, more = 6 * h + 1, 6 * h + EXTRA

            def times(part, i, rows):
                return (part.reshape(rows, PL, 128) * tws[pl.ds(i, rows), :][:, None, :]).reshape(
                    rows * PL, 128
                )

            scaled = jnp.concatenate(
                [times(x[:96], own, 6), times(x[96:128], 0, 2), times(x[128:], more, 6)], axis=0
            )
            res = jnp.dot(
                scaled, rw, precision=lax.Precision.HIGHEST, preferred_element_type=F32
            )
            res = 1.0 / (res + TAU_PRIOR)
            wts[pl.ds(pl.multiple_of(own * PL, PL), 96), :] = res[:96]
            wts[pl.ds(pl.multiple_of(more * PL, PL), 96), :] = res[128:]

            @pl.when(h == 0)
            def _():
                wts[pl.ds(0, PL), :] = res[96:112]

            return carry

        lax.fori_loop(0, 2, one, 0)

    def finish(i, sums):
        rows = pl.ds(pl.multiple_of(i * PL, PL), PL)
        inverse = wts[rows, :]
        for h in range(2):
            cols = pl.ds(h * K, K)
            top = TAU_PRIOR * ref[rows, cols].astype(F32) + sums[:, h * K : (h + 1) * K]
            out[rows, cols] = (top * inverse).astype(BF)

    def gather(t):
        pltpu.make_async_copy(zrecv.at[t], zrecv.at[t], z_r.at[t]).wait()

        def over_z(h, start):
            rows = pl.ds(pl.multiple_of(start, PL), PL)
            x = zrecv[t, h, rows, :].astype(F32)
            for z in range(1, NS // 2):
                x += zrecv[t, 2 * z + h, rows, :].astype(F32)
            return x

        def mirror(m, carry):
            msend[t, m] = over_z(m // 2, 2 * PL + lax.rem(m, 2) * PL).astype(BF)
            return carry

        lax.fori_loop(0, 4, mirror, 0)
        pltpu.make_async_remote_copy(
            src_ref=msend.at[t], dst_ref=mrecv.at[t], send_sem=m_s.at[t], recv_sem=m_r.at[t],
            device_id=(NB - 1 - mb, ms), device_id_type=MESH,
        ).start()

        def own(m, carry):
            h, j = m // 2, lax.rem(m, 2)
            finish(6 * h + 2 * t + 1 + j, over_z(h, j * PL))
            return carry

        lax.fori_loop(0, 4, own, 0)

    def consume(t, carry):
        @pl.when(jnp.logical_or(t < LAST, core == 0))
        def _():
            process(t)

        pl.when(t == 0)(weights)

        @pl.when(t > 0)
        def _():
            gather(t - 1)

        return carry

    load_ref.wait()
    lax.fori_loop(0, TILES, consume, 0)

    pltpu.make_async_copy(zgot, zgot, z_r.at[LAST]).wait()
    x = zgot[0].astype(F32)
    for z in range(1, NS // 2):
        x += zgot[z].astype(F32)
    finish(0, x)

    def drain(src, send_sem, recv_sem):
        return pltpu.make_async_remote_copy(
            src_ref=src, dst_ref=src, send_sem=send_sem, recv_sem=recv_sem,
            device_id=(mb, ms), device_id_type=MESH,
        )

    def mirrored(t, carry):
        drain(msend.at[t], m_s.at[t], m_r.at[t]).wait()

        def one(m, inner):
            i = 6 * (m // 2) + 2 * t + 1 + lax.rem(m, 2)

            @pl.when(i < KYB // 2)
            def _():
                finish(KYB - i, mrecv[t, m].astype(F32))

            return inner

        lax.fori_loop(0, 4, one, 0)
        return carry

    lax.fori_loop(0, SHARED, mirrored, 0)

    drain(crecv.at[pl.ds(0, 31)], code_s, code_r).wait_send()
    drain(nsend.at[pl.ds(0, 7)], n_s, n_r).wait_send()
    def drain_tile(t, carry):
        drain(sendb.at[t, pl.ds(0, 31)], row_s.at[t], row_r.at[t]).wait_send()
        drain(zsend.at[t, pl.ds(0, 7)], z_s.at[t], z_r.at[t]).wait_send()
        return carry

    lax.fori_loop(0, SHARED, drain_tile, 0)

    @pl.when(core == 0)
    def _():
        drain(sendb.at[LAST, pl.ds(0, 15)], row_s.at[LAST], row_r.at[LAST]).wait_send()
        drain(zsend.at[LAST, pl.ds(0, 7), pl.ds(0, PL)], z_s.at[LAST], z_r.at[LAST]).wait_send()

    @pl.when(core == 1)
    def _():
        drain(sendb.at[LAST, pl.ds(0, 16)], row_s.at[LAST], row_r.at[LAST]).wait_send()


def per_device(images, classes, shifts, defocus_class, defocus, run_counts, dest_map, ref):
    left, right = tables()
    vmem = pl.BlockSpec(memory_space=pltpu.VMEM)
    smem = pl.BlockSpec(memory_space=pltpu.SMEM)
    far = pl.BlockSpec(memory_space=pl.ANY)
    dma = pltpu.SemaphoreType.DMA
    out = pl.pallas_call(
        kernel,
        out_shape=jax.ShapeDtypeStruct((KYB * PL, 2 * K), BF),
        in_specs=[smem] * 4 + [vmem] * 2 + [far] * 4,
        out_specs=vmem,
        scratch_shapes=[
            pltpu.VMEM((PP, K, K), BF),
            pltpu.VMEM((2 * K, 2 * K), BF),
            pltpu.VMEM(dest_map.shape, jnp.int32),
            pltpu.VMEM((KYB * PL, 2 * K), BF),
            pltpu.VMEM((6, 64 * PP, 128), F32),
            pltpu.VMEM((K, 128), F32),
            pltpu.VMEM((32, 128), F32),
            pltpu.VMEM((32, 32, 128), BF),
            pltpu.VMEM((32 * 32, 128), F32),
            pltpu.VMEM((TILES, 32, PP, 128), F32),
            pltpu.VMEM((4, 32, PP, K), F32),
            pltpu.VMEM((2, 512, 2 * K), F32),
            pltpu.VMEM((512, 2 * K), BF),
            pltpu.VMEM((512, 2 * K), BF),
            pltpu.VMEM((TILES, 32, 16, 2 * K), BF),
            pltpu.VMEM((TILES, 32, 16, 2 * K), BF),
            pltpu.VMEM((32, 32, 128), BF),
            pltpu.VMEM((TILES, NS, 64, 2 * K), BF),
            pltpu.VMEM((SHARED, NS, 64, 2 * K), BF),
            pltpu.VMEM((NS // 2, PL, 2 * K), BF),
            pltpu.VMEM((NS, NCNT * 32, 128), BF),
            pltpu.VMEM((NS, NCNT * 32, 128), BF),
            pltpu.VMEM((SHARED, 4, PL, 2 * K), BF),
            pltpu.VMEM((SHARED, 4, PL, 2 * K), BF),
            pltpu.VMEM(((KYB + 1) * PL, K), F32),
            pltpu.VMEM((32, 128), F32),
            dma((PP,)), dma, dma, dma, dma, dma, dma((TILES,)), dma((TILES,)),
            dma((TILES,)), dma((TILES,)), dma, dma, dma((SHARED,)), dma((SHARED,)),
        ],
        compiler_params=pltpu.CompilerParams(
            collective_id=0, has_side_effects=True, vmem_limit_bytes=60 * 1024 * 1024
        ),
    )(
        classes, defocus_class, defocus, shifts.T, run_counts, jnp.asarray(left),
        images, jnp.asarray(right), dest_map,
        ref.reshape(KYB * PL, 2 * K),
    )
    return out.reshape(KYB, PL, 2 * K)


def solution(mesh):
    placed = (
        P(("batch", "slab"), None, None),
        P(("batch", "slab")),
        P(("batch", "slab"), None),
        P(("batch", "slab")),
        P(),
        P(("batch", "slab"), None),
        P(),
        P("batch", "slab", None),
    )
    return jax.shard_map(
        per_device, mesh=mesh, in_specs=placed, out_specs=P("batch", "slab", None), check_vma=False
    )
```

time: 73.8 us -> 76.8 us (1.041)
  Pallas kernels: 71.7 us -> 74.7 us
    pallas_call x1, Pallas kernels: 71.7 us -> 74.7 us  [per_device(): pl.pallas_call(kernel, out_shape=jax.ShapeDtypeStruct((KYB * PL, 2 * K),...]
where the time goes in v5:
time: 76.8 us; the launch traced here: 76.7 us
  Pallas kernels  74.7 us (97%)
  local copies, waits for them, and re-layouts  1.92 us (2%)
    pallas_call x1, Pallas kernels, per_device(): pl.pallas_call(kernel, out_shape=jax.ShapeDtypeStruct((KYB * PL, 2 * K),...  74.7 us
    unnamed x1, local copies, waits for them, and re-layouts  1.92 us

profile of v5, /device:TPU:1, one launch (start us, length us, event | category | flops | bytes accessed | tf_op | source)
XLA Modules:
  0.0 76.7 jit_solution(14175644288166187315)
XLA Ops:
  0.0 74.7 %shard_map.100 = bf16[384,768]{1,0:T(8,128)(2,1)} custom-call(s32[8]{0:T(128)} %classes.1, s32[8]{0:T(128)} %kinds_in.1, f32[16]{0:T(128)} %defocus.1, s32[2,8]{1,0:T(2,128)} %bitcast.5, s32[8,8]{1,0:T(8,128)} %counts.1, bf16[4,128,384]{2,1,0:T(8,128)(2,1)} %constant.4.clone.left, bf16[8,384,384]{2,1,0:T(8,128)(2,1)} %img_in.1, ...), custom_call_target="tpu_custom_call" | custom-call | tf_op jit(solution)/shard_map/pallas_call | solution.py:585
  74.8 1.9 %copy.12 = bf16[24,16,768]{2,1,0:T(8,128)(2,1)} copy(bf16[24,16,768]{2,1,0:T(8,128)(2,1)} %bitcast.3) | data formatting | bytes 1179648

commit v6 on v5

--- a/solution.py
+++ b/solution.py
@@ -27,6 +27,8 @@
 LAST = SHARED
 EXTRA = 13
 NCNT = TILES + 3
+MOVES = 40
+GROUP = 64
 TURNS = (
     (0, 1), (1, 0), (0, 3), (3, 0), (1, 1), (1, 3), (3, 3), (3, 1),
     (1, 2), (2, 1), (3, 2), (2, 3), (0, 2), (2, 0), (2, 2),
@@ -59,7 +61,7 @@
 def kernel(
     classes, kinds_in, defocus, shifts, counts, left, img_in, right_in, dest_in, ref_in,
     out,
-    img, right, dest, ref, scr, cscr, cwide, codes, cf, sc, vx, pq, wp, wm,
+    img, right, dest, ref, scr, cscr, cwide, codes, cf, sc, vx, table_x, table_s, pq, wp, wm,
     sendb, recvb, crecv, zsend, zrecv, zgot, nsend, nrecv, msend, mrecv, wts, tws,
     img_m, right_m, dest_m, ref_m, code_s, code_r, row_s, row_r, z_s, z_r, n_s, n_r, m_s, m_r,
 ):
@@ -199,11 +201,9 @@
             )
 
         cscr[...] = turned(place)
-        kind_row = turned(kind8)[0:1]
         shift_x = pick(row8, [shifts[0, p] for p in range(PP)])
         shift_y = pick(row8, [shifts[1, p] for p in range(PP)])
-        person = pick(lane8, [shift_x, shift_y, kind8, jnp.zeros_like(kind8)])
-        person = jnp.where(lane8 < 3, person, 0).astype(F32)
+        person = turned(pick(lane8, [kind8, shift_x, shift_y]))
         slot_one = (lax.broadcasted_iota(jnp.int32, (1, 128), 1) // PP) & 1
 
         def arrange(d, carry):
@@ -226,8 +226,7 @@
             return carry
 
         cwide[...] = jnp.zeros_like(cwide)
-        cwide[10:11, :] = kind_row
-        cwide[16:24, :] = person
+        cwide[10:13, :] = person[0:3]
         lax.fori_loop(0, 2 * NB, arrange, 0)
 
         def send_codes(q, carry):
@@ -259,7 +258,7 @@
     pltpu.make_async_copy(crecv, crecv, code_r).wait()
 
     def widen(i, carry):
-        cf[pl.ds(pl.multiple_of(i * 32, 32), 32), :] = crecv[i].astype(F32)
+        cf[pl.ds(pl.multiple_of(i * 16, 16), 16), :] = crecv[i].astype(F32)
         return carry
 
     lax.fori_loop(0, 32, widen, 0)
@@ -269,7 +268,7 @@
     mine = (lane // 16) == lax.rem(sub, 8)
 
     def pair_codes(row):
-        got = cf[pl.ds(row, 32, stride=32), :]
+        got = cf[pl.ds(row, 32, stride=16), :]
         return jnp.sum(jnp.where(mine, got, 0.0).reshape(4, 8, 128), axis=1)
 
     spot = lax.broadcasted_iota(jnp.int32, (256, 128), 0).astype(F32)
@@ -320,37 +319,67 @@
     part = (lane8 // 2) & 3
     slot_ky = mb * KYB + jnp.where(slot_of < 2 * SHARED, 6 * core + 1 + slot_of, 0)
     slot_sq = square(slot_ky)
-    col_sq = square(col)
     every = [defocus[i] for i in range(NDEF)]
-    quarter = 0.5 * math.pi
-
-    def prepare(i, carry):
-        own = cf[pl.ds(pl.multiple_of(i * 32 + 16, 16), 8), :]
-        sx, sy, kind = own[:, 0:1], own[:, 1:2], own[:, 2:3]
-        focus = jnp.full((PP, 1), every[0])
-        for n in range(1, NDEF):
-            focus = jnp.where(kind == n, every[n], focus)
-        arg = focus * slot_sq + PHASE_OFFSET
-        turn = phase(slot_ky, sy)
-        scal = jnp.sin(
-            jnp.where(
-                part == 0,
-                arg,
-                jnp.where(part == 1, arg + quarter, jnp.where(part == 2, turn - quarter, turn)),
+
+    def three(x):
+        high = x.astype(BF)
+        mid = (x - high.astype(F32)).astype(BF)
+        low = (x - high.astype(F32) - mid.astype(F32)).astype(BF)
+        return jnp.concatenate([high, mid, low], axis=0)
+
+    def rows_of(shape, axis=0):
+        return lax.broadcasted_iota(jnp.int32, shape, axis)
+
+    def tabulate():
+        turn = phase(rows_of((MOVES, K), 1), (rows_of((MOVES, K)) - 16).astype(F32))
+        arg = pick(rows_of((NDEF, K)), every) * square(rows_of((NDEF, K), 1))
+        spare = GROUP - MOVES - NDEF
+        for n, (move, kind) in enumerate(
+            (
+                (jnp.cos(turn), None),
+                (-jnp.sin(turn), None),
+                (None, jnp.sin(arg)),
+                (None, jnp.cos(arg)),
             )
-        )
-        sc[0, i] = scal
-        for t in range(1, TILES):
-            sc[t, i] = pltpu.roll(scal, 128 - 8 * t, 1)
-        arg_x = focus * col_sq
-        turn_x = phase(col, sx)
-        vx[0, i] = jnp.sin(arg_x)
-        vx[1, i] = jnp.cos(arg_x)
-        vx[2, i] = jnp.cos(turn_x)
-        vx[3, i] = -jnp.sin(turn_x)
-        return carry
-
-    lax.fori_loop(0, 32, prepare, 0)
+        ):
+            move = jnp.zeros((MOVES, K), F32) if move is None else move
+            kind = jnp.zeros((NDEF, K), F32) if kind is None else kind
+            full = jnp.concatenate([move, kind, jnp.zeros((spare, K), F32)], axis=0)
+            table_x[:, pl.ds(n * K, K)] = three(full)
+        turn = phase(slot_ky[0:1], (rows_of((MOVES, 128)) - 16).astype(F32))
+        arg = pick(rows_of((NDEF, 128)), every) * slot_sq[0:1] + PHASE_OFFSET
+        kind = part[0:1]
+        move = jnp.where(kind == 2, -jnp.cos(turn), jnp.where(kind == 3, jnp.sin(turn), 0.0))
+        tone = jnp.where(kind == 0, jnp.sin(arg), jnp.where(kind == 1, jnp.cos(arg), 0.0))
+        table_s[...] = three(
+            jnp.concatenate([move, tone, jnp.zeros((spare, 128), F32)], axis=0)
+        )
+
+    entry = (rows_of((3 * GROUP, 128)) & (GROUP - 1)).astype(F32)
+
+    def chosen(move4, table):
+        hot = jnp.concatenate(
+            [
+                jnp.where(
+                    (entry == move4[g : g + 1, :] + 16.0)
+                    | (entry == kind4[g : g + 1, :] + float(MOVES)),
+                    1.0,
+                    0.0,
+                ).astype(BF)
+                for g in range(4)
+            ],
+            axis=1,
+        )
+        return lax.dot_general(
+            hot, table, (((0,), (0,)), ((), ())), preferred_element_type=F32
+        )
+
+    tabulate()
+    vx[...] = chosen(pair_codes(11), table_x[...])
+    scal = chosen(pair_codes(12), table_s[...])
+    sc[0] = scal
+    for t in range(1, TILES):
+        sc[t] = pltpu.roll(scal, 128 - 8 * t, 1)
 
     load_right.wait()
 
@@ -371,15 +400,16 @@
         lax.fori_loop(0, 2, half, 0)
 
         def weigh(i, carry):
-            scal = sc[t, i]
             got = [[], [], [], []]
             for j in range(2):
+                rows = pl.ds(pl.multiple_of(i * 16 + j * 8, 8), 8)
+                scal = sc[t, rows, :]
                 sa, ca, er, ei = [scal[:, 2 * n + j : 2 * n + j + 1] for n in range(4)]
-                rows = pl.ds(pl.multiple_of(i * 16 + j * 8, 8), 8)
+                exr, exi, sb, cb = [vx[rows, pl.ds(n * K, K)] for n in range(4)]
                 pr, pi = pq[0, rows, pl.ds(0, K)], pq[0, rows, pl.ds(K, K)]
                 qr, qi = pq[1, rows, pl.ds(0, K)], pq[1, rows, pl.ds(K, K)]
-                ctf = sa * vx[1, i] + ca * vx[0, i]
-                gr, gi = ctf * vx[2, i], ctf * vx[3, i]
+                ctf = sa * cb + ca * sb
+                gr, gi = ctf * exr, ctf * exi
                 fa, fb, fc, fd = er * gr, ei * gi, er * gi, ei * gr
                 sr, si = pr + qr, pi + qi
                 fr, fi = fa - fb, fc + fd
@@ -395,7 +425,7 @@
                 to[rows, pl.ds((n % 2) * K, K)] = jnp.concatenate(got[n], axis=0).astype(BF)
             return carry
 
-        lax.fori_loop(0, 32, weigh, 0)
+        lax.fori_loop(0, 32, weigh, 0, unroll=2)
 
         def total(hot, rows):
             return jnp.dot(hot, rows, preferred_element_type=F32).astype(BF).reshape(NS, 32, 2 * K)
@@ -512,6 +542,27 @@
 
         lax.fori_loop(0, 4, own, 0)
 
+    def drain(src, send_sem, recv_sem):
+        return pltpu.make_async_remote_copy(
+            src_ref=src, dst_ref=src, send_sem=send_sem, recv_sem=recv_sem,
+            device_id=(mb, ms), device_id_type=MESH,
+        )
+
+    def mirrored(t, carry):
+        drain(msend.at[t], m_s.at[t], m_r.at[t]).wait()
+
+        def one(m, inner):
+            i = 6 * (m // 2) + 2 * t + 1 + lax.rem(m, 2)
+
+            @pl.when(i < KYB // 2)
+            def _():
+                finish(KYB - i, mrecv[t, m].astype(F32))
+
+            return inner
+
+        lax.fori_loop(0, 4, one, 0)
+        return carry
+
     def consume(t, carry):
         @pl.when(jnp.logical_or(t < LAST, core == 0))
         def _():
@@ -522,6 +573,10 @@
         @pl.when(t > 0)
         def _():
             gather(t - 1)
+
+        @pl.when(t > 1)
+        def _():
+            mirrored(t - 2, 0)
 
         return carry
 
@@ -534,28 +589,7 @@
         x += zgot[z].astype(F32)
     finish(0, x)
 
-    def drain(src, send_sem, recv_sem):
-        return pltpu.make_async_remote_copy(
-            src_ref=src, dst_ref=src, send_sem=send_sem, recv_sem=recv_sem,
-            device_id=(mb, ms), device_id_type=MESH,
-        )
-
-    def mirrored(t, carry):
-        drain(msend.at[t], m_s.at[t], m_r.at[t]).wait()
-
-        def one(m, inner):
-            i = 6 * (m // 2) + 2 * t + 1 + lax.rem(m, 2)
-
-            @pl.when(i < KYB // 2)
-            def _():
-                finish(KYB - i, mrecv[t, m].astype(F32))
-
-            return inner
-
-        lax.fori_loop(0, 4, one, 0)
-        return carry
-
-    lax.fori_loop(0, SHARED, mirrored, 0)
+    mirrored(SHARED - 1, 0)
 
     drain(crecv.at[pl.ds(0, 31)], code_s, code_r).wait_send()
     drain(nsend.at[pl.ds(0, 7)], n_s, n_r).wait_send()
@@ -594,17 +628,19 @@
             pltpu.VMEM((KYB * PL, 2 * K), BF),
             pltpu.VMEM((6, 64 * PP, 128), F32),
             pltpu.VMEM((K, 128), F32),
-            pltpu.VMEM((32, 128), F32),
-            pltpu.VMEM((32, 32, 128), BF),
-            pltpu.VMEM((32 * 32, 128), F32),
-            pltpu.VMEM((TILES, 32, PP, 128), F32),
-            pltpu.VMEM((4, 32, PP, K), F32),
+            pltpu.VMEM((16, 128), F32),
+            pltpu.VMEM((32, 16, 128), BF),
+            pltpu.VMEM((32 * 16, 128), F32),
+            pltpu.VMEM((TILES, 512, 128), F32),
+            pltpu.VMEM((512, 4 * K), F32),
+            pltpu.VMEM((3 * GROUP, 4 * K), BF),
+            pltpu.VMEM((3 * GROUP, 128), BF),
             pltpu.VMEM((2, 512, 2 * K), F32),
             pltpu.VMEM((512, 2 * K), BF),
             pltpu.VMEM((512, 2 * K), BF),
             pltpu.VMEM((TILES, 32, 16, 2 * K), BF),
             pltpu.VMEM((TILES, 32, 16, 2 * K), BF),
-            pltpu.VMEM((32, 32, 128), BF),
+            pltpu.VMEM((32, 16, 128), BF),
             pltpu.VMEM((TILES, NS, 64, 2 * K), BF),
             pltpu.VMEM((SHARED, NS, 64, 2 * K), BF),
             pltpu.VMEM((NS // 2, PL, 2 * K), BF),

time: 76.8 us -> 67.3 us (0.88)
  Pallas kernels: 74.7 us -> 65.2 us
    pallas_call x1, Pallas kernels: 74.7 us -> 65.2 us  [per_device(): pl.pallas_call(kernel, out_shape=jax.ShapeDtypeStruct((KYB * PL, 2 * K),...]
where the time goes in v6:
time: 67.3 us; the launch traced here: 67.1 us
  Pallas kernels  65.2 us (97%)
  local copies, waits for them, and re-layouts  1.92 us (3%)
    pallas_call x1, Pallas kernels, per_device(): pl.pallas_call(kernel, out_shape=jax.ShapeDtypeStruct((KYB * PL, 2 * K),...  65.2 us
    unnamed x1, local copies, waits for them, and re-layouts  1.92 us

profile of v6, /device:TPU:1, one launch (start us, length us, event | category | flops | bytes accessed | tf_op | source)
XLA Modules:
  0.0 67.1 jit_solution(10045494734533183584)
XLA Ops:
  0.0 65.2 %shard_map.100 = bf16[384,768]{1,0:T(8,128)(2,1)} custom-call(s32[8]{0:T(128)} %classes.1, s32[8]{0:T(128)} %kinds_in.1, f32[16]{0:T(128)} %defocus.1, s32[2,8]{1,0:T(2,128)} %bitcast.5, s32[8,8]{1,0:T(8,128)} %counts.1, bf16[4,128,384]{2,1,0:T(8,128)(2,1)} %constant.4.clone.left, bf16[8,384,384]{2,1,0:T(8,128)(2,1)} %img_in.1, ...), custom_call_target="tpu_custom_call" | custom-call | tf_op jit(solution)/shard_map/pallas_call | solution.py:619
  65.2 1.9 %copy.12 = bf16[24,16,768]{2,1,0:T(8,128)(2,1)} copy(bf16[24,16,768]{2,1,0:T(8,128)(2,1)} %bitcast.3) | data formatting | bytes 1179648

commit v7 on v6

--- a/solution.py
+++ b/solution.py
@@ -26,6 +26,7 @@
 F32 = jnp.float32
 LAST = SHARED
 EXTRA = 13
+HOPS = ((1, 0), (3, 1), (2, 0), (3, 0), (1, 1), (2, 1), (0, 1))
 NCNT = TILES + 3
 MOVES = 40
 GROUP = 64
@@ -154,13 +155,20 @@
     other = 1 - core
 
     def send_rows(t):
-        to_plane(mb, other, sendb.at[t, mb * 2 + other], recvb.at[t, me], row_s.at[t], row_r.at[t])
-        pltpu.make_async_copy(sendb.at[t, me], recvb.at[t, me], row_r.at[t]).start()
-        for flip in range(2):
-            h = core if flip == 0 else other
+        for h in range(2):
+            own = recvb.at[t, me]
+
+            @pl.when(core == h)
+            def _():
+                pltpu.make_async_copy(sendb.at[t, me], own, row_r.at[t]).start()
+
+            @pl.when(core != h)
+            def _():
+                to_plane(mb, h, sendb.at[t, mb * 2 + h], own, row_s.at[t], row_r.at[t])
+
             for turn in TURNS:
                 b = peer_of(turn)
-                to_plane(b, h, sendb.at[t, b * 2 + h], recvb.at[t, me], row_s.at[t], row_r.at[t])
+                to_plane(b, h, sendb.at[t, b * 2 + h], own, row_s.at[t], row_r.at[t])
 
     def send_last():
         t = LAST
@@ -245,15 +253,11 @@
         def _():
             pl.semaphore_wait(barrier, 31 + NS - 1)
 
-        @pl.when(t < LAST)
-        def _():
-            send_rows(t)
-
-        pl.when(t == LAST)(send_last)
+        send_rows(t)
         pl.when(t == 0)(tell)
         return carry
 
-    lax.fori_loop(0, TILES, produce, 0)
+    lax.fori_loop(0, 2, produce, 0)
 
     pltpu.make_async_copy(crecv, crecv, code_r).wait()
 
@@ -282,38 +286,44 @@
             axis=1,
         )
 
-    row_id = lax.broadcasted_iota(jnp.int32, (128, 128), 0)
-    row_class = jnp.where(row_id < 3 * NDEF, lax.rem(row_id, NDEF), -1).astype(F32)
+    def to_slab(src, dst, send_sem, recv_sem):
+        for dz, flip in HOPS:
+            z = lax.rem(mz + jnp.where(core == 0, dz, 4 - dz), 4)
+            peer = z * 2 + (1 - core if flip else core)
+            pltpu.make_async_remote_copy(
+                src_ref=src(peer), dst_ref=dst, send_sem=send_sem, recv_sem=recv_sem,
+                device_id=(mb, peer), device_id_type=MESH,
+            ).start()
+
     kind4 = pair_codes(10)
-    kinds = jnp.concatenate(
-        [jnp.where(row_class == kind4[g : g + 1, :], 1.0, 0.0).astype(BF) for g in range(4)],
-        axis=1,
-    )
-
-    def count(n, carry):
-        tally = lax.dot_general(
-            one_hot(pair_codes(jnp.where(n < TILES, n, n + SHARED))), kinds,
-            (((1,), (1,)), ((), ())), preferred_element_type=F32,
-        )
-        start = pl.multiple_of(n * 32, 32)
-        nsend[:, pl.ds(start, 32), :] = tally.astype(BF).reshape(NS, 32, 128)
-        return carry
-
-    lax.fori_loop(0, NCNT, count, 0)
-
-    def to_slab(q, src, dst, send_sem, recv_sem):
-        peer = lax.rem(ms + q, NS)
-        pltpu.make_async_remote_copy(
-            src_ref=src(peer), dst_ref=dst, send_sem=send_sem, recv_sem=recv_sem,
-            device_id=(mb, peer), device_id_type=MESH,
-        ).start()
-
-    pltpu.make_async_copy(nsend.at[ms], nrecv.at[ms], n_r).start()
-    def send_counts(q, carry):
-        to_slab(q, lambda peer: nsend.at[peer], nrecv.at[ms], n_s, n_r)
-        return carry
-
-    lax.fori_loop(1, NS, send_counts, 0)
+
+    def tally():
+        spot_z = lax.broadcasted_iota(jnp.int32, (128, 128), 0).astype(F32)
+        slot_k = ((lax.broadcasted_iota(jnp.int32, (4, 128), 1) // PP) & 1).astype(F32)
+        which = kind4 + NDEF * slot_k
+
+        def hot(code4):
+            return jnp.concatenate(
+                [
+                    jnp.where(spot_z == code4[g : g + 1, :], 1.0, 0.0).astype(BF)
+                    for g in range(4)
+                ],
+                axis=1,
+            )
+
+        def one(n, acc):
+            code4 = pair_codes(jnp.where(n < TILES, n, n + SHARED))
+            flat = code4 - 16.0 * jnp.floor(code4 * (1.0 / 16)) + 16.0 * jnp.floor(code4 * (1.0 / 32))
+            group = ((n & 3) * 2 * NDEF).astype(F32)
+            return acc + lax.dot_general(
+                hot(flat), hot(which + group), (((1,), (1,)), ((), ())), preferred_element_type=F32
+            )
+
+        for half, (low, high) in enumerate(((0, 4), (4, NCNT))):
+            acc = lax.fori_loop(low, high, one, jnp.zeros((128, 128), F32))
+            nsend[:, :, pl.ds(half * 128, 128)] = acc.astype(BF).reshape(NS, PL, 128)
+        to_slab(lambda peer: nsend.at[peer], nrecv.at[ms], n_s, n_r)
+        pltpu.make_async_copy(nsend.at[ms], nrecv.at[ms], n_r).start()
 
     slot_of = (lane8 // 8) * 2 + (lane8 & 1)
     part = (lane8 // 2) & 3
@@ -430,29 +440,33 @@
         def total(hot, rows):
             return jnp.dot(hot, rows, preferred_element_type=F32).astype(BF).reshape(NS, 32, 2 * K)
 
+        def give(start, size, dst):
+            rows = pl.ds(start, size)
+            to_slab(lambda peer: zsend.at[t, peer, rows], dst, z_s.at[t], z_r.at[t])
+            pltpu.make_async_copy(zsend.at[t, ms, rows], dst, z_r.at[t]).start()
+
+        @pl.when(t < LAST)
+        def _():
+            zsend[t, :, pl.ds(32, 32), :] = total(one_hot(pair_codes(TILES + t)), wm[...])
+            whole = jnp.logical_or(t < SHARED - 1, core == 0)
+
+            @pl.when(whole)
+            def _():
+                give(32, 32, zrecv.at[t, ms, pl.ds(32, 32)])
+
+            @pl.when(jnp.logical_not(whole))
+            def _():
+                give(32, PL, zrecv.at[t, ms, pl.ds(32, PL)])
+
         zsend[t, :, pl.ds(0, 32), :] = total(one_hot(pair_codes(t)), wp[...])
 
         @pl.when(t < LAST)
         def _():
-            zsend[t, :, pl.ds(32, 32), :] = total(one_hot(pair_codes(TILES + t)), wm[...])
-
-            def send(q, carry):
-                to_slab(q, lambda peer: zsend.at[t, peer], zrecv.at[t, ms], z_s.at[t], z_r.at[t])
-                return carry
-
-            lax.fori_loop(1, NS, send, 0)
-            pltpu.make_async_copy(zsend.at[t, ms], zrecv.at[t, ms], z_r.at[t]).start()
+            give(0, 32, zrecv.at[t, ms, pl.ds(0, 32)])
 
         @pl.when(t == LAST)
         def _():
-            top = pl.ds(0, PL)
-
-            def send(q, carry):
-                to_slab(q, lambda peer: zsend.at[t, peer, top], zgot.at[mz], z_s.at[t], z_r.at[t])
-                return carry
-
-            lax.fori_loop(1, NS, send, 0)
-            pltpu.make_async_copy(zsend.at[t, ms, top], zgot.at[mz], z_r.at[t]).start()
+            give(0, PL, zgot.at[mz])
 
     def weights():
         lane_k = lax.broadcasted_iota(jnp.int32, (32, 128), 1)
@@ -483,6 +497,18 @@
             for z in range(1, NS // 2):
                 x += nrecv[2 * z + h].astype(F32)
             own, more = 6 * h + 1, 6 * h + EXTRA
+            lane = lax.broadcasted_iota(jnp.int32, (PL, 128), 1)
+            blocks = []
+            for g in range(2 * NCNT):
+                part = x[:, g // 8 * 128 : g // 8 * 128 + 128]
+                turn = [
+                    pltpu.roll(part, (NDEF * (n - g)) % 128, 1) if (n - g) % 8 else part
+                    for n in range(3)
+                ]
+                blocks.append(
+                    jnp.where(lane < NDEF, turn[0], jnp.where(lane < 2 * NDEF, turn[1], turn[2]))
+                )
+            x = jnp.concatenate(blocks, axis=0)
 
             def times(part, i, rows):
                 return (part.reshape(rows, PL, 128) * tws[pl.ds(i, rows), :][:, None, :]).reshape(
@@ -516,7 +542,14 @@
             out[rows, cols] = (top * inverse).astype(BF)
 
     def gather(t):
-        pltpu.make_async_copy(zrecv.at[t], zrecv.at[t], z_r.at[t]).wait()
+        @pl.when(t < SHARED - 1)
+        def _():
+            pltpu.make_async_copy(zrecv.at[t], zrecv.at[t], z_r.at[t]).wait()
+
+        @pl.when(t == SHARED - 1)
+        def _():
+            some = zrecv.at[t, pl.ds(0, 7)]
+            pltpu.make_async_copy(some, some, z_r.at[t]).wait()
 
         def over_z(h, start):
             rows = pl.ds(pl.multiple_of(start, PL), PL)
@@ -529,11 +562,17 @@
             msend[t, m] = over_z(m // 2, 2 * PL + lax.rem(m, 2) * PL).astype(BF)
             return carry
 
-        lax.fori_loop(0, 4, mirror, 0)
-        pltpu.make_async_remote_copy(
-            src_ref=msend.at[t], dst_ref=mrecv.at[t], send_sem=m_s.at[t], recv_sem=m_r.at[t],
-            device_id=(NB - 1 - mb, ms), device_id_type=MESH,
-        ).start()
+        def pass_on(size):
+            rows = pl.ds(0, size)
+            lax.fori_loop(0, size, mirror, 0)
+            pltpu.make_async_remote_copy(
+                src_ref=msend.at[t, rows], dst_ref=mrecv.at[t, rows],
+                send_sem=m_s.at[t], recv_sem=m_r.at[t],
+                device_id=(NB - 1 - mb, ms), device_id_type=MESH,
+            ).start()
+
+        pl.when(t < SHARED - 1)(lambda: pass_on(4))
+        pl.when(t == SHARED - 1)(lambda: pass_on(3))
 
         def own(m, carry):
             h, j = m // 2, lax.rem(m, 2)
@@ -549,7 +588,14 @@
         )
 
     def mirrored(t, carry):
-        drain(msend.at[t], m_s.at[t], m_r.at[t]).wait()
+        @pl.when(t < SHARED - 1)
+        def _():
+            drain(msend.at[t], m_s.at[t], m_r.at[t]).wait()
+
+        @pl.when(t == SHARED - 1)
+        def _():
+            drain(msend.at[t, pl.ds(0, 3)], m_s.at[t], m_r.at[t]).wait()
+
 
         def one(m, inner):
             i = 6 * (m // 2) + 2 * t + 1 + lax.rem(m, 2)
@@ -568,21 +614,34 @@
         def _():
             process(t)
 
-        pl.when(t == 0)(weights)
-
-        @pl.when(t > 0)
+        @pl.when(t < 2)
+        def _():
+            compute(t + 2)
+
+        @pl.when(t == 0)
+        def _():
+            send_rows(2)
+
+        @pl.when(t == 1)
+        def _():
+            send_last()
+            tally()
+            weights()
+
+        @pl.when(jnp.logical_or(t == 1, t == 2))
         def _():
             gather(t - 1)
 
-        @pl.when(t > 1)
-        def _():
-            mirrored(t - 2, 0)
+        @pl.when(t == LAST)
+        def _():
+            lax.fori_loop(0, 2, mirrored, 0)
 
         return carry
 
     load_ref.wait()
     lax.fori_loop(0, TILES, consume, 0)
 
+    gather(SHARED - 1)
     pltpu.make_async_copy(zgot, zgot, z_r.at[LAST]).wait()
     x = zgot[0].astype(F32)
     for z in range(1, NS // 2):
@@ -595,7 +654,16 @@
     drain(nsend.at[pl.ds(0, 7)], n_s, n_r).wait_send()
     def drain_tile(t, carry):
         drain(sendb.at[t, pl.ds(0, 31)], row_s.at[t], row_r.at[t]).wait_send()
-        drain(zsend.at[t, pl.ds(0, 7)], z_s.at[t], z_r.at[t]).wait_send()
+        whole = jnp.logical_or(t < SHARED - 1, core == 0)
+
+        @pl.when(whole)
+        def _():
+            drain(zsend.at[t, pl.ds(0, 7)], z_s.at[t], z_r.at[t]).wait_send()
+
+        @pl.when(jnp.logical_not(whole))
+        def _():
+            drain(zsend.at[t, pl.ds(0, 7), pl.ds(0, 48)], z_s.at[t], z_r.at[t]).wait_send()
+
         return carry
 
     lax.fori_loop(0, SHARED, drain_tile, 0)
@@ -644,8 +712,8 @@
             pltpu.VMEM((TILES, NS, 64, 2 * K), BF),
             pltpu.VMEM((SHARED, NS, 64, 2 * K), BF),
             pltpu.VMEM((NS // 2, PL, 2 * K), BF),
-            pltpu.VMEM((NS, NCNT * 32, 128), BF),
-            pltpu.VMEM((NS, NCNT * 32, 128), BF),
+            pltpu.VMEM((NS, PL, 256), BF),
+            pltpu.VMEM((NS, PL, 256), BF),
             pltpu.VMEM((SHARED, 4, PL, 2 * K), BF),
             pltpu.VMEM((SHARED, 4, PL, 2 * K), BF),
             pltpu.VMEM(((KYB + 1) * PL, K), F32),

time: 67.3 us -> 71.7 us (1.065)
  Pallas kernels: 65.2 us -> 69.6 us
    pallas_call x1, Pallas kernels: 65.2 us -> 69.6 us  [per_device(): pl.pallas_call(kernel, out_shape=jax.ShapeDtypeStruct((KYB * PL, 2 * K),...]
where the time goes in v7:
time: 71.7 us; the launch traced here: 71.5 us
  Pallas kernels  69.6 us (97%)
  local copies, waits for them, and re-layouts  1.92 us (3%)
    pallas_call x1, Pallas kernels, per_device(): pl.pallas_call(kernel, out_shape=jax.ShapeDtypeStruct((KYB * PL, 2 * K),...  69.6 us
    unnamed x1, local copies, waits for them, and re-layouts  1.92 us

profile of v7, /device:TPU:1, one launch (start us, length us, event | category | flops | bytes accessed | tf_op | source)
XLA Modules:
  0.0 71.5 jit_solution(17511310107822873926)
XLA Ops:
  0.0 69.6 %shard_map.100 = bf16[384,768]{1,0:T(8,128)(2,1)} custom-call(s32[8]{0:T(128)} %classes.1, s32[8]{0:T(128)} %kinds_in.1, f32[16]{0:T(128)} %defocus.1, s32[2,8]{1,0:T(2,128)} %bitcast.5, s32[8,8]{1,0:T(8,128)} %counts.1, bf16[4,128,384]{2,1,0:T(8,128)(2,1)} %constant.4.clone.left, bf16[8,384,384]{2,1,0:T(8,128)(2,1)} %img_in.1, ...), custom_call_target="tpu_custom_call" | custom-call | tf_op jit(solution)/shard_map/pallas_call | solution.py:687
  69.6 1.9 %copy.12 = bf16[24,16,768]{2,1,0:T(8,128)(2,1)} copy(bf16[24,16,768]{2,1,0:T(8,128)(2,1)} %bitcast.3) | data formatting | bytes 1179648

commit v8 on v7

--- a/solution.py
+++ b/solution.py
@@ -64,7 +64,7 @@
     out,
     img, right, dest, ref, scr, cscr, cwide, codes, cf, sc, vx, table_x, table_s, pq, wp, wm,
     sendb, recvb, crecv, zsend, zrecv, zgot, nsend, nrecv, msend, mrecv, wts, tws,
-    img_m, right_m, dest_m, ref_m, code_s, code_r, row_s, row_r, z_s, z_r, n_s, n_r, m_s, m_r,
+    img_m, right_m, dest_m, ref_m, code_s, code_r, row_s, row_r, z_s, z_r, y_s, y_r, n_s, n_r, m_s, m_r,
 ):
     mb = lax.axis_index("batch")
     ms = lax.axis_index("slab")
@@ -440,10 +440,10 @@
         def total(hot, rows):
             return jnp.dot(hot, rows, preferred_element_type=F32).astype(BF).reshape(NS, 32, 2 * K)
 
-        def give(start, size, dst):
+        def give(start, size, dst, send_sem, recv_sem):
             rows = pl.ds(start, size)
-            to_slab(lambda peer: zsend.at[t, peer, rows], dst, z_s.at[t], z_r.at[t])
-            pltpu.make_async_copy(zsend.at[t, ms, rows], dst, z_r.at[t]).start()
+            to_slab(lambda peer: zsend.at[t, peer, rows], dst, send_sem, recv_sem)
+            pltpu.make_async_copy(zsend.at[t, ms, rows], dst, recv_sem).start()
 
         @pl.when(t < LAST)
         def _():
@@ -452,21 +452,21 @@
 
             @pl.when(whole)
             def _():
-                give(32, 32, zrecv.at[t, ms, pl.ds(32, 32)])
+                give(32, 32, zrecv.at[t, ms, pl.ds(32, 32)], y_s.at[t], y_r.at[t])
 
             @pl.when(jnp.logical_not(whole))
             def _():
-                give(32, PL, zrecv.at[t, ms, pl.ds(32, PL)])
+                give(32, PL, zrecv.at[t, ms, pl.ds(32, PL)], y_s.at[t], y_r.at[t])
 
         zsend[t, :, pl.ds(0, 32), :] = total(one_hot(pair_codes(t)), wp[...])
 
         @pl.when(t < LAST)
         def _():
-            give(0, 32, zrecv.at[t, ms, pl.ds(0, 32)])
+            give(0, 32, zrecv.at[t, ms, pl.ds(0, 32)], z_s.at[t], z_r.at[t])
 
         @pl.when(t == LAST)
         def _():
-            give(0, PL, zgot.at[mz])
+            give(0, PL, zgot.at[mz], z_s.at[t], z_r.at[t])
 
     def weights():
         lane_k = lax.broadcasted_iota(jnp.int32, (32, 128), 1)
@@ -544,12 +544,13 @@
     def gather(t):
         @pl.when(t < SHARED - 1)
         def _():
-            pltpu.make_async_copy(zrecv.at[t], zrecv.at[t], z_r.at[t]).wait()
+            some = zrecv.at[t, :, pl.ds(32, 32)]
+            pltpu.make_async_copy(some, some, y_r.at[t]).wait()
 
         @pl.when(t == SHARED - 1)
         def _():
-            some = zrecv.at[t, pl.ds(0, 7)]
-            pltpu.make_async_copy(some, some, z_r.at[t]).wait()
+            some = zrecv.at[t, pl.ds(0, 6), pl.ds(32, 32)]
+            pltpu.make_async_copy(some, some, y_r.at[t]).wait()
 
         def over_z(h, start):
             rows = pl.ds(pl.multiple_of(start, PL), PL)
@@ -574,6 +575,9 @@
         pl.when(t < SHARED - 1)(lambda: pass_on(4))
         pl.when(t == SHARED - 1)(lambda: pass_on(3))
 
+        some = zrecv.at[t, :, pl.ds(0, 32)]
+        pltpu.make_async_copy(some, some, z_r.at[t]).wait()
+
         def own(m, carry):
             h, j = m // 2, lax.rem(m, 2)
             finish(6 * h + 2 * t + 1 + j, over_z(h, j * PL))
@@ -625,7 +629,6 @@
         @pl.when(t == 1)
         def _():
             send_last()
-            tally()
             weights()
 
         @pl.when(jnp.logical_or(t == 1, t == 2))
@@ -638,6 +641,7 @@
 
         return carry
 
+    tally()
     load_ref.wait()
     lax.fori_loop(0, TILES, consume, 0)
 
@@ -658,12 +662,13 @@
 
         @pl.when(whole)
         def _():
-            drain(zsend.at[t, pl.ds(0, 7)], z_s.at[t], z_r.at[t]).wait_send()
+            drain(zsend.at[t, pl.ds(0, 7), pl.ds(0, 32)], y_s.at[t], y_r.at[t]).wait_send()
 
         @pl.when(jnp.logical_not(whole))
         def _():
-            drain(zsend.at[t, pl.ds(0, 7), pl.ds(0, 48)], z_s.at[t], z_r.at[t]).wait_send()
-
+            drain(zsend.at[t, pl.ds(0, 7), pl.ds(0, PL)], y_s.at[t], y_r.at[t]).wait_send()
+
+        drain(zsend.at[t, pl.ds(0, 7), pl.ds(0, 32)], z_s.at[t], z_r.at[t]).wait_send()
         return carry
 
     lax.fori_loop(0, SHARED, drain_tile, 0)
@@ -719,7 +724,8 @@
             pltpu.VMEM(((KYB + 1) * PL, K), F32),
             pltpu.VMEM((32, 128), F32),
             dma((PP,)), dma, dma, dma, dma, dma, dma((TILES,)), dma((TILES,)),
-            dma((TILES,)), dma((TILES,)), dma, dma, dma((SHARED,)), dma((SHARED,)),
+            dma((TILES,)), dma((TILES,)), dma((SHARED,)), dma((SHARED,)), dma, dma,
+            dma((SHARED,)), dma((SHARED,)),
         ],
         compiler_params=pltpu.CompilerParams(
             collective_id=0, has_side_effects=True, vmem_limit_bytes=60 * 1024 * 1024

time: 71.7 us -> 62.5 us (0.87)
  Pallas kernels: 69.6 us -> 60.4 us
    pallas_call x1, Pallas kernels: 69.6 us -> 60.4 us  [per_device(): pl.pallas_call(kernel, out_shape=jax.ShapeDtypeStruct((KYB * PL, 2 * K),...]
where the time goes in v8:
time: 62.5 us; the launch traced here: 62.4 us
  Pallas kernels  60.4 us (97%)
  local copies, waits for them, and re-layouts  1.92 us (3%)
    pallas_call x1, Pallas kernels, per_device(): pl.pallas_call(kernel, out_shape=jax.ShapeDtypeStruct((KYB * PL, 2 * K),...  60.4 us
    unnamed x1, local copies, waits for them, and re-layouts  1.92 us

profile of v8, /device:TPU:1, one launch (start us, length us, event | category | flops | bytes accessed | tf_op | source)
XLA Modules:
  0.0 62.4 jit_solution(15912207186922945363)
XLA Ops:
  0.0 60.4 %shard_map.100 = bf16[384,768]{1,0:T(8,128)(2,1)} custom-call(s32[8]{0:T(128)} %classes.1, s32[8]{0:T(128)} %kinds_in.1, f32[16]{0:T(128)} %defocus.1, s32[2,8]{1,0:T(2,128)} %bitcast.5, s32[8,8]{1,0:T(8,128)} %counts.1, bf16[4,128,384]{2,1,0:T(8,128)(2,1)} %constant.4.clone.left, bf16[8,384,384]{2,1,0:T(8,128)(2,1)} %img_in.1, ...), custom_call_target="tpu_custom_call" | custom-call | tf_op jit(solution)/shard_map/pallas_call | solution.py:692
  60.5 1.9 %copy.12 = bf16[24,16,768]{2,1,0:T(8,128)(2,1)} copy(bf16[24,16,768]{2,1,0:T(8,128)(2,1)} %bitcast.3) | data formatting | bytes 1179648

commit v9 on v8

--- a/solution.py
+++ b/solution.py
@@ -86,7 +86,7 @@
     load_right = pltpu.make_async_copy(right_in, right, right_m)
     load_dest = pltpu.make_async_copy(dest_in, dest, dest_m)
     load_ref = pltpu.make_async_copy(ref_in, ref, ref_m)
-    for load in (*loads, load_dest, load_right, load_ref):
+    for load in (load_dest, *loads, load_right, load_ref):
         load.start()
 
     def greet_plane(q, carry):
@@ -237,6 +237,7 @@
         cwide[10:13, :] = person[0:3]
         lax.fori_loop(0, 2 * NB, arrange, 0)
 
+    def tell_send():
         def send_codes(q, carry):
             i = lax.rem(me + q, 32)
             to_plane(i // 2, lax.rem(i, 2), codes.at[i], crecv.at[me], code_s, code_r)
@@ -245,85 +246,6 @@
         pltpu.make_async_copy(codes.at[me], crecv.at[me], code_r).start()
         lax.fori_loop(1, 32, send_codes, 0)
 
-
-    def produce(t, carry):
-        compute(t)
-
-        @pl.when(t == 0)
-        def _():
-            pl.semaphore_wait(barrier, 31 + NS - 1)
-
-        send_rows(t)
-        pl.when(t == 0)(tell)
-        return carry
-
-    lax.fori_loop(0, 2, produce, 0)
-
-    pltpu.make_async_copy(crecv, crecv, code_r).wait()
-
-    def widen(i, carry):
-        cf[pl.ds(pl.multiple_of(i * 16, 16), 16), :] = crecv[i].astype(F32)
-        return carry
-
-    lax.fori_loop(0, 32, widen, 0)
-
-    lane = lax.broadcasted_iota(jnp.int32, (32, 128), 1)
-    sub = lax.broadcasted_iota(jnp.int32, (32, 128), 0)
-    mine = (lane // 16) == lax.rem(sub, 8)
-
-    def pair_codes(row):
-        got = cf[pl.ds(row, 32, stride=16), :]
-        return jnp.sum(jnp.where(mine, got, 0.0).reshape(4, 8, 128), axis=1)
-
-    spot = lax.broadcasted_iota(jnp.int32, (256, 128), 0).astype(F32)
-
-    def one_hot(code4):
-        return jnp.concatenate(
-            [
-                jnp.where(spot == code4[g : g + 1, :], 1.0, 0.0).astype(BF)
-                for g in range(4)
-            ],
-            axis=1,
-        )
-
-    def to_slab(src, dst, send_sem, recv_sem):
-        for dz, flip in HOPS:
-            z = lax.rem(mz + jnp.where(core == 0, dz, 4 - dz), 4)
-            peer = z * 2 + (1 - core if flip else core)
-            pltpu.make_async_remote_copy(
-                src_ref=src(peer), dst_ref=dst, send_sem=send_sem, recv_sem=recv_sem,
-                device_id=(mb, peer), device_id_type=MESH,
-            ).start()
-
-    kind4 = pair_codes(10)
-
-    def tally():
-        spot_z = lax.broadcasted_iota(jnp.int32, (128, 128), 0).astype(F32)
-        slot_k = ((lax.broadcasted_iota(jnp.int32, (4, 128), 1) // PP) & 1).astype(F32)
-        which = kind4 + NDEF * slot_k
-
-        def hot(code4):
-            return jnp.concatenate(
-                [
-                    jnp.where(spot_z == code4[g : g + 1, :], 1.0, 0.0).astype(BF)
-                    for g in range(4)
-                ],
-                axis=1,
-            )
-
-        def one(n, acc):
-            code4 = pair_codes(jnp.where(n < TILES, n, n + SHARED))
-            flat = code4 - 16.0 * jnp.floor(code4 * (1.0 / 16)) + 16.0 * jnp.floor(code4 * (1.0 / 32))
-            group = ((n & 3) * 2 * NDEF).astype(F32)
-            return acc + lax.dot_general(
-                hot(flat), hot(which + group), (((1,), (1,)), ((), ())), preferred_element_type=F32
-            )
-
-        for half, (low, high) in enumerate(((0, 4), (4, NCNT))):
-            acc = lax.fori_loop(low, high, one, jnp.zeros((128, 128), F32))
-            nsend[:, :, pl.ds(half * 128, 128)] = acc.astype(BF).reshape(NS, PL, 128)
-        to_slab(lambda peer: nsend.at[peer], nrecv.at[ms], n_s, n_r)
-        pltpu.make_async_copy(nsend.at[ms], nrecv.at[ms], n_r).start()
 
     slot_of = (lane8 // 8) * 2 + (lane8 & 1)
     part = (lane8 // 2) & 3
@@ -365,6 +287,88 @@
             jnp.concatenate([move, tone, jnp.zeros((spare, 128), F32)], axis=0)
         )
 
+    tell()
+    tabulate()
+
+    def produce(t, carry):
+        compute(t)
+
+        @pl.when(t == 0)
+        def _():
+            pl.semaphore_wait(barrier, 31 + NS - 1)
+            tell_send()
+
+        send_rows(t)
+        return carry
+
+    lax.fori_loop(0, 2, produce, 0)
+
+    pltpu.make_async_copy(crecv, crecv, code_r).wait()
+
+    def widen(i, carry):
+        cf[pl.ds(pl.multiple_of(i * 16, 16), 16), :] = crecv[i].astype(F32)
+        return carry
+
+    lax.fori_loop(0, 32, widen, 0)
+
+    lane = lax.broadcasted_iota(jnp.int32, (32, 128), 1)
+    sub = lax.broadcasted_iota(jnp.int32, (32, 128), 0)
+    mine = (lane // 16) == lax.rem(sub, 8)
+
+    def pair_codes(row):
+        got = cf[pl.ds(row, 32, stride=16), :]
+        return jnp.sum(jnp.where(mine, got, 0.0).reshape(4, 8, 128), axis=1)
+
+    spot = lax.broadcasted_iota(jnp.int32, (256, 128), 0).astype(F32)
+
+    def one_hot(code4):
+        return jnp.concatenate(
+            [
+                jnp.where(spot == code4[g : g + 1, :], 1.0, 0.0).astype(BF)
+                for g in range(4)
+            ],
+            axis=1,
+        )
+
+    def to_slab(src, dst, send_sem, recv_sem):
+        for dz, flip in HOPS:
+            z = lax.rem(mz + jnp.where(core == 0, dz, 4 - dz), 4)
+            peer = z * 2 + (1 - core if flip else core)
+            pltpu.make_async_remote_copy(
+                src_ref=src(peer), dst_ref=dst, send_sem=send_sem, recv_sem=recv_sem,
+                device_id=(mb, peer), device_id_type=MESH,
+            ).start()
+
+    kind4 = pair_codes(10)
+
+    def tally():
+        spot_z = lax.broadcasted_iota(jnp.int32, (128, 128), 0).astype(F32)
+        slot_k = ((lax.broadcasted_iota(jnp.int32, (4, 128), 1) // PP) & 1).astype(F32)
+        which = kind4 + NDEF * slot_k
+
+        def hot(code4):
+            return jnp.concatenate(
+                [
+                    jnp.where(spot_z == code4[g : g + 1, :], 1.0, 0.0).astype(BF)
+                    for g in range(4)
+                ],
+                axis=1,
+            )
+
+        def one(n, acc):
+            code4 = pair_codes(jnp.where(n < TILES, n, n + SHARED))
+            flat = code4 - 16.0 * jnp.floor(code4 * (1.0 / 16)) + 16.0 * jnp.floor(code4 * (1.0 / 32))
+            group = ((n & 3) * 2 * NDEF).astype(F32)
+            return acc + lax.dot_general(
+                hot(flat), hot(which + group), (((1,), (1,)), ((), ())), preferred_element_type=F32
+            )
+
+        for half, (low, high) in enumerate(((0, 4), (4, NCNT))):
+            acc = lax.fori_loop(low, high, one, jnp.zeros((128, 128), F32))
+            nsend[:, :, pl.ds(half * 128, 128)] = acc.astype(BF).reshape(NS, PL, 128)
+        to_slab(lambda peer: nsend.at[peer], nrecv.at[ms], n_s, n_r)
+        pltpu.make_async_copy(nsend.at[ms], nrecv.at[ms], n_r).start()
+
     entry = (rows_of((3 * GROUP, 128)) & (GROUP - 1)).astype(F32)
 
     def chosen(move4, table):
@@ -384,7 +388,6 @@
             hot, table, (((0,), (0,)), ((), ())), preferred_element_type=F32
         )
 
-    tabulate()
     vx[...] = chosen(pair_codes(11), table_x[...])
     scal = chosen(pair_codes(12), table_s[...])
     sc[0] = scal
@@ -435,7 +438,7 @@
                 to[rows, pl.ds((n % 2) * K, K)] = jnp.concatenate(got[n], axis=0).astype(BF)
             return carry
 
-        lax.fori_loop(0, 32, weigh, 0, unroll=2)
+        lax.fori_loop(0, 32, weigh, 0, unroll=4)
 
         def total(hot, rows):
             return jnp.dot(hot, rows, preferred_element_type=F32).astype(BF).reshape(NS, 32, 2 * K)

time: 62.5 us -> 59.1 us (0.946)
  Pallas kernels: 60.4 us -> 57.1 us
    pallas_call x1, Pallas kernels: 60.4 us -> 57.1 us  [per_device(): pl.pallas_call(kernel, out_shape=jax.ShapeDtypeStruct((KYB * PL, 2 * K),...]
where the time goes in v9:
time: 59.1 us; the launch traced here: 59 us
  Pallas kernels  57.1 us (97%)
  local copies, waits for them, and re-layouts  1.92 us (3%)
    pallas_call x1, Pallas kernels, per_device(): pl.pallas_call(kernel, out_shape=jax.ShapeDtypeStruct((KYB * PL, 2 * K),...  57.1 us
    unnamed x1, local copies, waits for them, and re-layouts  1.92 us

profile of v9, /device:TPU:1, one launch (start us, length us, event | category | flops | bytes accessed | tf_op | source)
XLA Modules:
  0.0 59.0 jit_solution(11945947194118565050)
XLA Ops:
  0.0 57.1 %shard_map.100 = bf16[384,768]{1,0:T(8,128)(2,1)} custom-call(s32[8]{0:T(128)} %classes.1, s32[8]{0:T(128)} %kinds_in.1, f32[16]{0:T(128)} %defocus.1, s32[2,8]{1,0:T(2,128)} %bitcast.5, s32[8,8]{1,0:T(8,128)} %counts.1, bf16[4,128,384]{2,1,0:T(8,128)(2,1)} %constant.4.clone.left, bf16[8,384,384]{2,1,0:T(8,128)(2,1)} %img_in.1, ...), custom_call_target="tpu_custom_call" | custom-call | tf_op jit(solution)/shard_map/pallas_call | solution.py:695
  57.1 1.9 %copy.12 = bf16[24,16,768]{2,1,0:T(8,128)(2,1)} copy(bf16[24,16,768]{2,1,0:T(8,128)(2,1)} %bitcast.3) | data formatting | bytes 1179648

commit v10 on v9

--- a/solution.py
+++ b/solution.py
@@ -63,8 +63,8 @@
     classes, kinds_in, defocus, shifts, counts, left, img_in, right_in, dest_in, ref_in,
     out,
     img, right, dest, ref, scr, cscr, cwide, codes, cf, sc, vx, table_x, table_s, pq, wp, wm,
-    sendb, recvb, crecv, zsend, zrecv, zgot, nsend, nrecv, msend, mrecv, wts, tws,
-    img_m, right_m, dest_m, ref_m, code_s, code_r, row_s, row_r, z_s, z_r, y_s, y_r, n_s, n_r, m_s, m_r,
+    sendb, recvb, crecv, zsend, zrecv, zgot, nsend, nrecv, msend, mrecv, wts, tws, held,
+    out_m, img_m, right_m, dest_m, ref_m, code_s, code_r, row_s, row_r, z_s, z_r, y_s, y_r, n_s, n_r, m_s, m_r,
 ):
     mb = lax.axis_index("batch")
     ms = lax.axis_index("slab")
@@ -542,7 +542,8 @@
         for h in range(2):
             cols = pl.ds(h * K, K)
             top = TAU_PRIOR * ref[rows, cols].astype(F32) + sums[:, h * K : (h + 1) * K]
-            out[rows, cols] = (top * inverse).astype(BF)
+            held[rows, cols] = (top * inverse).astype(BF)
+        pltpu.make_async_copy(held.at[rows], out.at[rows], out_m).start()
 
     def gather(t):
         @pl.when(t < SHARED - 1)
@@ -658,6 +659,7 @@
     mirrored(SHARED - 1, 0)
 
     drain(crecv.at[pl.ds(0, 31)], code_s, code_r).wait_send()
+    pltpu.make_async_copy(held, out, out_m).wait()
     drain(nsend.at[pl.ds(0, 7)], n_s, n_r).wait_send()
     def drain_tile(t, carry):
         drain(sendb.at[t, pl.ds(0, 31)], row_s.at[t], row_r.at[t]).wait_send()
@@ -696,7 +698,7 @@
         kernel,
         out_shape=jax.ShapeDtypeStruct((KYB * PL, 2 * K), BF),
         in_specs=[smem] * 4 + [vmem] * 2 + [far] * 4,
-        out_specs=vmem,
+        out_specs=far,
         scratch_shapes=[
             pltpu.VMEM((PP, K, K), BF),
             pltpu.VMEM((2 * K, 2 * K), BF),
@@ -726,7 +728,8 @@
             pltpu.VMEM((SHARED, 4, PL, 2 * K), BF),
             pltpu.VMEM(((KYB + 1) * PL, K), F32),
             pltpu.VMEM((32, 128), F32),
-            dma((PP,)), dma, dma, dma, dma, dma, dma((TILES,)), dma((TILES,)),
+            pltpu.VMEM((KYB * PL, 2 * K), BF),
+            dma, dma((PP,)), dma, dma, dma, dma, dma, dma((TILES,)), dma((TILES,)),
             dma((TILES,)), dma((TILES,)), dma((SHARED,)), dma((SHARED,)), dma, dma,
             dma((SHARED,)), dma((SHARED,)),
         ],

time: 59.1 us -> 58.9 us (level)
  no operation moved by 1% of the time
where the time goes in v10:
time: 58.9 us; the launch traced here: 58.7 us
  Pallas kernels  56.8 us (96%)
  local copies, waits for them, and re-layouts  1.92 us (3%)
    pallas_call x1, Pallas kernels, per_device(): pl.pallas_call(kernel, out_shape=jax.ShapeDtypeStruct((KYB * PL, 2 * K),...  56.8 us
    unnamed x1, local copies, waits for them, and re-layouts  1.92 us

profile of v10, /device:TPU:1, one launch (start us, length us, event | category | flops | bytes accessed | tf_op | source)
XLA Modules:
  0.0 58.7 jit_solution(17481051705378166566)
XLA Ops:
  0.0 56.8 %shard_map.100 = bf16[384,768]{1,0:T(8,128)(2,1)} custom-call(s32[8]{0:T(128)} %classes.1, s32[8]{0:T(128)} %kinds_in.1, f32[16]{0:T(128)} %defocus.1, s32[2,8]{1,0:T(2,128)} %bitcast.5, s32[8,8]{1,0:T(8,128)} %counts.1, bf16[4,128,384]{2,1,0:T(8,128)(2,1)} %constant.4.clone.left, bf16[8,384,384]{2,1,0:T(8,128)(2,1)} %img_in.1, ...), custom_call_target="tpu_custom_call" | custom-call | tf_op jit(solution)/shard_map/pallas_call | solution.py:697
  56.8 1.9 %copy.12 = bf16[24,16,768]{2,1,0:T(8,128)(2,1)} copy(bf16[24,16,768]{2,1,0:T(8,128)(2,1)} %bitcast.3) | data formatting | bytes 1179648

commit v11 on v10

--- a/solution.py
+++ b/solution.py
@@ -412,7 +412,7 @@
 
         lax.fori_loop(0, 2, half, 0)
 
-        def weigh(i, carry):
+        def weigh(i, carry, mirrored=True):
             got = [[], [], [], []]
             for j in range(2):
                 rows = pl.ds(pl.multiple_of(i * 16 + j * 8, 8), 8)
@@ -428,17 +428,26 @@
                 fr, fi = fa - fb, fc + fd
                 got[0].append(sr * fr - si * fi)
                 got[1].append(sr * fi + si * fr)
+                if not mirrored:
+                    continue
                 sr, si = pr - qr, pi - qi
                 fr, fi = fa + fb, fc - fd
                 got[2].append(sr * fr - si * fi)
                 got[3].append(sr * fi + si * fr)
             rows = pl.ds(pl.multiple_of(i * 16, 16), 16)
-            for n in range(4):
+            for n in range(4 if mirrored else 2):
                 to = wp if n < 2 else wm
                 to[rows, pl.ds((n % 2) * K, K)] = jnp.concatenate(got[n], axis=0).astype(BF)
             return carry
 
-        lax.fori_loop(0, 32, weigh, 0, unroll=4)
+        @pl.when(t < LAST)
+        def _():
+            lax.fori_loop(0, 32, weigh, 0, unroll=4)
+
+        @pl.when(t == LAST)
+        def _():
+            lax.fori_loop(0, 32, lambda i, carry: weigh(i, carry, False), 0, unroll=4)
+
 
         def total(hot, rows):
             return jnp.dot(hot, rows, preferred_element_type=F32).astype(BF).reshape(NS, 32, 2 * K)
@@ -639,10 +648,6 @@
         def _():
             gather(t - 1)
 
-        @pl.when(t == LAST)
-        def _():
-            lax.fori_loop(0, 2, mirrored, 0)
-
         return carry
 
     tally()
@@ -656,7 +661,7 @@
         x += zgot[z].astype(F32)
     finish(0, x)
 
-    mirrored(SHARED - 1, 0)
+    lax.fori_loop(0, SHARED, mirrored, 0)
 
     drain(crecv.at[pl.ds(0, 31)], code_s, code_r).wait_send()
     pltpu.make_async_copy(held, out, out_m).wait()

time: 58.9 us -> 58.9 us (level)
  no operation moved by 1% of the time
where the time goes in v11:
time: 58.9 us; the launch traced here: 58.8 us
  Pallas kernels  56.8 us (96%)
  local copies, waits for them, and re-layouts  1.92 us (3%)
    pallas_call x1, Pallas kernels, per_device(): pl.pallas_call(kernel, out_shape=jax.ShapeDtypeStruct((KYB * PL, 2 * K),...  56.8 us
    unnamed x1, local copies, waits for them, and re-layouts  1.92 us

profile of v11, /device:TPU:1, one launch (start us, length us, event | category | flops | bytes accessed | tf_op | source)
XLA Modules:
  0.0 58.8 jit_solution(2958081548769841437)
XLA Ops:
  0.0 56.8 %shard_map.100 = bf16[384,768]{1,0:T(8,128)(2,1)} custom-call(s32[8]{0:T(128)} %classes.1, s32[8]{0:T(128)} %kinds_in.1, f32[16]{0:T(128)} %defocus.1, s32[2,8]{1,0:T(2,128)} %bitcast.5, s32[8,8]{1,0:T(8,128)} %counts.1, bf16[4,128,384]{2,1,0:T(8,128)(2,1)} %constant.4.clone.left, bf16[8,384,384]{2,1,0:T(8,128)(2,1)} %img_in.1, ...), custom_call_target="tpu_custom_call" | custom-call | tf_op jit(solution)/shard_map/pallas_call | solution.py:702
  56.8 1.9 %copy.12 = bf16[24,16,768]{2,1,0:T(8,128)(2,1)} copy(bf16[24,16,768]{2,1,0:T(8,128)(2,1)} %bitcast.3) | data formatting | bytes 1179648
